TPU v7x, 256 devices: a whole 4x4x8 slice. The times are simulated.
256 devices in a mesh: sec: 32 (over z_hi, y, core), narrow: 8 (over x, z_lo).
Axes of the slice: x: 4, y: 4, z: 8 (z_hi: 4, z_lo: 2; z = z_hi * 2 + z_lo), core: 2. Of those that a mesh axis runs over, the one named last changes fastest.
Arguments:
- tokens: bfloat16 [4096, 2048], P('sec'), may hold values from -8 to 8
- attn_gain: float32 [2048], replicated, may hold values from 0.5 to 1.5
- w_query: bfloat16 [2048, 4096], P(None, 'narrow'), may hold values from -0.125 to 0.125
- w_key: bfloat16 [2048, 512], P(None, 'narrow'), may hold values from -0.125 to 0.125
- w_value: bfloat16 [2048, 512], P(None, 'narrow'), may hold values from -0.125 to 0.125
- query_gain: float32 [128], replicated, may hold values from 0.6 to 6
- key_gain: float32 [128], replicated, may hold values from 0.6 to 6
- w_out: bfloat16 [4096, 2048], P('narrow'), may hold values from -0.09375 to 0.09375
- moe_gain: float32 [2048], replicated, may hold values from 0.5 to 1.5
- expert_ids: int32 [4096, 8], P('sec'), may hold values from 0 to 127, all different within a row; in each aligned block of 16 rows (0 to 15, 16 to 31, ...) at most 2 rows name the same one
- expert_weights: float32 [4096, 8], P('sec'), may hold values from 0.05 to 1
- w_gate: bfloat16 [128, 2048, 768], P('sec', None, 'narrow'), may hold values from -0.125 to 0.125
- w_up: bfloat16 [128, 2048, 768], P('sec', None, 'narrow'), may hold values from -0.125 to 0.125
- w_down: bfloat16 [128, 768, 2048], P('sec', 'narrow'), may hold values from -0.21875 to 0.21875
Outputs:
- layer_out: bfloat16 [4096, 2048], P(('sec', 'narrow'))
Inputs may be any that keep to these rules, and one draw needn't show every extreme that they name: `expert_ids`: each row names 8 different experts. In each aligned block of 16 rows no expert is named by more than 2 rows, a bound that some block reaches.
All inputs are finite; a program needn't handle non-finite values.
Results may differ from a plain program's by a relative error of at most 0.009.
Values may be sent and summed in bfloat16 or wider, within the bound.
No kernel may reach another device: no remote copies, remote signals or barrier semaphores. Data moves between devices by JAX's collectives and lax.ppermute only.
A program may use at most 128 MiB of HBM per device.

v0:
```python
import math

import jax
import jax.numpy as jnp
from jax import lax
from jax.experimental import pallas as pl
from jax.experimental.pallas import tpu as pltpu
from jax.sharding import Mesh
from jax.sharding import PartitionSpec as P


D = 2048
KV_HEADS = 4
HEAD = 128
TOPK = 8
CAP = 2
ZH, Y, C, X, ZL = 4, 4, 2, 4, 2
SEC = ("zh", "y", "c")
NARROW = ("x", "zl")
PLANE = ("y", "x", "zl")

norm_eps = 1e-06
ATTEND_VMEM = 16 * 1024 * 1024
EXPERT_VMEM = 24 * 1024 * 1024
BF = jnp.bfloat16
F32 = jnp.float32


def rms_norm(inputs, gain):
    widened = inputs.astype(F32)
    return (
        widened * lax.rsqrt(jnp.mean(widened * widened, axis=-1, keepdims=True) + norm_eps) * gain
    )


def angles_of(positions):
    half = HEAD // 2
    inverse = jnp.exp(-jnp.log(1000000.0) * jnp.arange(half, dtype=F32) * 2.0 / HEAD)
    angles = positions.astype(F32)[:, None] * inverse[None, :]
    return jnp.cos(angles), jnp.sin(angles)


def attention_kernel(where_ref, q_ref, own_ref, other_ref, w_out_ref, out_ref, q_all, acc, peak, total, attended):
    rows = q_ref.shape[0]
    heads = q_ref.shape[1] // HEAD
    pair_here = where_ref[0]
    core = where_ref[1]
    factor = math.log2(math.e) / math.sqrt(HEAD)
    for h in range(heads):
        q_all[h * rows : (h + 1) * rows, :] = q_ref[:, h * HEAD : (h + 1) * HEAD]
    acc[...] = jnp.zeros_like(acc)
    total[...] = jnp.zeros_like(total)
    peak[...] = jnp.full_like(peak, -1e30)

    def step(group, last):
        zh = group // 2
        y = group % 2 * 2
        sources = ((own_ref, y), (other_ref, y), (own_ref, y + 1), (other_ref, y + 1))
        keys = jnp.concatenate([ref[at, zh, 0] for ref, at in sources], axis=1)
        values = jnp.concatenate([ref[at, zh, 1] for ref, at in sources], axis=0)
        s = jnp.dot(q_all[...], keys, preferred_element_type=F32)
        if last:
            row = lax.broadcasted_iota(jnp.int32, s.shape, 0) % rows
            column = lax.broadcasted_iota(jnp.int32, s.shape, 1)
            piece = column // HEAD
            section = 4 * group + piece // 2 * 2 + jnp.where(piece % 2 == 0, core, 1 - core)
            allowed = section * HEAD + column % HEAD <= (2 * pair_here + core) * rows + row
            s = jnp.where(allowed, s, -1e30)
        parts = [s[:, i * HEAD : (i + 1) * HEAD] for i in range(4)]
        highest = jnp.maximum(jnp.maximum(parts[0], parts[1]), jnp.maximum(parts[2], parts[3]))
        old = peak[...]
        new = jnp.maximum(old, jnp.max(highest, axis=-1, keepdims=True))
        p = jnp.exp2((s - new) * factor)
        if last:
            p = jnp.where(allowed, p, 0.0)
        parts = [p[:, i * HEAD : (i + 1) * HEAD] for i in range(4)]
        scale = jnp.exp2((old - new) * factor)
        total[...] = total[...] * scale + ((parts[0] + parts[1]) + (parts[2] + parts[3]))
        acc[...] = acc[...] * scale + jnp.dot(p.astype(BF), values, preferred_element_type=F32)
        peak[...] = new

    @pl.loop(0, pair_here // 2)
    def _(group):
        step(group, False)

    step(pair_here // 2, True)
    summed = jnp.sum(total[...], axis=-1, keepdims=True)
    for h in range(heads):
        part = slice(h * rows, (h + 1) * rows)
        attended[:, h * HEAD : (h + 1) * HEAD] = (acc[part, :] / summed[part]).astype(BF)
    width = 512
    for at in range(0, D, width):
        out_ref[:, at : at + width] = jnp.dot(
            attended[...], w_out_ref[:, at : at + width], preferred_element_type=F32
        ).astype(BF)


def attention(where, query, own, other, w_out):
    rows = query.shape[0]
    heads = query.shape[1] // HEAD
    vmem = pl.BlockSpec(memory_space=pltpu.VMEM)
    return pl.pallas_call(
        attention_kernel,
        out_shape=jax.ShapeDtypeStruct((rows, D), BF),
        in_specs=[pl.BlockSpec(memory_space=pltpu.SMEM), vmem, vmem, vmem, vmem],
        out_specs=vmem,
        scratch_shapes=[
            pltpu.VMEM((heads * rows, HEAD), BF),
            pltpu.VMEM((heads * rows, HEAD), F32),
            pltpu.VMEM((heads * rows, 1), F32),
            pltpu.VMEM((heads * rows, HEAD), F32),
            pltpu.VMEM((rows, heads * HEAD), BF),
        ],
        compiler_params=pltpu.CompilerParams(vmem_limit_bytes=ATTEND_VMEM),
        cost_estimate=pl.CostEstimate(
            flops=1400000000, bytes_accessed=5000000, transcendentals=2000000
        ),
        name="attend",
    )(where, query, own, other, w_out)


def expert_kernel(rows_ref, *refs):
    pieces = refs[:8]
    out_ref, weights, active, sems = refs[8:]
    width = pieces[0].shape[0] // 3

    def copy(part, i):
        return pltpu.make_async_copy(
            pieces[i].at[pl.ds(part * width, width)],
            weights.at[part, pl.ds(i * width, width)],
            sems.at[part, i],
        )

    for half in range(2):
        for part in range(2):
            for i in range(4):
                copy(part, 4 * half + i).start()
    for i in range(8):
        copy(2, i).start()
    rows = rows_ref[...]
    for half in range(2):
        for part in range(2):
            for i in range(4):
                copy(part, 4 * half + i).wait()
        span = slice(4 * half * width, 4 * (half + 1) * width)
        gate = lax.dot_general(
            weights[0, span], rows, (((1,), (1,)), ((), ())), preferred_element_type=F32
        )
        up = lax.dot_general(
            weights[1, span], rows, (((1,), (1,)), ((), ())), preferred_element_type=F32
        )
        active[span, :] = (gate / (1.0 + jnp.exp(-gate)) * up).astype(BF)
    for i in range(8):
        copy(2, i).wait()
    acts = active[...].T
    span = 512
    for at in range(0, D, span):
        out_ref[:, at : at + span] = jnp.dot(
            acts, weights[2, :, at : at + span], preferred_element_type=F32
        ).astype(BF)


def expert(rows, pieces):
    count = rows.shape[0]
    width = pieces[0].shape[0] // 3
    vmem = pl.BlockSpec(memory_space=pltpu.VMEM)
    hbm = pl.BlockSpec(memory_space=pl.ANY)
    return pl.pallas_call(
        expert_kernel,
        out_shape=jax.ShapeDtypeStruct((count, D), BF),
        in_specs=[vmem] + [hbm] * 8,
        out_specs=vmem,
        scratch_shapes=[
            pltpu.VMEM((3, 8 * width, D), BF),
            pltpu.VMEM((8 * width, count), BF),
            pltpu.SemaphoreType.DMA((3, 8)),
        ],
        compiler_params=pltpu.CompilerParams(vmem_limit_bytes=EXPERT_VMEM),
        cost_estimate=pl.CostEstimate(
            flops=2400000000, bytes_accessed=11500000, transcendentals=200000
        ),
        name="expert",
    )(rows, *pieces)


def pack_kernel(x_ref, gate_ref, up_ref, down_ref, *refs):
    outs, sems = refs[:X], refs[X]
    width = down_ref.shape[1]

    def copy(k, part):
        source = (gate_ref, up_ref, down_ref)[part]
        return pltpu.make_async_copy(
            source.at[(x_ref[0] + k) % X],
            outs[k].at[pl.ds(part * width, width)],
            sems.at[k, part],
        )

    for k in range(X):
        for part in range(3):
            copy(k, part).start()
    for k in range(X):
        for part in range(3):
            copy(k, part).wait()


def pack(x, gate_t, up_t, w_down):
    width = w_down.shape[1]
    hbm = pl.BlockSpec(memory_space=pl.ANY)
    return pl.pallas_call(
        pack_kernel,
        out_shape=[jax.ShapeDtypeStruct((3 * width, D), BF)] * X,
        in_specs=[pl.BlockSpec(memory_space=pltpu.SMEM), hbm, hbm, hbm],
        out_specs=[pl.BlockSpec(memory_space=pltpu.VMEM)] * X,
        scratch_shapes=[pltpu.SemaphoreType.DMA((X, 3))],
        cost_estimate=pl.CostEstimate(flops=0, bytes_accessed=9500000, transcendentals=0),
        name="pack",
    )(x.reshape(1).astype(jnp.int32), gate_t, up_t, w_down)


def spread(piece, axes, members):
    copies = jnp.broadcast_to(piece[None], (members, *piece.shape))
    return lax.all_to_all(copies, axes, 0, 0, tiled=True)


def turned(axis_size, by):
    return [(i, (i + by) % axis_size) for i in range(axis_size)]


def weight_pieces(w_gate, w_up, w_down, c, x, zl):
    packed = pack(x, jnp.swapaxes(w_gate, 1, 2), jnp.swapaxes(w_up, 1, 2), w_down)
    own = []
    for k in range(X):
        pairs = []
        for cs in range(C):
            for xs in range(X):
                for zs in range(ZL):
                    source = (cs * X + xs) * ZL + zs
                    target = (zs * X + (xs + k) % X) * ZL + cs
                    if source != target:
                        pairs.append((source, target))
        moved = lax.ppermute(packed[k], ("c", "x", "zl"), pairs)
        if k == 0:
            moved = jnp.where(zl == c, packed[k], moved)
        own.append(moved)
    other = []
    for k in range(X):
        other.append(lax.ppermute(own[k], "c", [(0, 1), (1, 0)]))
    return own + other


def on_device(
    tokens,
    attn_gain,
    w_query,
    w_key,
    w_value,
    query_gain,
    key_gain,
    w_out,
    moe_gain,
    expert_ids,
    expert_weights,
    w_gate,
    w_up,
    w_down,
):
    zh, y, c = lax.axis_index("zh"), lax.axis_index("y"), lax.axis_index("c")
    x, zl = lax.axis_index("x"), lax.axis_index("zl")
    sec = (zh * Y + y) * C + c
    narrow = x * ZL + zl
    local_rows = tokens.shape[0]
    share = local_rows // (X * ZL)
    positions = sec * local_rows + jnp.arange(local_rows, dtype=jnp.int32)
    cosine, sine = angles_of(positions)
    half = HEAD // 2

    pieces = weight_pieces(w_gate, w_up, w_down, c, x, zl)

    normed = rms_norm(tokens, attn_gain).astype(BF)

    def columns(w):
        turned_w = lax.dot_general(
            w, normed, (((0,), (1,)), ((), ())), preferred_element_type=F32
        )
        return jnp.swapaxes(turned_w.reshape(-1, KV_HEADS, local_rows), 0, 1)

    both = jnp.stack([columns(w_key), columns(w_value)], axis=1)
    both = both.reshape(X * ZL, -1, local_rows)
    one = lax.all_to_all(both, NARROW, 0, 0, tiled=True).reshape(HEAD, local_rows)
    key_t = one * lax.rsqrt(jnp.mean(one * one, axis=0, keepdims=True) + norm_eps)
    key_t = key_t * key_gain[:, None]
    cos_t, sin_t = cosine.T, sine.T
    lead, trail = key_t[:half], key_t[half:]
    key_t = jnp.concatenate(
        [lead * cos_t - trail * sin_t, trail * cos_t + lead * sin_t], axis=0
    ).astype(BF)
    piece = jnp.where(zl == 0, key_t, one.T.astype(BF))
    ring = spread(piece, ("zh", "zl"), ZH * ZL)
    own = spread(ring, "y", Y)
    own = own.reshape(Y, ZH, ZL, HEAD, HEAD)
    other = lax.ppermute(own, "c", [(0, 1), (1, 0)])

    query = jnp.dot(normed, w_query, preferred_element_type=F32).reshape(local_rows, -1, HEAD)
    query = rms_norm(query, query_gain)
    lead, trail = query[..., :half], query[..., half:]
    cos_q, sin_q = cosine[:, None, :], sine[:, None, :]
    query = jnp.concatenate(
        [lead * cos_q - trail * sin_q, trail * cos_q + lead * sin_q], axis=-1
    ).astype(BF)
    query = query.reshape(local_rows, -1)

    where = jnp.stack([zh * Y + y, c]).astype(jnp.int32)
    partial = attention(where, query, own, other, w_out)
    blocks = lax.all_to_all(partial.reshape(X * ZL, share, D), NARROW, 0, 0, tiled=True)
    mixed = jnp.sum(blocks.astype(F32), axis=0)
    own_tokens = lax.dynamic_slice_in_dim(tokens, narrow * share, share, 0)
    carried = (own_tokens.astype(F32) + mixed).astype(BF)
    moe_in = rms_norm(carried, moe_gain).astype(BF)

    ids = lax.dynamic_slice_in_dim(expert_ids, narrow * share, share, 0)
    weights = lax.dynamic_slice_in_dim(expert_weights, narrow * share, share, 0)
    gates = weights / jnp.sum(weights, axis=-1, keepdims=True)
    gates_high = gates.astype(BF)
    gates_low = (gates - gates_high.astype(F32)).astype(BF)
    tail = jnp.concatenate(
        [
            ids.astype(BF),
            gates_high,
            gates_low,
            jnp.zeros((share, 128 - 3 * TOPK), BF),
        ],
        axis=1,
    )
    packet = jnp.concatenate([moe_in, tail], axis=1)
    packets = [packet] + [lax.ppermute(packet, "zh", turned(ZH, k)) for k in range(1, ZH)]
    packets = jnp.concatenate(packets, axis=0)
    rows = packets[:, :D]
    routes = packets[:, D:].astype(F32)
    ids_f = routes[:, :TOPK]
    gates_all = routes[:, TOPK : 2 * TOPK] + routes[:, 2 * TOPK : 3 * TOPK]
    chips = jnp.arange(Y * X * ZL, dtype=jnp.int32)
    expert_of = (
        zh * (Y * X * ZL) + chips // (X * ZL) * (X * ZL) + chips % ZL * X + chips // ZL % X
    ).astype(F32)
    hits = ids_f[:, :, None] == expert_of[None, None, :]
    named = jnp.any(hits, axis=1).reshape(ZH, share, -1)
    gate_of = jnp.sum(jnp.where(hits, gates_all[:, :, None], 0.0), axis=1).reshape(ZH, share, -1)
    named_f = named.astype(F32)
    earlier = jnp.cumsum(named_f, axis=1) - named_f
    slot = jnp.arange(CAP, dtype=F32)
    chosen = named[..., None] & (earlier[..., None] == slot)
    same = jnp.eye(ZH, dtype=jnp.bool_)
    table = chosen[:, :, :, None, :] & same[:, None, None, :, None]
    table = table.reshape(ZH * share, -1)
    shared_gate = jnp.broadcast_to(
        gate_of[:, :, :, None, None], (ZH, share, Y * X * ZL, ZH, CAP)
    ).reshape(ZH * share, -1)
    outgoing = lax.dot_general(
        table.astype(BF), rows, (((0,), (0,)), ((), ())), preferred_element_type=F32
    ).astype(BF)
    arrived = lax.all_to_all(
        outgoing.reshape(Y * X * ZL, ZH * CAP, D), PLANE, 0, 0, tiled=True
    ).reshape(-1, D)
    answers = expert(arrived, pieces)
    returned = lax.all_to_all(
        answers.reshape(Y * X * ZL, ZH * CAP, D), PLANE, 0, 0, tiled=True
    ).reshape(-1, D)
    mixing = jnp.where(table, shared_gate, 0.0)
    mixing_high = mixing.astype(BF)
    mixing_low = (mixing - mixing_high.astype(F32)).astype(BF)
    sums = jnp.dot(mixing_high, returned, preferred_element_type=F32) + jnp.dot(
        mixing_low, returned, preferred_element_type=F32
    )
    sums = sums.reshape(ZH, share, D)
    result = carried.astype(F32) + sums[0]
    for k in range(1, ZH):
        back = lax.ppermute(sums[k].astype(BF), "zh", turned(ZH, -k))
        result = result + back.astype(F32)
    return result.astype(BF)


def solution(mesh):
    split = Mesh(mesh.devices.reshape(ZH, Y, C, X, ZL), ("zh", "y", "c", "x", "zl"))
    in_specs = (
        P(SEC, None),
        P(),
        P(None, NARROW),
        P(None, NARROW),
        P(None, NARROW),
        P(),
        P(),
        P(NARROW, None),
        P(),
        P(SEC, None),
        P(SEC, None),
        P(SEC, None, NARROW),
        P(SEC, None, NARROW),
        P(SEC, NARROW, None),
    )
    out_specs = P(SEC + NARROW, None)

    return jax.shard_map(
        on_device, mesh=split, in_specs=in_specs, out_specs=out_specs, check_vma=False
    )
```

profile of v0, /device:TPU:32, one launch (start us, length us, event | category | flops | bytes accessed | tf_op | source)
XLA Modules:
  0.0 195.0 jit_solution(10285114143744390732)
XLA Ops:
  0.0 1.4 fusion.1
  1.4 1.5 fusion.37
  3.0 0.4 fusion.35
  3.3 0.6 pad_maximum_fusion.7
  4.0 5.8 %all-to-all-start = ((f32[8,16,128]{2,1,0:T(8,128)}), f32[8,16,128]{2,1,0:T(8,128)S(1)}, u32[]{:S(2)}, u32[]{:S(2)}) async-start(f32[8,16,128]{2,1,0:T(8,128)} %bitcast.10), calls=%async_computation | async-start | bytes 131072 | tf_op jit(solution)/shard_map/all_to_all | solution.py:289
  9.8 5.0 %all-to-all-done = f32[8,16,128]{2,1,0:T(8,128)S(1)} async-done(((f32[8,16,128]{2,1,0:T(8,128)}), f32[8,16,128]{2,1,0:T(8,128)S(1)}, u32[]{:S(2)}, u32[]{:S(2)}) %all-to-all-start) | async-done | bytes 65568 | tf_op jit(solution)/shard_map/all_to_all | solution.py:289
  15.1 0.2 fusion.23
  15.3 17.7 %all_to_all.30 = bf16[8,128,128]{2,1,0:T(8,128)(2,1)S(1)} all-to-all(bf16[8,128,128]{2,1,0:T(8,128)(2,1)S(1)} %broadcast_in_dim.21), channel_id=1, replica_groups=mesh['zh'=4,'y'=4,'c'=2,'x'=4,'zl'=2] {'zh','zl'}, dimensions={0} | all-to-all | bytes 524288 | tf_op jit(solution)/shard_map/all_to_all | solution.py:222
  33.0 1.2 broadcast_in_dim.22
  34.2 4.5 %all-to-all-start.2 = ((bf16[4,8,128,128]{3,2,1,0:T(8,128)(2,1)}), bf16[4,8,128,128]{3,2,1,0:T(8,128)(2,1)S(1)}, u32[]{:S(2)}, u32[]{:S(2)}) async-start(bf16[4,8,128,128]{3,2,1,0:T(8,128)(2,1)} %broadcast_in_dim.22), calls=%async_computation.2 | async-start | bytes 2097152 | tf_op jit(solution)/shard_map/all_to_all | solution.py:222
  38.7 2.3 %fusion.39 = f32[128,512]{1,0:T(8,128)} fusion(bf16[2048,512]{1,0:T(8,128)(2,1)S(1)} %copy-done, bf16[128,2048]{1,0:T(8,128)(2,1)} %param.14, f32[2048]{0:T(1024)S(1)} %copy-done.14, f32[128]{0:T(128)S(1)} %add_rsqrt_fusion.3), kind=kOutput, calls=%fused_computation.96 | convolution fusion | flops 269484032 | bytes 2892288 | tf_op jit(solution)/shard_map/dot_general | solution.py:303
  41.0 1.0 reshape.252
  42.0 0.2 multiply_reduce_fusion
  42.2 8.6 %all-to-all-done.2 = bf16[4,8,128,128]{3,2,1,0:T(8,128)(2,1)S(1)} async-done(((bf16[4,8,128,128]{3,2,1,0:T(8,128)(2,1)}), bf16[4,8,128,128]{3,2,1,0:T(8,128)(2,1)S(1)}, u32[]{:S(2)}, u32[]{:S(2)}) %all-to-all-start.2) | async-done | bytes 1048608 | tf_op jit(solution)/shard_map/all_to_all | solution.py:222
  50.9 0.3 multiply_cosine_fusion
  51.2 0.2 multiply_multiply_fusion
  51.4 0.3 subtract_convert_fusion
  51.7 0.2 pad_maximum_fusion.6
  52.0 1.5 collective-permute-done.other_ref
  53.5 2.0 %attend.1 = bf16[128,2048]{1,0:T(8,128)(2,1)S(1)} custom-call(s32[2]{0:T(128)S(1)} %pad_add_fusion.where_ref, bf16[128,512]{1,0:T(8,128)(2,1)S(1)} %bitcast.59, bf16[4,4,2,128,128]{4,3,2,1,0:T(8,128)(2,1)S(1)} %bitcast.57, bf16[4,4,2,128,128]{4,3,2,1,0:T(8,128)(2,1)S(1)} %collective-permute-done.other_ref, bf16[512,2048]{1,0:T(8,128)(2,1)S(1)} %copy-done.11), custom_call_target="tpu_custom_call" | custom-call | flops 1400000000 | bytes 5000000 | tf_op jit(solution)/shard_map/attend/pallas_call | solution.py:102
  55.6 0.8 copy-done.10
  56.3 5.1 %all-to-all-start.3 = ((bf16[8,16,2048]{2,1,0:T(8,128)(2,1)}), bf16[8,16,2048]{2,1,0:T(8,128)(2,1)S(1)}, u32[]{:S(2)}, u32[]{:S(2)}) async-start(bf16[8,16,2048]{2,1,0:T(8,128)(2,1)} %bitcast.58), calls=%async_computation.3 | async-start | bytes 1048576 | tf_op jit(solution)/shard_map/all_to_all | solution.py:314
  61.4 4.6 %pack.1 = (bf16[288,2048]{1,0:T(8,128)(2,1)}, bf16[288,2048]{1,0:T(8,128)(2,1)}, bf16[288,2048]{1,0:T(8,128)(2,1)}, bf16[288,2048]{1,0:T(8,128)(2,1)}) custom-call(s32[1]{0:T(128)} %bitcast.19.x_ref, bf16[4,96,2048]{2,1,0:T(8,128)(2,1)} %bitcast.60, bf16[4,96,2048]{2,1,0:T(8,128)(2,1)} %bitcast.61, bf16[4,96,2048]{2,1,0:T(8,128)(2,1)} %down_ref.1), custom_call_target="tpu_custom_call" | custom-call | bytes 9500000 | tf_op jit(solution)/shard_map/pack/pallas_call | solution.py:209
  66.1 1.9 collective-permute-start.4
  68.0 4.3 %collective-permute-start.6 = (bf16[288,2048]{1,0:T(8,128)(2,1)}, bf16[288,2048]{1,0:T(8,128)(2,1)}, u32[]{:S(2)}, u32[]{:S(2)}) collective-permute-start(bf16[288,2048]{1,0:T(8,128)(2,1)} %get-tuple-element.11), channel_id=1, source_target_pairs={{0,4},{1,12},{2,6},{3,14},{4,0},{5,8},{6,2},{7,10},{8,5},{9,13},{1... | collective-permute-start | bytes 3538952 | tf_op jit(solution)/shard_map/ppermute | solution.py:241
  72.7 1.0 fusion.10
  73.9 1.7 collective-permute-start.1
  75.6 6.8 %collective-permute-start.2 = (bf16[16,2176]{1,0:T(8,128)(2,1)S(1)}, bf16[16,2176]{1,0:T(8,128)(2,1)S(1)}, u32[]{:S(2)}, u32[]{:S(2)}) collective-permute-start(bf16[16,2176]{1,0:T(8,128)(2,1)S(1)} %concatenate.16), channel_id=1, source_target_pairs={{0,128},{64,192},{128,0},{192,64},{1,129},{65,193},{129,1},{193,65... | collective-permute-start | bytes 208904 | tf_op jit(solution)/shard_map/ppermute | solution.py:335
  82.4 0.3 collective-permute-start.3
  82.7 26.7 %collective-permute-start.7 = (bf16[288,2048]{1,0:T(8,128)(2,1)}, bf16[288,2048]{1,0:T(8,128)(2,1)}, u32[]{:S(2)}, u32[]{:S(2)}) collective-permute-start(bf16[288,2048]{1,0:T(8,128)(2,1)} %get-tuple-element.12), channel_id=1, source_target_pairs={{0,6},{1,14},{2,0},{3,8},{4,2},{5,10},{6,4},{7,12},{8,7},{9,15},{1... | collective-permute-start | bytes 3538952 | tf_op jit(solution)/shard_map/ppermute | solution.py:241
  110.1 0.2 broadcast_and_fusion
  110.3 0.2 and.108
  110.5 1.4 fusion
  111.9 6.0 %all-to-all-start.4 = ((bf16[32,8,2048]{2,1,0:T(8,128)(2,1)}), bf16[32,8,2048]{2,1,0:T(8,128)(2,1)}, u32[]{:S(2)}, u32[]{:S(2)}) async-start(bf16[32,8,2048]{2,1,0:T(8,128)(2,1)} %fusion), calls=%async_computation.4 | async-start | bytes 2097152 | tf_op jit(solution)/shard_map/all_to_all | solution.py:361
  117.9 1.4 broadcast_select_fusion.refs_0_
  119.3 1.6 collective-permute-start.8
  121.0 6.1 %collective-permute-done.7.refs_3_ = bf16[288,2048]{1,0:T(8,128)(2,1)} collective-permute-done((bf16[288,2048]{1,0:T(8,128)(2,1)}, bf16[288,2048]{1,0:T(8,128)(2,1)}, u32[]{:S(2)}, u32[]{:S(2)}) %collective-permute-start.7) | collective-permute-done | bytes 1179680 | tf_op jit(solution)/shard_map/ppermute | solution.py:241
  127.2 14.8 %collective-permute-done.5.refs_1_ = bf16[288,2048]{1,0:T(8,128)(2,1)} collective-permute-done((bf16[288,2048]{1,0:T(8,128)(2,1)}, bf16[288,2048]{1,0:T(8,128)(2,1)}, u32[]{:S(2)}, u32[]{:S(2)}) %collective-permute-start.5) | collective-permute-done | bytes 1179680 | tf_op jit(solution)/shard_map/ppermute | solution.py:241
  142.0 1.0 copy-done.2
  143.0 1.1 copy-done.4
  144.1 1.1 copy-done.6
  145.2 1.0 copy-done.8
  146.2 1.1 all-to-all-done.4
  147.3 1.3 copy-done.3
  148.6 1.3 copy-done.5
  149.9 1.3 copy-done.7
  151.1 1.3 copy-done.9
  152.4 7.4 %expert.1 = bf16[256,2048]{1,0:T(8,128)(2,1)S(1)} custom-call(bf16[256,2048]{1,0:T(8,128)(2,1)} %bitcast.18.rows_ref, bf16[288,2048]{1,0:T(8,128)(2,1)S(1)} %broadcast_select_fusion.refs_0_, bf16[288,2048]{1,0:T(8,128)(2,1)} %collective-permute-done.5.refs_1_, bf16[288,2048]{1,0:T(8,128)(2,1)} %collective-permute-done.6.refs_2_, ...), custom_call_target="tpu_custom_call" | custom-call | flops 2400000000 | bytes 11500000 | tf_op jit(solution)/shard_map/expert/pallas_call | solution.py:168
  159.9 1.0 copy-done.1
  160.8 8.7 %all-to-all-start.5 = ((bf16[32,8,2048]{2,1,0:T(8,128)(2,1)}), bf16[32,8,2048]{2,1,0:T(8,128)(2,1)S(1)}, u32[]{:S(2)}, u32[]{:S(2)}) async-start(bf16[32,8,2048]{2,1,0:T(8,128)(2,1)} %bitcast.55), calls=%async_computation.5 | async-start | bytes 2097152 | tf_op jit(solution)/shard_map/all_to_all | solution.py:365
  169.9 1.0 fusion.7
  170.9 0.8 convert_element_type.157
  171.7 1.0 select_convert_fusion
  172.7 0.2 convert_element_type.153
  172.9 11.1 %all-to-all-done.5 = bf16[32,8,2048]{2,1,0:T(8,128)(2,1)S(1)} async-done(((bf16[32,8,2048]{2,1,0:T(8,128)(2,1)}), bf16[32,8,2048]{2,1,0:T(8,128)(2,1)S(1)}, u32[]{:S(2)}, u32[]{:S(2)}) %all-to-all-start.5) | async-done | bytes 1048608 | tf_op jit(solution)/shard_map/all_to_all | solution.py:365
  184.0 1.2 fusion.4
  185.2 0.3 fusion.44
  185.5 0.1 collective-permute-start.12
  185.6 0.4 collective-permute-start.13
  186.1 2.5 %collective-permute-start.14 = (bf16[16,2048]{1,0:T(8,128)(2,1)S(1)}, bf16[16,2048]{1,0:T(8,128)(2,1)S(1)}, u32[]{:S(2)}, u32[]{:S(2)}) collective-permute-start(bf16[16,2048]{1,0:T(8,128)(2,1)S(1)} %get-tuple-element.20), channel_id=1, source_target_pairs={{0,64},{64,128},{128,192},{192,0},{1,65},{65,129},{129,193},{193,1... | collective-permute-start | bytes 196616 | tf_op jit(solution)/shard_map/ppermute | solution.py:377
  188.5 2.3 %collective-permute-done.12 = bf16[16,2048]{1,0:T(8,128)(2,1)S(1)} collective-permute-done((bf16[16,2048]{1,0:T(8,128)(2,1)S(1)}, bf16[16,2048]{1,0:T(8,128)(2,1)S(1)}, u32[]{:S(2)}, u32[]{:S(2)}) %collective-permute-start.12) | collective-permute-done | bytes 65568 | tf_op jit(solution)/shard_map/ppermute | solution.py:377
  190.8 3.0 %collective-permute-done.13 = bf16[16,2048]{1,0:T(8,128)(2,1)S(1)} collective-permute-done((bf16[16,2048]{1,0:T(8,128)(2,1)S(1)}, bf16[16,2048]{1,0:T(8,128)(2,1)S(1)}, u32[]{:S(2)}, u32[]{:S(2)}) %collective-permute-start.13) | collective-permute-done | bytes 65568 | tf_op jit(solution)/shard_map/ppermute | solution.py:377
  193.9 0.5 collective-permute-done.14
  194.4 0.7 fusion.16
  (89 shorter events, 2.3 us)
Async XLA Ops:
  0.0 38.7 %copy-start = (bf16[2048,512]{1,0:T(8,128)(2,1)S(1)}, bf16[2048,512]{1,0:T(8,128)(2,1)}, u32[]{:S(2)}) copy-start(bf16[2048,512]{1,0:T(8,128)(2,1)} %param.16) | copy-start | bytes 6291460
  0.0 2.9 %copy-start.12 = (bf16[128,2048]{1,0:T(8,128)(2,1)S(1)}, bf16[128,2048]{1,0:T(8,128)(2,1)}, u32[]{:S(2)}) copy-start(bf16[128,2048]{1,0:T(8,128)(2,1)} %param.14) | copy-start | bytes 1572868
  0.0 2.9 %copy-start.14 = (f32[2048]{0:T(1024)S(1)}, f32[2048]{0:T(1024)}, u32[]{:S(2)}) copy-start(f32[2048]{0:T(1024)} %param.15) | copy-start | bytes 24580
  0.0 2.9 %copy-start.20 = (bf16[2048,64]{0,1:T(8,128)(2,1)S(1)}, bf16[2048,64]{0,1:T(8,128)(2,1)}, u32[]{:S(2)}) copy-start(bf16[2048,64]{0,1:T(8,128)(2,1)} %param.18) | copy-start | bytes 786436
  1.4 13.6 %copy-start.18 = (f32[128]{0:T(128)S(1)}, f32[128]{0:T(128)}, u32[]{:S(2)}) copy-start(f32[128]{0:T(128)} %param.20) | copy-start | bytes 1540
  4.0 10.8 %all-to-all-start = ((f32[8,16,128]{2,1,0:T(8,128)}), f32[8,16,128]{2,1,0:T(8,128)S(1)}, u32[]{:S(2)}, u32[]{:S(2)}) async-start(f32[8,16,128]{2,1,0:T(8,128)} %bitcast.10), calls=%async_computation | async-start | bytes 131072 | tf_op jit(solution)/shard_map/all_to_all | solution.py:289
  34.2 16.6 %all-to-all-start.2 = ((bf16[4,8,128,128]{3,2,1,0:T(8,128)(2,1)}), bf16[4,8,128,128]{3,2,1,0:T(8,128)(2,1)S(1)}, u32[]{:S(2)}, u32[]{:S(2)}) async-start(bf16[4,8,128,128]{3,2,1,0:T(8,128)(2,1)} %broadcast_in_dim.22), calls=%async_computation.2 | async-start | bytes 2097152 | tf_op jit(solution)/shard_map/all_to_all | solution.py:222
  38.7 12.5 %copy-start.19 = (f32[128]{0:T(128)S(1)}, f32[128]{0:T(128)}, u32[]{:S(2)}) copy-start(f32[128]{0:T(128)} %param.19) | copy-start | bytes 1540
  50.8 2.7 %collective-permute-start = (bf16[4,4,2,128,128]{4,3,2,1,0:T(8,128)(2,1)S(1)}, bf16[4,4,2,128,128]{4,3,2,1,0:T(8,128)(2,1)S(1)}, u32[]{:S(2)}, u32[]{:S(2)}) collective-permute-start(bf16[4,4,2,128,128]{4,3,2,1,0:T(8,128)(2,1)S(1)} %bitcast.56), channel_id=1, source_target_pairs={{0,8},{8,0},{1,9},{9,1},{2,10},{10,2},{3,11},{11,3},{4,12},{12,4},... | collective-permute-start | bytes 3145736 | tf_op jit(solution)/shard_map/ppermute | solution.py:301
  50.9 2.6 %copy-start.11 = (bf16[512,2048]{1,0:T(8,128)(2,1)S(1)}, bf16[512,2048]{1,0:T(8,128)(2,1)}, u32[]{:S(2)}) copy-start(bf16[512,2048]{1,0:T(8,128)(2,1)} %w_out_ref.1) | copy-start | bytes 6291460
  55.5 0.8 copy-start.10
  56.3 16.3 %all-to-all-start.3 = ((bf16[8,16,2048]{2,1,0:T(8,128)(2,1)}), bf16[8,16,2048]{2,1,0:T(8,128)(2,1)S(1)}, u32[]{:S(2)}, u32[]{:S(2)}) async-start(bf16[8,16,2048]{2,1,0:T(8,128)(2,1)} %bitcast.58), calls=%async_computation.3 | async-start | bytes 1048576 | tf_op jit(solution)/shard_map/all_to_all | solution.py:314
  61.4 10.8 %copy-start.16 = (f32[128,8]{0,1:T(8,128)S(1)}, f32[128,8]{0,1:T(8,128)}, u32[]{:S(2)}) copy-start(f32[128,8]{0,1:T(8,128)} %param.24) | copy-start | bytes 12292
  61.4 11.0 %copy-start.17 = (s32[128,8]{0,1:T(8,128)S(1)}, s32[128,8]{0,1:T(8,128)}, u32[]{:S(2)}) copy-start(s32[128,8]{0,1:T(8,128)} %param.23) | copy-start | bytes 12292
  61.4 12.3 %copy-start.15 = (f32[2048]{0:T(1024)S(1)}, f32[2048]{0:T(1024)}, u32[]{:S(2)}) copy-start(f32[2048]{0:T(1024)} %param.22) | copy-start | bytes 24580
  66.1 51.8 %collective-permute-start.4 = (bf16[288,2048]{1,0:T(8,128)(2,1)}, bf16[288,2048]{1,0:T(8,128)(2,1)}, u32[]{:S(2)}, u32[]{:S(2)}) collective-permute-start(bf16[288,2048]{1,0:T(8,128)(2,1)} %get-tuple-element.9), channel_id=1, source_target_pairs={{1,8},{3,10},{5,12},{7,14},{8,1},{10,3},{12,5},{14,7},{17,24},{19,... | collective-permute-start | bytes 3538952 | tf_op jit(solution)/shard_map/ppermute | solution.py:241
  68.0 52.9 %collective-permute-start.6 = (bf16[288,2048]{1,0:T(8,128)(2,1)}, bf16[288,2048]{1,0:T(8,128)(2,1)}, u32[]{:S(2)}, u32[]{:S(2)}) collective-permute-start(bf16[288,2048]{1,0:T(8,128)(2,1)} %get-tuple-element.11), channel_id=1, source_target_pairs={{0,4},{1,12},{2,6},{3,14},{4,0},{5,8},{6,2},{7,10},{8,5},{9,13},{1... | collective-permute-start | bytes 3538952 | tf_op jit(solution)/shard_map/ppermute | solution.py:241
  73.9 8.7 %collective-permute-start.1 = (bf16[16,2176]{1,0:T(8,128)(2,1)S(1)}, bf16[16,2176]{1,0:T(8,128)(2,1)S(1)}, u32[]{:S(2)}, u32[]{:S(2)}) collective-permute-start(bf16[16,2176]{1,0:T(8,128)(2,1)S(1)} %concatenate.16), channel_id=1, source_target_pairs={{0,64},{64,128},{128,192},{192,0},{1,65},{65,129},{129,193},{193,1... | collective-permute-start | bytes 208904 | tf_op jit(solution)/shard_map/ppermute | solution.py:335
  75.6 33.8 %collective-permute-start.2 = (bf16[16,2176]{1,0:T(8,128)(2,1)S(1)}, bf16[16,2176]{1,0:T(8,128)(2,1)S(1)}, u32[]{:S(2)}, u32[]{:S(2)}) collective-permute-start(bf16[16,2176]{1,0:T(8,128)(2,1)S(1)} %concatenate.16), channel_id=1, source_target_pairs={{0,128},{64,192},{128,0},{192,64},{1,129},{65,193},{129,1},{193,65... | collective-permute-start | bytes 208904 | tf_op jit(solution)/shard_map/ppermute | solution.py:335
  82.4 27.0 %collective-permute-start.3 = (bf16[16,2176]{1,0:T(8,128)(2,1)S(1)}, bf16[16,2176]{1,0:T(8,128)(2,1)S(1)}, u32[]{:S(2)}, u32[]{:S(2)}) collective-permute-start(bf16[16,2176]{1,0:T(8,128)(2,1)S(1)} %concatenate.16), channel_id=1, source_target_pairs={{0,192},{64,0},{128,64},{192,128},{1,193},{65,1},{129,65},{193,129... | collective-permute-start | bytes 208904 | tf_op jit(solution)/shard_map/ppermute | solution.py:335
  82.7 44.5 %collective-permute-start.7 = (bf16[288,2048]{1,0:T(8,128)(2,1)}, bf16[288,2048]{1,0:T(8,128)(2,1)}, u32[]{:S(2)}, u32[]{:S(2)}) collective-permute-start(bf16[288,2048]{1,0:T(8,128)(2,1)} %get-tuple-element.12), channel_id=1, source_target_pairs={{0,6},{1,14},{2,0},{3,8},{4,2},{5,10},{6,4},{7,12},{8,7},{9,15},{1... | collective-permute-start | bytes 3538952 | tf_op jit(solution)/shard_map/ppermute | solution.py:241
  109.4 32.6 %collective-permute-start.5 = (bf16[288,2048]{1,0:T(8,128)(2,1)}, bf16[288,2048]{1,0:T(8,128)(2,1)}, u32[]{:S(2)}, u32[]{:S(2)}) collective-permute-start(bf16[288,2048]{1,0:T(8,128)(2,1)} %get-tuple-element.10), channel_id=1, source_target_pairs={{0,2},{1,10},{2,4},{3,12},{4,6},{5,14},{6,0},{7,8},{8,3},{9,11},{1... | collective-permute-start | bytes 3538952 | tf_op jit(solution)/shard_map/ppermute | solution.py:241
  110.1 1.8 copy-start.13
  111.9 35.4 %all-to-all-start.4 = ((bf16[32,8,2048]{2,1,0:T(8,128)(2,1)}), bf16[32,8,2048]{2,1,0:T(8,128)(2,1)}, u32[]{:S(2)}, u32[]{:S(2)}) async-start(bf16[32,8,2048]{2,1,0:T(8,128)(2,1)} %fusion), calls=%async_computation.4 | async-start | bytes 2097152 | tf_op jit(solution)/shard_map/all_to_all | solution.py:361
  119.3 22.7 %collective-permute-start.8 = (bf16[288,2048]{1,0:T(8,128)(2,1)S(1)}, bf16[288,2048]{1,0:T(8,128)(2,1)S(1)}, u32[]{:S(2)}, u32[]{:S(2)}) collective-permute-start(bf16[288,2048]{1,0:T(8,128)(2,1)S(1)} %broadcast_select_fusion.refs_0_), channel_id=1, source_target_pairs={{0,8},{8,0},{1,9},{9,1},{2,10},{10,2},{3,11},{11,3},{4,12},{12,4},... | collective-permute-start | bytes 3538952 | tf_op jit(solution)/shard_map/ppermute | solution.py:247
  120.9 22.1 %collective-permute-start.10 = (bf16[288,2048]{1,0:T(8,128)(2,1)}, bf16[288,2048]{1,0:T(8,128)(2,1)S(1)}, u32[]{:S(2)}, u32[]{:S(2)}) collective-permute-start(bf16[288,2048]{1,0:T(8,128)(2,1)} %collective-permute-done.6.refs_2_), channel_id=1, source_target_pairs={{0,8},{8,0},{1,9},{9,1},{2,10},{10,2},{3,11},{11,3},{4,12},{12,4},... | collective-permute-start | bytes 3538952 | tf_op jit(solution)/shard_map/ppermute | solution.py:247
  127.2 16.9 %collective-permute-start.11 = (bf16[288,2048]{1,0:T(8,128)(2,1)}, bf16[288,2048]{1,0:T(8,128)(2,1)S(1)}, u32[]{:S(2)}, u32[]{:S(2)}) collective-permute-start(bf16[288,2048]{1,0:T(8,128)(2,1)} %collective-permute-done.7.refs_3_), channel_id=1, source_target_pairs={{0,8},{8,0},{1,9},{9,1},{2,10},{10,2},{3,11},{11,3},{4,12},{12,4},... | collective-permute-start | bytes 3538952 | tf_op jit(solution)/shard_map/ppermute | solution.py:247
  142.0 3.2 %collective-permute-start.9 = (bf16[288,2048]{1,0:T(8,128)(2,1)}, bf16[288,2048]{1,0:T(8,128)(2,1)S(1)}, u32[]{:S(2)}, u32[]{:S(2)}) collective-permute-start(bf16[288,2048]{1,0:T(8,128)(2,1)} %collective-permute-done.5.refs_1_), channel_id=1, source_target_pairs={{0,8},{8,0},{1,9},{9,1},{2,10},{10,2},{3,11},{11,3},{4,12},{12,4},... | collective-permute-start | bytes 3538952 | tf_op jit(solution)/shard_map/ppermute | solution.py:247
  142.0 1.0 copy-start.2
  143.0 1.1 copy-start.4
  144.1 1.1 copy-start.6
  145.2 1.0 copy-start.8
  147.3 1.3 copy-start.3
  148.6 1.3 copy-start.5
  149.9 1.3 copy-start.7
  151.1 1.3 copy-start.9
  159.8 1.0 copy-start.1
  160.8 23.2 %all-to-all-start.5 = ((bf16[32,8,2048]{2,1,0:T(8,128)(2,1)}), bf16[32,8,2048]{2,1,0:T(8,128)(2,1)S(1)}, u32[]{:S(2)}, u32[]{:S(2)}) async-start(bf16[32,8,2048]{2,1,0:T(8,128)(2,1)} %bitcast.55), calls=%async_computation.5 | async-start | bytes 2097152 | tf_op jit(solution)/shard_map/all_to_all | solution.py:365
  185.5 5.3 %collective-permute-start.12 = (bf16[16,2048]{1,0:T(8,128)(2,1)S(1)}, bf16[16,2048]{1,0:T(8,128)(2,1)S(1)}, u32[]{:S(2)}, u32[]{:S(2)}) collective-permute-start(bf16[16,2048]{1,0:T(8,128)(2,1)S(1)} %get-tuple-element.19), channel_id=1, source_target_pairs={{0,192},{64,0},{128,64},{192,128},{1,193},{65,1},{129,65},{193,129... | collective-permute-start | bytes 196616 | tf_op jit(solution)/shard_map/ppermute | solution.py:377
  185.6 8.2 %collective-permute-start.13 = (bf16[16,2048]{1,0:T(8,128)(2,1)S(1)}, bf16[16,2048]{1,0:T(8,128)(2,1)S(1)}, u32[]{:S(2)}, u32[]{:S(2)}) collective-permute-start(bf16[16,2048]{1,0:T(8,128)(2,1)S(1)} %get-tuple-element.21), channel_id=1, source_target_pairs={{0,128},{64,192},{128,0},{192,64},{1,129},{65,193},{129,1},{193,65... | collective-permute-start | bytes 196616 | tf_op jit(solution)/shard_map/ppermute | solution.py:377
  186.1 8.3 %collective-permute-start.14 = (bf16[16,2048]{1,0:T(8,128)(2,1)S(1)}, bf16[16,2048]{1,0:T(8,128)(2,1)S(1)}, u32[]{:S(2)}, u32[]{:S(2)}) collective-permute-start(bf16[16,2048]{1,0:T(8,128)(2,1)S(1)} %get-tuple-element.20), channel_id=1, source_target_pairs={{0,64},{64,128},{128,192},{192,0},{1,65},{65,129},{129,193},{193,1... | collective-permute-start | bytes 196616 | tf_op jit(solution)/shard_map/ppermute | solution.py:377
where the time goes:
time: 198 us; the launch traced here: 195 us
  starting transfers between devices  76.3 us (39%)
  waiting for transfers between devices  54.2 us (27%)
  blocking collectives  17.7 us (9%)
  local copies, waits for them, and re-layouts  15.6 us (8%)
  Pallas kernels  14.1 us (7%)
  other arithmetic  9.64 us (5%)
  matrix products  6.99 us (4%)
    ppermute x4, starting transfers between devices, weight_pieces(): moved = lax.ppermute(packed[k], ('c', 'x', 'zl'), pairs)  32.9 us
    ppermute x4, waiting for transfers between devices, weight_pieces(): moved = lax.ppermute(packed[k], ('c', 'x', 'zl'), pairs)  21 us
    all_to_all x1, blocking collectives, spread(): return lax.all_to_all(copies, axes, 0, 0, tiled=True)  17.7 us
    unnamed x45, local copies, waits for them, and re-layouts  11.3 us
    all_to_all x1, waiting for transfers between devices, on_device(): lax.all_to_all(answers.reshape(Y * X * ZL, ZH * CAP, D), PLANE, 0, 0, til...  11.1 us
    ppermute x3, starting transfers between devices, on_device(): lax.ppermute(packet, 'zh', turned(ZH, k))  8.73 us
    all_to_all x1, starting transfers between devices, on_device(): lax.all_to_all(answers.reshape(Y * X * ZL, ZH * CAP, D), PLANE, 0, 0, til...  8.71 us
    all_to_all x1, waiting for transfers between devices, spread(): return lax.all_to_all(copies, axes, 0, 0, tiled=True)  8.62 us
  transfers between devices with their start and end apart: 20, of which 10 were waited for; matrix products, arithmetic and copies ran while one was open for 7% of the time, Pallas kernels for 2%

commit v1 on v0

--- a/solution.py
+++ b/solution.py
@@ -14,6 +14,7 @@
 HEAD = 128
 TOPK = 8
 CAP = 2
+SPAN = 512
 ZH, Y, C, X, ZL = 4, 4, 2, 4, 2
 SEC = ("zh", "y", "c")
 NARROW = ("x", "zl")
@@ -21,7 +22,7 @@
 
 norm_eps = 1e-06
 ATTEND_VMEM = 16 * 1024 * 1024
-EXPERT_VMEM = 24 * 1024 * 1024
+EXPERT_VMEM = 60 * 1024 * 1024
 BF = jnp.bfloat16
 F32 = jnp.float32
 
@@ -40,7 +41,9 @@
     return jnp.cos(angles), jnp.sin(angles)
 
 
-def attention_kernel(where_ref, q_ref, own_ref, other_ref, w_out_ref, out_ref, q_all, acc, peak, total, attended):
+def attention_kernel(
+    where_ref, q_ref, own_ref, other_ref, w_out_ref, out_ref, q_all, acc, peak, total, attended, out, sems
+):
     rows = q_ref.shape[0]
     heads = q_ref.shape[1] // HEAD
     pair_here = where_ref[0]
@@ -88,11 +91,17 @@
     for h in range(heads):
         part = slice(h * rows, (h + 1) * rows)
         attended[:, h * HEAD : (h + 1) * HEAD] = (acc[part, :] / summed[part]).astype(BF)
-    width = 512
-    for at in range(0, D, width):
-        out_ref[:, at : at + width] = jnp.dot(
-            attended[...], w_out_ref[:, at : at + width], preferred_element_type=F32
+    copies = []
+    for i in range(D // SPAN):
+        out[i] = jnp.dot(
+            attended[...], w_out_ref[:, i * SPAN : (i + 1) * SPAN], preferred_element_type=F32
         ).astype(BF)
+        copies.append(
+            pltpu.make_async_copy(out.at[i], out_ref.at[:, pl.ds(i * SPAN, SPAN)], sems.at[i])
+        )
+        copies[i].start()
+    for copy in copies:
+        copy.wait()
 
 
 def attention(where, query, own, other, w_out):
@@ -103,13 +112,15 @@
         attention_kernel,
         out_shape=jax.ShapeDtypeStruct((rows, D), BF),
         in_specs=[pl.BlockSpec(memory_space=pltpu.SMEM), vmem, vmem, vmem, vmem],
-        out_specs=vmem,
+        out_specs=pl.BlockSpec(memory_space=pltpu.HBM),
         scratch_shapes=[
             pltpu.VMEM((heads * rows, HEAD), BF),
             pltpu.VMEM((heads * rows, HEAD), F32),
             pltpu.VMEM((heads * rows, 1), F32),
             pltpu.VMEM((heads * rows, HEAD), F32),
             pltpu.VMEM((rows, heads * HEAD), BF),
+            pltpu.VMEM((D // SPAN, rows, SPAN), BF),
+            pltpu.SemaphoreType.DMA((D // SPAN,)),
         ],
         compiler_params=pltpu.CompilerParams(vmem_limit_bytes=ATTEND_VMEM),
         cost_estimate=pl.CostEstimate(
@@ -121,10 +132,10 @@
 
 def expert_kernel(rows_ref, *refs):
     pieces = refs[:8]
-    out_ref, weights, active, sems = refs[8:]
+    out_ref, weights, active, out, sems, out_sems = refs[8:]
     width = pieces[0].shape[0] // 3
 
-    def copy(part, i):
+    def fetch(part, i):
         return pltpu.make_async_copy(
             pieces[i].at[pl.ds(part * width, width)],
             weights.at[part, pl.ds(i * width, width)],
@@ -134,14 +145,14 @@
     for half in range(2):
         for part in range(2):
             for i in range(4):
-                copy(part, 4 * half + i).start()
+                fetch(part, 4 * half + i).start()
     for i in range(8):
-        copy(2, i).start()
+        fetch(2, i).start()
     rows = rows_ref[...]
     for half in range(2):
         for part in range(2):
             for i in range(4):
-                copy(part, 4 * half + i).wait()
+                fetch(part, 4 * half + i).wait()
         span = slice(4 * half * width, 4 * (half + 1) * width)
         gate = lax.dot_general(
             weights[0, span], rows, (((1,), (1,)), ((), ())), preferred_element_type=F32
@@ -151,13 +162,19 @@
         )
         active[span, :] = (gate / (1.0 + jnp.exp(-gate)) * up).astype(BF)
     for i in range(8):
-        copy(2, i).wait()
+        fetch(2, i).wait()
     acts = active[...].T
-    span = 512
-    for at in range(0, D, span):
-        out_ref[:, at : at + span] = jnp.dot(
-            acts, weights[2, :, at : at + span], preferred_element_type=F32
+    copies = []
+    for i in range(D // SPAN):
+        out[i] = jnp.dot(
+            acts, weights[2, :, i * SPAN : (i + 1) * SPAN], preferred_element_type=F32
         ).astype(BF)
+        copies.append(
+            pltpu.make_async_copy(out.at[i], out_ref.at[:, pl.ds(i * SPAN, SPAN)], out_sems.at[i])
+        )
+        copies[i].start()
+    for copy in copies:
+        copy.wait()
 
 
 def expert(rows, pieces):
@@ -169,11 +186,13 @@
         expert_kernel,
         out_shape=jax.ShapeDtypeStruct((count, D), BF),
         in_specs=[vmem] + [hbm] * 8,
-        out_specs=vmem,
+        out_specs=pl.BlockSpec(memory_space=pltpu.HBM),
         scratch_shapes=[
             pltpu.VMEM((3, 8 * width, D), BF),
             pltpu.VMEM((8 * width, count), BF),
+            pltpu.VMEM((D // SPAN, count, SPAN), BF),
             pltpu.SemaphoreType.DMA((3, 8)),
+            pltpu.SemaphoreType.DMA((D // SPAN,)),
         ],
         compiler_params=pltpu.CompilerParams(vmem_limit_bytes=EXPERT_VMEM),
         cost_estimate=pl.CostEstimate(

time: 198 us -> 192 us (0.970)
  local copies, waits for them, and re-layouts: 15.6 us -> 8.56 us
    unnamed x45 -> x35, local copies, waits for them, and re-layouts: 11.3 us -> 4.18 us
where the time goes in v1:
time: 192 us; the launch traced here: 189 us
  starting transfers between devices  76.1 us (40%)
  waiting for transfers between devices  55.4 us (29%)
  blocking collectives  17.7 us (9%)
  Pallas kernels  14.3 us (7%)
  other arithmetic  9.64 us (5%)
  local copies, waits for them, and re-layouts  8.56 us (4%)
  matrix products  6.98 us (4%)
    ppermute x4, starting transfers between devices, weight_pieces(): moved = lax.ppermute(packed[k], ('c', 'x', 'zl'), pairs)  32.9 us
    ppermute x4, waiting for transfers between devices, weight_pieces(): moved = lax.ppermute(packed[k], ('c', 'x', 'zl'), pairs)  21.1 us
    all_to_all x1, blocking collectives, spread(): return lax.all_to_all(copies, axes, 0, 0, tiled=True)  17.7 us
    all_to_all x1, waiting for transfers between devices, on_device(): lax.all_to_all(answers.reshape(Y * X * ZL, ZH * CAP, D), PLANE, 0, 0, til...  11.1 us
    all_to_all x1, starting transfers between devices, on_device(): lax.all_to_all(answers.reshape(Y * X * ZL, ZH * CAP, D), PLANE, 0, 0, til...  8.74 us
    ppermute x3, starting transfers between devices, on_device(): lax.ppermute(packet, 'zh', turned(ZH, k))  8.73 us
    all_to_all x1, waiting for transfers between devices, spread(): return lax.all_to_all(copies, axes, 0, 0, tiled=True)  8.63 us
    pallas_call x1, Pallas kernels, expert(): pl.pallas_call(expert_kernel, out_shape=jax.ShapeDtypeStruct((count, D),...  7.14 us
  transfers between devices with their start and end apart: 20, of which 10 were waited for; matrix products, arithmetic and copies ran while one was open for 7% of the time, Pallas kernels for 2%

profile of v1, /device:TPU:32, one launch (start us, length us, event | category | flops | bytes accessed | tf_op | source)
XLA Modules:
  0.0 189.3 jit_solution(13036166847730371612)
XLA Ops:
  0.0 1.4 fusion.1
  1.4 1.5 fusion.37
  3.0 0.4 fusion.35
  3.3 0.6 pad_maximum_fusion.7
  4.0 5.8 %all-to-all-start = ((f32[8,16,128]{2,1,0:T(8,128)}), f32[8,16,128]{2,1,0:T(8,128)S(1)}, u32[]{:S(2)}, u32[]{:S(2)}) async-start(f32[8,16,128]{2,1,0:T(8,128)} %bitcast.10), calls=%async_computation | async-start | bytes 131072 | tf_op jit(solution)/shard_map/all_to_all | solution.py:308
  9.8 5.0 %all-to-all-done = f32[8,16,128]{2,1,0:T(8,128)S(1)} async-done(((f32[8,16,128]{2,1,0:T(8,128)}), f32[8,16,128]{2,1,0:T(8,128)S(1)}, u32[]{:S(2)}, u32[]{:S(2)}) %all-to-all-start) | async-done | bytes 65568 | tf_op jit(solution)/shard_map/all_to_all | solution.py:308
  14.8 0.1 copy.65
  15.1 0.2 fusion.23
  15.3 17.7 %all_to_all.30 = bf16[8,128,128]{2,1,0:T(8,128)(2,1)S(1)} all-to-all(bf16[8,128,128]{2,1,0:T(8,128)(2,1)S(1)} %broadcast_in_dim.21), channel_id=1, replica_groups=mesh['zh'=4,'y'=4,'c'=2,'x'=4,'zl'=2] {'zh','zl'}, dimensions={0} | all-to-all | bytes 524288 | tf_op jit(solution)/shard_map/all_to_all | solution.py:241
  33.0 1.2 broadcast_in_dim.22
  34.3 4.5 %all-to-all-start.2 = ((bf16[4,8,128,128]{3,2,1,0:T(8,128)(2,1)}), bf16[4,8,128,128]{3,2,1,0:T(8,128)(2,1)S(1)}, u32[]{:S(2)}, u32[]{:S(2)}) async-start(bf16[4,8,128,128]{3,2,1,0:T(8,128)(2,1)} %broadcast_in_dim.22), calls=%async_computation.2 | async-start | bytes 2097152 | tf_op jit(solution)/shard_map/all_to_all | solution.py:241
  38.7 2.2 %fusion.39 = f32[128,512]{1,0:T(8,128)} fusion(bf16[2048,512]{1,0:T(8,128)(2,1)S(1)} %copy-done, bf16[128,2048]{1,0:T(8,128)(2,1)} %param.14, f32[2048]{0:T(1024)S(1)} %copy-done.9, f32[128]{0:T(128)S(1)} %add_rsqrt_fusion.3), kind=kOutput, calls=%fused_computation.96 | convolution fusion | flops 269484032 | bytes 2892288 | tf_op jit(solution)/shard_map/dot_general | solution.py:322
  41.0 1.0 reshape.252
  42.0 0.2 multiply_reduce_fusion
  42.2 8.6 %all-to-all-done.2 = bf16[4,8,128,128]{3,2,1,0:T(8,128)(2,1)S(1)} async-done(((bf16[4,8,128,128]{3,2,1,0:T(8,128)(2,1)}), bf16[4,8,128,128]{3,2,1,0:T(8,128)(2,1)S(1)}, u32[]{:S(2)}, u32[]{:S(2)}) %all-to-all-start.2) | async-done | bytes 1048608 | tf_op jit(solution)/shard_map/all_to_all | solution.py:241
  50.9 0.3 multiply_cosine_fusion
  51.2 0.2 multiply_multiply_fusion
  51.4 0.3 subtract_convert_fusion
  51.7 0.2 pad_maximum_fusion.6
  52.0 1.5 collective-permute-done.other_ref
  53.5 2.6 %attend.1 = bf16[128,2048]{1,0:T(8,128)(2,1)S(1)} custom-call(s32[2]{0:T(128)S(1)} %pad_add_fusion.where_ref, bf16[128,512]{1,0:T(8,128)(2,1)S(1)} %bitcast.58, bf16[4,4,2,128,128]{4,3,2,1,0:T(8,128)(2,1)S(1)} %bitcast.56, bf16[4,4,2,128,128]{4,3,2,1,0:T(8,128)(2,1)S(1)} %collective-permute-done.other_ref, bf16[512,2048]{1,0:T(8,128)(2,1)S(1)} %copy-done.2), custom_call_target="tpu_custom_call" | custom-call | flops 1400000000 | bytes 5000000 | tf_op jit(solution)/shard_map/attend/pallas_call | solution.py:111
  56.2 0.8 copy-done.1
  57.0 5.1 %all-to-all-start.3 = ((bf16[8,16,2048]{2,1,0:T(8,128)(2,1)}), bf16[8,16,2048]{2,1,0:T(8,128)(2,1)S(1)}, u32[]{:S(2)}, u32[]{:S(2)}) async-start(bf16[8,16,2048]{2,1,0:T(8,128)(2,1)} %bitcast.57), calls=%async_computation.3 | async-start | bytes 1048576 | tf_op jit(solution)/shard_map/all_to_all | solution.py:333
  62.0 4.6 %pack.1 = (bf16[288,2048]{1,0:T(8,128)(2,1)}, bf16[288,2048]{1,0:T(8,128)(2,1)}, bf16[288,2048]{1,0:T(8,128)(2,1)}, bf16[288,2048]{1,0:T(8,128)(2,1)}) custom-call(s32[1]{0:T(128)} %bitcast.19.x_ref, bf16[4,96,2048]{2,1,0:T(8,128)(2,1)} %bitcast.60, bf16[4,96,2048]{2,1,0:T(8,128)(2,1)} %bitcast.61, bf16[4,96,2048]{2,1,0:T(8,128)(2,1)} %down_ref.1), custom_call_target="tpu_custom_call" | custom-call | bytes 9500000 | tf_op jit(solution)/shard_map/pack/pallas_call | solution.py:228
  66.6 1.9 %collective-permute-start.4 = (bf16[288,2048]{1,0:T(8,128)(2,1)}, bf16[288,2048]{1,0:T(8,128)(2,1)}, u32[]{:S(2)}, u32[]{:S(2)}) collective-permute-start(bf16[288,2048]{1,0:T(8,128)(2,1)} %get-tuple-element.9), channel_id=1, source_target_pairs={{1,8},{3,10},{5,12},{7,14},{8,1},{10,3},{12,5},{14,7},{17,24},{19,... | collective-permute-start | bytes 3538952 | tf_op jit(solution)/shard_map/ppermute | solution.py:260
  68.5 4.3 %collective-permute-start.6 = (bf16[288,2048]{1,0:T(8,128)(2,1)}, bf16[288,2048]{1,0:T(8,128)(2,1)}, u32[]{:S(2)}, u32[]{:S(2)}) collective-permute-start(bf16[288,2048]{1,0:T(8,128)(2,1)} %get-tuple-element.11), channel_id=1, source_target_pairs={{0,4},{1,12},{2,6},{3,14},{4,0},{5,8},{6,2},{7,10},{8,5},{9,13},{1... | collective-permute-start | bytes 3538952 | tf_op jit(solution)/shard_map/ppermute | solution.py:260
  73.3 1.0 fusion.10
  74.4 0.1 concatenate.16
  74.5 1.7 collective-permute-start.1
  76.2 6.8 %collective-permute-start.2 = (bf16[16,2176]{1,0:T(8,128)(2,1)S(1)}, bf16[16,2176]{1,0:T(8,128)(2,1)S(1)}, u32[]{:S(2)}, u32[]{:S(2)}) collective-permute-start(bf16[16,2176]{1,0:T(8,128)(2,1)S(1)} %concatenate.16), channel_id=1, source_target_pairs={{0,128},{64,192},{128,0},{192,64},{1,129},{65,193},{129,1},{193,65... | collective-permute-start | bytes 208904 | tf_op jit(solution)/shard_map/ppermute | solution.py:354
  83.0 0.3 collective-permute-start.3
  83.2 26.7 %collective-permute-start.7 = (bf16[288,2048]{1,0:T(8,128)(2,1)}, bf16[288,2048]{1,0:T(8,128)(2,1)}, u32[]{:S(2)}, u32[]{:S(2)}) collective-permute-start(bf16[288,2048]{1,0:T(8,128)(2,1)} %get-tuple-element.12), channel_id=1, source_target_pairs={{0,6},{1,14},{2,0},{3,8},{4,2},{5,10},{6,4},{7,12},{8,7},{9,15},{1... | collective-permute-start | bytes 3538952 | tf_op jit(solution)/shard_map/ppermute | solution.py:260
  110.1 0.1 compare_reduce_fusion
  110.2 0.1 copy.69
  110.3 0.1 copy.70
  110.7 0.2 broadcast_and_fusion
  110.9 0.2 and.108
  111.1 1.4 fusion
  112.5 6.0 %all-to-all-start.4 = ((bf16[32,8,2048]{2,1,0:T(8,128)(2,1)}), bf16[32,8,2048]{2,1,0:T(8,128)(2,1)}, u32[]{:S(2)}, u32[]{:S(2)}) async-start(bf16[32,8,2048]{2,1,0:T(8,128)(2,1)} %fusion), calls=%async_computation.4 | async-start | bytes 2097152 | tf_op jit(solution)/shard_map/all_to_all | solution.py:380
  118.5 1.4 broadcast_select_fusion.refs_0_
  119.9 1.4 collective-permute-start.8
  121.3 0.1 collective-permute-start.10
  121.4 6.3 %collective-permute-done.7.refs_3_ = bf16[288,2048]{1,0:T(8,128)(2,1)} collective-permute-done((bf16[288,2048]{1,0:T(8,128)(2,1)}, bf16[288,2048]{1,0:T(8,128)(2,1)}, u32[]{:S(2)}, u32[]{:S(2)}) %collective-permute-start.7) | collective-permute-done | bytes 1179680 | tf_op jit(solution)/shard_map/ppermute | solution.py:260
  127.7 14.8 %collective-permute-done.5.refs_1_ = bf16[288,2048]{1,0:T(8,128)(2,1)} collective-permute-done((bf16[288,2048]{1,0:T(8,128)(2,1)}, bf16[288,2048]{1,0:T(8,128)(2,1)}, u32[]{:S(2)}, u32[]{:S(2)}) %collective-permute-start.5) | collective-permute-done | bytes 1179680 | tf_op jit(solution)/shard_map/ppermute | solution.py:260
  142.6 1.0 copy-done.5
  143.6 1.0 copy-done.6
  144.6 1.1 copy-done.7
  145.7 2.1 %all-to-all-done.4 = bf16[32,8,2048]{2,1,0:T(8,128)(2,1)} async-done(((bf16[32,8,2048]{2,1,0:T(8,128)(2,1)}), bf16[32,8,2048]{2,1,0:T(8,128)(2,1)}, u32[]{:S(2)}, u32[]{:S(2)}) %all-to-all-start.4) | async-done | bytes 1048608 | tf_op jit(solution)/shard_map/all_to_all | solution.py:380
  147.9 7.1 %expert.1 = bf16[256,2048]{1,0:T(8,128)(2,1)} custom-call(bf16[256,2048]{1,0:T(8,128)(2,1)} %bitcast.18.rows_ref, bf16[288,2048]{1,0:T(8,128)(2,1)} %copy-done.3, bf16[288,2048]{1,0:T(8,128)(2,1)} %collective-permute-done.5.refs_1_, bf16[288,2048]{1,0:T(8,128)(2,1)} %collective-permute-done.6.refs_2_, bf16[288,2048]{1,0:T(8,128)(2,1)} %collective-permute-done.7.refs_3_, ...), custom_call_target="tpu_custom_call" | custom-call | flops 2400000000 | bytes 11500000 | tf_op jit(solution)/shard_map/expert/pallas_call | solution.py:185
  155.0 8.7 %all-to-all-start.5 = ((bf16[32,8,2048]{2,1,0:T(8,128)(2,1)}), bf16[32,8,2048]{2,1,0:T(8,128)(2,1)S(1)}, u32[]{:S(2)}, u32[]{:S(2)}) async-start(bf16[32,8,2048]{2,1,0:T(8,128)(2,1)} %bitcast.59), calls=%async_computation.5 | async-start | bytes 2097152 | tf_op jit(solution)/shard_map/all_to_all | solution.py:384
  163.9 0.1 fusion.9
  164.1 1.0 fusion.7
  165.2 0.8 convert_element_type.157
  166.0 1.0 select_convert_fusion
  166.9 0.2 convert_element_type.153
  167.1 11.1 %all-to-all-done.5 = bf16[32,8,2048]{2,1,0:T(8,128)(2,1)S(1)} async-done(((bf16[32,8,2048]{2,1,0:T(8,128)(2,1)}), bf16[32,8,2048]{2,1,0:T(8,128)(2,1)S(1)}, u32[]{:S(2)}, u32[]{:S(2)}) %all-to-all-start.5) | async-done | bytes 1048608 | tf_op jit(solution)/shard_map/all_to_all | solution.py:384
  178.2 1.2 fusion.4
  179.4 0.3 fusion.44
  179.8 0.4 collective-permute-start.13
  180.3 2.5 %collective-permute-start.14 = (bf16[16,2048]{1,0:T(8,128)(2,1)S(1)}, bf16[16,2048]{1,0:T(8,128)(2,1)S(1)}, u32[]{:S(2)}, u32[]{:S(2)}) collective-permute-start(bf16[16,2048]{1,0:T(8,128)(2,1)S(1)} %get-tuple-element.20), channel_id=1, source_target_pairs={{0,64},{64,128},{128,192},{192,0},{1,65},{65,129},{129,193},{193,1... | collective-permute-start | bytes 196616 | tf_op jit(solution)/shard_map/ppermute | solution.py:396
  182.7 2.3 %collective-permute-done.12 = bf16[16,2048]{1,0:T(8,128)(2,1)S(1)} collective-permute-done((bf16[16,2048]{1,0:T(8,128)(2,1)S(1)}, bf16[16,2048]{1,0:T(8,128)(2,1)S(1)}, u32[]{:S(2)}, u32[]{:S(2)}) %collective-permute-start.12) | collective-permute-done | bytes 65568 | tf_op jit(solution)/shard_map/ppermute | solution.py:396
  185.0 3.0 %collective-permute-done.13 = bf16[16,2048]{1,0:T(8,128)(2,1)S(1)} collective-permute-done((bf16[16,2048]{1,0:T(8,128)(2,1)S(1)}, bf16[16,2048]{1,0:T(8,128)(2,1)S(1)}, u32[]{:S(2)}, u32[]{:S(2)}) %collective-permute-start.13) | collective-permute-done | bytes 65568 | tf_op jit(solution)/shard_map/ppermute | solution.py:396
  188.1 0.5 collective-permute-done.14
  188.6 0.7 fusion.16
  (79 shorter events, 1.7 us)
Async XLA Ops:
  0.0 38.7 %copy-start = (bf16[2048,512]{1,0:T(8,128)(2,1)S(1)}, bf16[2048,512]{1,0:T(8,128)(2,1)}, u32[]{:S(2)}) copy-start(bf16[2048,512]{1,0:T(8,128)(2,1)} %param.16) | copy-start | bytes 6291460
  0.0 2.9 %copy-start.4 = (bf16[128,2048]{1,0:T(8,128)(2,1)S(1)}, bf16[128,2048]{1,0:T(8,128)(2,1)}, u32[]{:S(2)}) copy-start(bf16[128,2048]{1,0:T(8,128)(2,1)} %param.14) | copy-start | bytes 1572868
  0.0 2.9 %copy-start.9 = (f32[2048]{0:T(1024)S(1)}, f32[2048]{0:T(1024)}, u32[]{:S(2)}) copy-start(f32[2048]{0:T(1024)} %param.15) | copy-start | bytes 24580
  0.0 2.9 %copy-start.15 = (bf16[2048,64]{0,1:T(8,128)(2,1)S(1)}, bf16[2048,64]{0,1:T(8,128)(2,1)}, u32[]{:S(2)}) copy-start(bf16[2048,64]{0,1:T(8,128)(2,1)} %param.18) | copy-start | bytes 786436
  1.4 13.6 %copy-start.13 = (f32[128]{0:T(128)S(1)}, f32[128]{0:T(128)}, u32[]{:S(2)}) copy-start(f32[128]{0:T(128)} %param.20) | copy-start | bytes 1540
  4.0 10.8 %all-to-all-start = ((f32[8,16,128]{2,1,0:T(8,128)}), f32[8,16,128]{2,1,0:T(8,128)S(1)}, u32[]{:S(2)}, u32[]{:S(2)}) async-start(f32[8,16,128]{2,1,0:T(8,128)} %bitcast.10), calls=%async_computation | async-start | bytes 131072 | tf_op jit(solution)/shard_map/all_to_all | solution.py:308
  34.3 16.6 %all-to-all-start.2 = ((bf16[4,8,128,128]{3,2,1,0:T(8,128)(2,1)}), bf16[4,8,128,128]{3,2,1,0:T(8,128)(2,1)S(1)}, u32[]{:S(2)}, u32[]{:S(2)}) async-start(bf16[4,8,128,128]{3,2,1,0:T(8,128)(2,1)} %broadcast_in_dim.22), calls=%async_computation.2 | async-start | bytes 2097152 | tf_op jit(solution)/shard_map/all_to_all | solution.py:241
  38.7 12.5 %copy-start.14 = (f32[128]{0:T(128)S(1)}, f32[128]{0:T(128)}, u32[]{:S(2)}) copy-start(f32[128]{0:T(128)} %param.19) | copy-start | bytes 1540
  50.8 2.7 %collective-permute-start = (bf16[4,4,2,128,128]{4,3,2,1,0:T(8,128)(2,1)S(1)}, bf16[4,4,2,128,128]{4,3,2,1,0:T(8,128)(2,1)S(1)}, u32[]{:S(2)}, u32[]{:S(2)}) collective-permute-start(bf16[4,4,2,128,128]{4,3,2,1,0:T(8,128)(2,1)S(1)} %bitcast.55), channel_id=1, source_target_pairs={{0,8},{8,0},{1,9},{9,1},{2,10},{10,2},{3,11},{11,3},{4,12},{12,4},... | collective-permute-start | bytes 3145736 | tf_op jit(solution)/shard_map/ppermute | solution.py:320
  50.9 2.6 %copy-start.2 = (bf16[512,2048]{1,0:T(8,128)(2,1)S(1)}, bf16[512,2048]{1,0:T(8,128)(2,1)}, u32[]{:S(2)}) copy-start(bf16[512,2048]{1,0:T(8,128)(2,1)} %w_out_ref.1) | copy-start | bytes 6291460
  56.2 0.8 copy-start.1
  57.0 16.2 %all-to-all-start.3 = ((bf16[8,16,2048]{2,1,0:T(8,128)(2,1)}), bf16[8,16,2048]{2,1,0:T(8,128)(2,1)S(1)}, u32[]{:S(2)}, u32[]{:S(2)}) async-start(bf16[8,16,2048]{2,1,0:T(8,128)(2,1)} %bitcast.57), calls=%async_computation.3 | async-start | bytes 1048576 | tf_op jit(solution)/shard_map/all_to_all | solution.py:333
  62.0 10.8 %copy-start.11 = (f32[128,8]{0,1:T(8,128)S(1)}, f32[128,8]{0,1:T(8,128)}, u32[]{:S(2)}) copy-start(f32[128,8]{0,1:T(8,128)} %param.24) | copy-start | bytes 12292
  62.0 10.9 %copy-start.12 = (s32[128,8]{0,1:T(8,128)S(1)}, s32[128,8]{0,1:T(8,128)}, u32[]{:S(2)}) copy-start(s32[128,8]{0,1:T(8,128)} %param.23) | copy-start | bytes 12292
  62.0 12.2 %copy-start.10 = (f32[2048]{0:T(1024)S(1)}, f32[2048]{0:T(1024)}, u32[]{:S(2)}) copy-start(f32[2048]{0:T(1024)} %param.22) | copy-start | bytes 24580
  66.6 51.9 %collective-permute-start.4 = (bf16[288,2048]{1,0:T(8,128)(2,1)}, bf16[288,2048]{1,0:T(8,128)(2,1)}, u32[]{:S(2)}, u32[]{:S(2)}) collective-permute-start(bf16[288,2048]{1,0:T(8,128)(2,1)} %get-tuple-element.9), channel_id=1, source_target_pairs={{1,8},{3,10},{5,12},{7,14},{8,1},{10,3},{12,5},{14,7},{17,24},{19,... | collective-permute-start | bytes 3538952 | tf_op jit(solution)/shard_map/ppermute | solution.py:260
  68.5 52.8 %collective-permute-start.6 = (bf16[288,2048]{1,0:T(8,128)(2,1)}, bf16[288,2048]{1,0:T(8,128)(2,1)}, u32[]{:S(2)}, u32[]{:S(2)}) collective-permute-start(bf16[288,2048]{1,0:T(8,128)(2,1)} %get-tuple-element.11), channel_id=1, source_target_pairs={{0,4},{1,12},{2,6},{3,14},{4,0},{5,8},{6,2},{7,10},{8,5},{9,13},{1... | collective-permute-start | bytes 3538952 | tf_op jit(solution)/shard_map/ppermute | solution.py:260
  74.5 8.7 %collective-permute-start.1 = (bf16[16,2176]{1,0:T(8,128)(2,1)S(1)}, bf16[16,2176]{1,0:T(8,128)(2,1)S(1)}, u32[]{:S(2)}, u32[]{:S(2)}) collective-permute-start(bf16[16,2176]{1,0:T(8,128)(2,1)S(1)} %concatenate.16), channel_id=1, source_target_pairs={{0,64},{64,128},{128,192},{192,0},{1,65},{65,129},{129,193},{193,1... | collective-permute-start | bytes 208904 | tf_op jit(solution)/shard_map/ppermute | solution.py:354
  76.2 33.8 %collective-permute-start.2 = (bf16[16,2176]{1,0:T(8,128)(2,1)S(1)}, bf16[16,2176]{1,0:T(8,128)(2,1)S(1)}, u32[]{:S(2)}, u32[]{:S(2)}) collective-permute-start(bf16[16,2176]{1,0:T(8,128)(2,1)S(1)} %concatenate.16), channel_id=1, source_target_pairs={{0,128},{64,192},{128,0},{192,64},{1,129},{65,193},{129,1},{193,65... | collective-permute-start | bytes 208904 | tf_op jit(solution)/shard_map/ppermute | solution.py:354
  83.0 27.0 %collective-permute-start.3 = (bf16[16,2176]{1,0:T(8,128)(2,1)S(1)}, bf16[16,2176]{1,0:T(8,128)(2,1)S(1)}, u32[]{:S(2)}, u32[]{:S(2)}) collective-permute-start(bf16[16,2176]{1,0:T(8,128)(2,1)S(1)} %concatenate.16), channel_id=1, source_target_pairs={{0,192},{64,0},{128,64},{192,128},{1,193},{65,1},{129,65},{193,129... | collective-permute-start | bytes 208904 | tf_op jit(solution)/shard_map/ppermute | solution.py:354
  83.2 44.5 %collective-permute-start.7 = (bf16[288,2048]{1,0:T(8,128)(2,1)}, bf16[288,2048]{1,0:T(8,128)(2,1)}, u32[]{:S(2)}, u32[]{:S(2)}) collective-permute-start(bf16[288,2048]{1,0:T(8,128)(2,1)} %get-tuple-element.12), channel_id=1, source_target_pairs={{0,6},{1,14},{2,0},{3,8},{4,2},{5,10},{6,4},{7,12},{8,7},{9,15},{1... | collective-permute-start | bytes 3538952 | tf_op jit(solution)/shard_map/ppermute | solution.py:260
  109.9 32.6 %collective-permute-start.5 = (bf16[288,2048]{1,0:T(8,128)(2,1)}, bf16[288,2048]{1,0:T(8,128)(2,1)}, u32[]{:S(2)}, u32[]{:S(2)}) collective-permute-start(bf16[288,2048]{1,0:T(8,128)(2,1)} %get-tuple-element.10), channel_id=1, source_target_pairs={{0,2},{1,10},{2,4},{3,12},{4,6},{5,14},{6,0},{7,8},{8,3},{9,11},{1... | collective-permute-start | bytes 3538952 | tf_op jit(solution)/shard_map/ppermute | solution.py:260
  110.7 1.8 copy-start.8
  112.5 35.4 %all-to-all-start.4 = ((bf16[32,8,2048]{2,1,0:T(8,128)(2,1)}), bf16[32,8,2048]{2,1,0:T(8,128)(2,1)}, u32[]{:S(2)}, u32[]{:S(2)}) async-start(bf16[32,8,2048]{2,1,0:T(8,128)(2,1)} %fusion), calls=%async_computation.4 | async-start | bytes 2097152 | tf_op jit(solution)/shard_map/all_to_all | solution.py:380
  119.9 28.0 %copy-start.3 = (bf16[288,2048]{1,0:T(8,128)(2,1)}, bf16[288,2048]{1,0:T(8,128)(2,1)S(1)}, u32[]{:S(2)}) copy-start(bf16[288,2048]{1,0:T(8,128)(2,1)S(1)} %broadcast_select_fusion.refs_0_) | copy-start | bytes 3538948
  119.9 22.7 %collective-permute-start.8 = (bf16[288,2048]{1,0:T(8,128)(2,1)S(1)}, bf16[288,2048]{1,0:T(8,128)(2,1)S(1)}, u32[]{:S(2)}, u32[]{:S(2)}) collective-permute-start(bf16[288,2048]{1,0:T(8,128)(2,1)S(1)} %broadcast_select_fusion.refs_0_), channel_id=1, source_target_pairs={{0,8},{8,0},{1,9},{9,1},{2,10},{10,2},{3,11},{11,3},{4,12},{12,4},... | collective-permute-start | bytes 3538952 | tf_op jit(solution)/shard_map/ppermute | solution.py:266
  121.3 22.3 %collective-permute-start.10 = (bf16[288,2048]{1,0:T(8,128)(2,1)}, bf16[288,2048]{1,0:T(8,128)(2,1)S(1)}, u32[]{:S(2)}, u32[]{:S(2)}) collective-permute-start(bf16[288,2048]{1,0:T(8,128)(2,1)} %collective-permute-done.6.refs_2_), channel_id=1, source_target_pairs={{0,8},{8,0},{1,9},{9,1},{2,10},{10,2},{3,11},{11,3},{4,12},{12,4},... | collective-permute-start | bytes 3538952 | tf_op jit(solution)/shard_map/ppermute | solution.py:266
  127.7 16.9 %collective-permute-start.11 = (bf16[288,2048]{1,0:T(8,128)(2,1)}, bf16[288,2048]{1,0:T(8,128)(2,1)S(1)}, u32[]{:S(2)}, u32[]{:S(2)}) collective-permute-start(bf16[288,2048]{1,0:T(8,128)(2,1)} %collective-permute-done.7.refs_3_), channel_id=1, source_target_pairs={{0,8},{8,0},{1,9},{9,1},{2,10},{10,2},{3,11},{11,3},{4,12},{12,4},... | collective-permute-start | bytes 3538952 | tf_op jit(solution)/shard_map/ppermute | solution.py:266
  142.6 3.2 %collective-permute-start.9 = (bf16[288,2048]{1,0:T(8,128)(2,1)}, bf16[288,2048]{1,0:T(8,128)(2,1)}, u32[]{:S(2)}, u32[]{:S(2)}) collective-permute-start(bf16[288,2048]{1,0:T(8,128)(2,1)} %collective-permute-done.5.refs_1_), channel_id=1, source_target_pairs={{0,8},{8,0},{1,9},{9,1},{2,10},{10,2},{3,11},{11,3},{4,12},{12,4},... | collective-permute-start | bytes 3538952 | tf_op jit(solution)/shard_map/ppermute | solution.py:266
  142.6 1.0 copy-start.5
  143.6 1.0 copy-start.6
  144.6 1.1 copy-start.7
  155.0 23.2 %all-to-all-start.5 = ((bf16[32,8,2048]{2,1,0:T(8,128)(2,1)}), bf16[32,8,2048]{2,1,0:T(8,128)(2,1)S(1)}, u32[]{:S(2)}, u32[]{:S(2)}) async-start(bf16[32,8,2048]{2,1,0:T(8,128)(2,1)} %bitcast.59), calls=%async_computation.5 | async-start | bytes 2097152 | tf_op jit(solution)/shard_map/all_to_all | solution.py:384
  179.7 5.3 %collective-permute-start.12 = (bf16[16,2048]{1,0:T(8,128)(2,1)S(1)}, bf16[16,2048]{1,0:T(8,128)(2,1)S(1)}, u32[]{:S(2)}, u32[]{:S(2)}) collective-permute-start(bf16[16,2048]{1,0:T(8,128)(2,1)S(1)} %get-tuple-element.19), channel_id=1, source_target_pairs={{0,192},{64,0},{128,64},{192,128},{1,193},{65,1},{129,65},{193,129... | collective-permute-start | bytes 196616 | tf_op jit(solution)/shard_map/ppermute | solution.py:396
  179.8 8.3 %collective-permute-start.13 = (bf16[16,2048]{1,0:T(8,128)(2,1)S(1)}, bf16[16,2048]{1,0:T(8,128)(2,1)S(1)}, u32[]{:S(2)}, u32[]{:S(2)}) collective-permute-start(bf16[16,2048]{1,0:T(8,128)(2,1)S(1)} %get-tuple-element.21), channel_id=1, source_target_pairs={{0,128},{64,192},{128,0},{192,64},{1,129},{65,193},{129,1},{193,65... | collective-permute-start | bytes 196616 | tf_op jit(solution)/shard_map/ppermute | solution.py:396
  180.3 8.3 %collective-permute-start.14 = (bf16[16,2048]{1,0:T(8,128)(2,1)S(1)}, bf16[16,2048]{1,0:T(8,128)(2,1)S(1)}, u32[]{:S(2)}, u32[]{:S(2)}) collective-permute-start(bf16[16,2048]{1,0:T(8,128)(2,1)S(1)} %get-tuple-element.20), channel_id=1, source_target_pairs={{0,64},{64,128},{128,192},{192,0},{1,65},{65,129},{129,193},{193,1... | collective-permute-start | bytes 196616 | tf_op jit(solution)/shard_map/ppermute | solution.py:396

commit v2 on v1

--- a/solution.py
+++ b/solution.py
@@ -314,7 +314,23 @@
         [lead * cos_t - trail * sin_t, trail * cos_t + lead * sin_t], axis=0
     ).astype(BF)
     piece = jnp.where(zl == 0, key_t, one.T.astype(BF))
-    ring = spread(piece, ("zh", "zl"), ZH * ZL)
+
+    ids = lax.dynamic_slice_in_dim(expert_ids, narrow * share, share, 0)
+    weights = lax.dynamic_slice_in_dim(expert_weights, narrow * share, share, 0)
+    gates = weights / jnp.sum(weights, axis=-1, keepdims=True)
+    gates_high = gates.astype(BF)
+    gates_low = (gates - gates_high.astype(F32)).astype(BF)
+    tail = jnp.concatenate(
+        [ids.astype(BF), gates_high, gates_low, jnp.zeros((share, HEAD - 3 * TOPK), BF)], axis=1
+    )
+    ring = spread(jnp.concatenate([piece, tail], axis=0), ("zh", "zl"), ZH * ZL)
+    tails = ring[:, HEAD:].reshape(ZH, ZL, share, HEAD)
+    tails = lax.dynamic_index_in_dim(tails, zl, 1, keepdims=False)
+    routes = jnp.concatenate(
+        [lax.dynamic_index_in_dim(tails, (zh - k) % ZH, 0, keepdims=False) for k in range(ZH)],
+        axis=0,
+    ).astype(F32)
+    ring = ring[:, :HEAD]
     own = spread(ring, "y", Y)
     own = own.reshape(Y, ZH, ZL, HEAD, HEAD)
     other = lax.ppermute(own, "c", [(0, 1), (1, 0)])
@@ -336,25 +352,8 @@
     carried = (own_tokens.astype(F32) + mixed).astype(BF)
     moe_in = rms_norm(carried, moe_gain).astype(BF)
 
-    ids = lax.dynamic_slice_in_dim(expert_ids, narrow * share, share, 0)
-    weights = lax.dynamic_slice_in_dim(expert_weights, narrow * share, share, 0)
-    gates = weights / jnp.sum(weights, axis=-1, keepdims=True)
-    gates_high = gates.astype(BF)
-    gates_low = (gates - gates_high.astype(F32)).astype(BF)
-    tail = jnp.concatenate(
-        [
-            ids.astype(BF),
-            gates_high,
-            gates_low,
-            jnp.zeros((share, 128 - 3 * TOPK), BF),
-        ],
-        axis=1,
-    )
-    packet = jnp.concatenate([moe_in, tail], axis=1)
-    packets = [packet] + [lax.ppermute(packet, "zh", turned(ZH, k)) for k in range(1, ZH)]
-    packets = jnp.concatenate(packets, axis=0)
-    rows = packets[:, :D]
-    routes = packets[:, D:].astype(F32)
+    rows = [moe_in] + [lax.ppermute(moe_in, "zh", turned(ZH, k)) for k in range(1, ZH)]
+    rows = jnp.concatenate(rows, axis=0)
     ids_f = routes[:, :TOPK]
     gates_all = routes[:, TOPK : 2 * TOPK] + routes[:, 2 * TOPK : 3 * TOPK]
     chips = jnp.arange(Y * X * ZL, dtype=jnp.int32)

time: 192 us -> 213 us (1.11)
  waiting for transfers between devices: 55.4 us -> 85.9 us
  starting transfers between devices: 76.1 us -> 64.9 us
    ppermute x3, waiting for transfers between devices: 0.01 us -> 48.9 us  [on_device(): lax.ppermute(moe_in, 'zh', turned(ZH, k))]
    ppermute x4, starting transfers between devices: 32.9 us -> 9.41 us  [weight_pieces(): moved = lax.ppermute(packed[k], ('c', 'x', 'zl'), pairs)]
    ppermute x4, waiting for transfers between devices: 21.1 us -> 0.01 us  [weight_pieces(): moved = lax.ppermute(packed[k], ('c', 'x', 'zl'), pairs)]
    ppermute x3, starting transfers between devices: 8.73 us -> 16.1 us  [on_device(): lax.ppermute(moe_in, 'zh', turned(ZH, k))]
    ppermute x3, starting transfers between devices: 3 us -> 10.2 us  [on_device(): back = lax.ppermute(sums[k].astype(BF), 'zh', turned(ZH, -k))]
    ppermute x3, waiting for transfers between devices: 5.84 us -> 1.9 us  [on_device(): back = lax.ppermute(sums[k].astype(BF), 'zh', turned(ZH, -k))]
    ppermute x4, waiting for transfers between devices: 0.01 us -> 3.89 us  [weight_pieces(): other.append(lax.ppermute(own[k], 'c', [(0, 1), (1, 0)]))]
    all_to_all x1, starting transfers between devices: 8.74 us -> 5.39 us  [on_device(): lax.all_to_all(answers.reshape(Y * X * ZL, ZH * CAP, D), PLANE, 0, 0, til...]
  transfers between devices with their start and end apart: 20 -> 20, of which waited for: 10 -> 14; matrix products, arithmetic and copies ran while one was open for 7% -> 7% of each run, Pallas kernels for 2% -> 2%
where the time goes in v2:
time: 213 us; the launch traced here: 210 us
  waiting for transfers between devices  85.9 us (40%)
  starting transfers between devices  64.9 us (30%)
  blocking collectives  18.3 us (9%)
  Pallas kernels  14.3 us (7%)
  other arithmetic  9.78 us (5%)
  local copies, waits for them, and re-layouts  9.54 us (4%)
  matrix products  6.98 us (3%)
    ppermute x3, waiting for transfers between devices, on_device(): lax.ppermute(moe_in, 'zh', turned(ZH, k))  48.9 us
    all_to_all x1, blocking collectives, spread(): return lax.all_to_all(copies, axes, 0, 0, tiled=True)  18.3 us
    ppermute x3, starting transfers between devices, on_device(): lax.ppermute(moe_in, 'zh', turned(ZH, k))  16.1 us
    all_to_all x1, waiting for transfers between devices, on_device(): lax.all_to_all(answers.reshape(Y * X * ZL, ZH * CAP, D), PLANE, 0, 0, til...  13.6 us
    ppermute x3, starting transfers between devices, on_device(): back = lax.ppermute(sums[k].astype(BF), 'zh', turned(ZH, -k))  10.2 us
    ppermute x4, starting transfers between devices, weight_pieces(): moved = lax.ppermute(packed[k], ('c', 'x', 'zl'), pairs)  9.41 us
    all_to_all x1, waiting for transfers between devices, spread(): return lax.all_to_all(copies, axes, 0, 0, tiled=True)  8.47 us
    all_to_all x1, starting transfers between devices, on_device(): lax.all_to_all(outgoing.reshape(Y * X * ZL, ZH * CAP, D), PLANE, 0, 0, ti...  7.55 us
  transfers between devices with their start and end apart: 20, of which 14 were waited for; matrix products, arithmetic and copies ran while one was open for 7% of the time, Pallas kernels for 2%

profile of v2, /device:TPU:32, one launch (start us, length us, event | category | flops | bytes accessed | tf_op | source)
XLA Modules:
  0.0 210.2 jit_solution(17197939985005444660)
XLA Ops:
  0.0 1.4 fusion.1
  1.4 1.5 fusion.41
  3.0 0.4 fusion.43
  3.4 0.6 pad_maximum_fusion.1
  4.0 5.8 %all-to-all-start = ((f32[8,16,128]{2,1,0:T(8,128)}), f32[8,16,128]{2,1,0:T(8,128)S(1)}, u32[]{:S(2)}, u32[]{:S(2)}) async-start(f32[8,16,128]{2,1,0:T(8,128)} %bitcast.10), calls=%async_computation | async-start | bytes 131072 | tf_op jit(solution)/shard_map/all_to_all | solution.py:308
  10.2 4.6 %all-to-all-done = f32[8,16,128]{2,1,0:T(8,128)S(1)} async-done(((f32[8,16,128]{2,1,0:T(8,128)}), f32[8,16,128]{2,1,0:T(8,128)S(1)}, u32[]{:S(2)}, u32[]{:S(2)}) %all-to-all-start) | async-done | bytes 65568 | tf_op jit(solution)/shard_map/all_to_all | solution.py:308
  15.1 0.2 fusion.29
  15.5 18.3 %all_to_all.30 = bf16[8,144,128]{2,1,0:T(8,128)(2,1)S(1)} all-to-all(bf16[8,144,128]{2,1,0:T(8,128)(2,1)S(1)} %broadcast_in_dim.22), channel_id=1, replica_groups=mesh['zh'=4,'y'=4,'c'=2,'x'=4,'zl'=2] {'zh','zl'}, dimensions={0} | all-to-all | bytes 589824 | tf_op jit(solution)/shard_map/all_to_all | solution.py:241
  33.8 0.7 copy-done.5
  34.5 1.3 broadcast_in_dim.23
  35.8 4.5 %all-to-all-start.2 = ((bf16[4,8,128,128]{3,2,1,0:T(8,128)(2,1)}), bf16[4,8,128,128]{3,2,1,0:T(8,128)(2,1)S(1)}, u32[]{:S(2)}, u32[]{:S(2)}) async-start(bf16[4,8,128,128]{3,2,1,0:T(8,128)(2,1)} %broadcast_in_dim.23), calls=%async_computation.2 | async-start | bytes 2097152 | tf_op jit(solution)/shard_map/all_to_all | solution.py:241
  40.3 2.2 %fusion.45 = f32[128,512]{1,0:T(8,128)} fusion(bf16[2048,512]{1,0:T(8,128)(2,1)S(1)} %copy-done, bf16[128,2048]{1,0:T(8,128)(2,1)} %param.14, f32[2048]{0:T(1024)S(1)} %copy-done.10, f32[128]{0:T(128)S(1)} %add_rsqrt_fusion.3), kind=kOutput, calls=%fused_computation.107 | convolution fusion | flops 269484032 | bytes 2892288 | tf_op jit(solution)/shard_map/dot_general | solution.py:338
  42.5 1.0 reshape.263
  43.5 0.2 multiply_reduce_fusion
  43.8 8.5 %all-to-all-done.2 = bf16[4,8,128,128]{3,2,1,0:T(8,128)(2,1)S(1)} async-done(((bf16[4,8,128,128]{3,2,1,0:T(8,128)(2,1)}), bf16[4,8,128,128]{3,2,1,0:T(8,128)(2,1)S(1)}, u32[]{:S(2)}, u32[]{:S(2)}) %all-to-all-start.2) | async-done | bytes 1048608 | tf_op jit(solution)/shard_map/all_to_all | solution.py:241
  52.3 0.3 multiply_cosine_fusion
  52.6 0.2 multiply_multiply_fusion
  52.8 0.3 subtract_convert_fusion
  53.1 0.2 pad_maximum_fusion
  53.4 1.5 collective-permute-done.other_ref
  54.9 2.6 %attend.1 = bf16[128,2048]{1,0:T(8,128)(2,1)S(1)} custom-call(s32[2]{0:T(128)S(1)} %pad_add_fusion.where_ref, bf16[128,512]{1,0:T(8,128)(2,1)S(1)} %bitcast.63, bf16[4,4,2,128,128]{4,3,2,1,0:T(8,128)(2,1)S(1)} %bitcast.61, bf16[4,4,2,128,128]{4,3,2,1,0:T(8,128)(2,1)S(1)} %collective-permute-done.other_ref, bf16[512,2048]{1,0:T(8,128)(2,1)S(1)} %copy-done.2), custom_call_target="tpu_custom_call" | custom-call | flops 1400000000 | bytes 5000000 | tf_op jit(solution)/shard_map/attend/pallas_call | solution.py:111
  57.6 0.8 copy-done.1
  58.3 5.0 %all-to-all-start.3 = ((bf16[8,16,2048]{2,1,0:T(8,128)(2,1)}), bf16[8,16,2048]{2,1,0:T(8,128)(2,1)S(1)}, u32[]{:S(2)}, u32[]{:S(2)}) async-start(bf16[8,16,2048]{2,1,0:T(8,128)(2,1)} %bitcast.62), calls=%async_computation.3 | async-start | bytes 1048576 | tf_op jit(solution)/shard_map/all_to_all | solution.py:349
  63.3 4.6 %pack.1 = (bf16[288,2048]{1,0:T(8,128)(2,1)}, bf16[288,2048]{1,0:T(8,128)(2,1)}, bf16[288,2048]{1,0:T(8,128)(2,1)}, bf16[288,2048]{1,0:T(8,128)(2,1)}) custom-call(s32[1]{0:T(128)} %bitcast.24.x_ref, bf16[4,96,2048]{2,1,0:T(8,128)(2,1)} %bitcast.65, bf16[4,96,2048]{2,1,0:T(8,128)(2,1)} %bitcast.66, bf16[4,96,2048]{2,1,0:T(8,128)(2,1)} %down_ref.1), custom_call_target="tpu_custom_call" | custom-call | bytes 9500000 | tf_op jit(solution)/shard_map/pack/pallas_call | solution.py:228
  67.9 1.9 collective-permute-start.4
  69.8 2.7 %collective-permute-start.5 = (bf16[288,2048]{1,0:T(8,128)(2,1)}, bf16[288,2048]{1,0:T(8,128)(2,1)}, u32[]{:S(2)}, u32[]{:S(2)}) collective-permute-start(bf16[288,2048]{1,0:T(8,128)(2,1)} %get-tuple-element.10), channel_id=1, source_target_pairs={{0,2},{1,10},{2,4},{3,12},{4,6},{5,14},{6,0},{7,8},{8,3},{9,11},{1... | collective-permute-start | bytes 3538952 | tf_op jit(solution)/shard_map/ppermute | solution.py:260
  72.6 2.2 %collective-permute-start.6 = (bf16[288,2048]{1,0:T(8,128)(2,1)}, bf16[288,2048]{1,0:T(8,128)(2,1)}, u32[]{:S(2)}, u32[]{:S(2)}) collective-permute-start(bf16[288,2048]{1,0:T(8,128)(2,1)} %get-tuple-element.11), channel_id=1, source_target_pairs={{0,4},{1,12},{2,6},{3,14},{4,0},{5,8},{6,2},{7,10},{8,5},{9,13},{1... | collective-permute-start | bytes 3538952 | tf_op jit(solution)/shard_map/ppermute | solution.py:260
  74.7 2.6 %collective-permute-start.7 = (bf16[288,2048]{1,0:T(8,128)(2,1)}, bf16[288,2048]{1,0:T(8,128)(2,1)}, u32[]{:S(2)}, u32[]{:S(2)}) collective-permute-start(bf16[288,2048]{1,0:T(8,128)(2,1)} %get-tuple-element.12), channel_id=1, source_target_pairs={{0,6},{1,14},{2,0},{3,8},{4,2},{5,10},{6,4},{7,12},{8,7},{9,15},{1... | collective-permute-start | bytes 3538952 | tf_op jit(solution)/shard_map/ppermute | solution.py:260
  78.3 1.0 fusion.16
  79.4 6.8 %collective-permute-start.3 = (bf16[16,2048]{1,0:T(8,128)(2,1)S(1)}, bf16[16,2048]{1,0:T(8,128)(2,1)S(1)}, u32[]{:S(2)}, u32[]{:S(2)}) collective-permute-start(bf16[16,2048]{1,0:T(8,128)(2,1)S(1)} %fusion.18), channel_id=1, source_target_pairs={{0,192},{64,0},{128,64},{192,128},{1,193},{65,1},{129,65},{193,129... | collective-permute-start | bytes 196616 | tf_op jit(solution)/shard_map/ppermute | solution.py:355
  86.4 43.6 %collective-permute-done.3 = bf16[16,2048]{1,0:T(8,128)(2,1)S(1)} collective-permute-done((bf16[16,2048]{1,0:T(8,128)(2,1)S(1)}, bf16[16,2048]{1,0:T(8,128)(2,1)S(1)}, u32[]{:S(2)}, u32[]{:S(2)}) %collective-permute-start.3) | collective-permute-done | bytes 65568 | tf_op jit(solution)/shard_map/ppermute | solution.py:355
  130.0 6.3 %collective-permute-start.2 = (bf16[16,2048]{1,0:T(8,128)(2,1)S(1)}, bf16[16,2048]{1,0:T(8,128)(2,1)S(1)}, u32[]{:S(2)}, u32[]{:S(2)}) collective-permute-start(bf16[16,2048]{1,0:T(8,128)(2,1)S(1)} %fusion.18), channel_id=1, source_target_pairs={{0,128},{64,192},{128,0},{192,64},{1,129},{65,193},{129,1},{193,65... | collective-permute-start | bytes 196616 | tf_op jit(solution)/shard_map/ppermute | solution.py:355
  136.4 2.3 %collective-permute-done.2 = bf16[16,2048]{1,0:T(8,128)(2,1)S(1)} collective-permute-done((bf16[16,2048]{1,0:T(8,128)(2,1)S(1)}, bf16[16,2048]{1,0:T(8,128)(2,1)S(1)}, u32[]{:S(2)}, u32[]{:S(2)}) %collective-permute-start.2) | collective-permute-done | bytes 65568 | tf_op jit(solution)/shard_map/ppermute | solution.py:355
  138.7 2.9 %collective-permute-start.1 = (bf16[16,2048]{1,0:T(8,128)(2,1)S(1)}, bf16[16,2048]{1,0:T(8,128)(2,1)S(1)}, u32[]{:S(2)}, u32[]{:S(2)}) collective-permute-start(bf16[16,2048]{1,0:T(8,128)(2,1)S(1)} %fusion.18), channel_id=1, source_target_pairs={{0,64},{64,128},{128,192},{192,0},{1,65},{65,129},{129,193},{193,1... | collective-permute-start | bytes 196616 | tf_op jit(solution)/shard_map/ppermute | solution.py:355
  141.6 0.2 broadcast_and_fusion
  141.8 0.2 and.129
  142.0 3.1 %collective-permute-done.1 = bf16[16,2048]{1,0:T(8,128)(2,1)S(1)} collective-permute-done((bf16[16,2048]{1,0:T(8,128)(2,1)S(1)}, bf16[16,2048]{1,0:T(8,128)(2,1)S(1)}, u32[]{:S(2)}, u32[]{:S(2)}) %collective-permute-start.1) | collective-permute-done | bytes 65568 | tf_op jit(solution)/shard_map/ppermute | solution.py:355
  145.1 1.4 fusion
  146.5 7.6 %all-to-all-start.4 = ((bf16[32,8,2048]{2,1,0:T(8,128)(2,1)}), bf16[32,8,2048]{2,1,0:T(8,128)(2,1)}, u32[]{:S(2)}, u32[]{:S(2)}) async-start(bf16[32,8,2048]{2,1,0:T(8,128)(2,1)} %fusion), calls=%async_computation.4 | async-start | bytes 2097152 | tf_op jit(solution)/shard_map/all_to_all | solution.py:379
  154.1 1.4 broadcast_select_fusion.refs_0_
  155.6 0.5 collective-permute-start.9
  156.2 0.4 collective-permute-start.11
  156.6 1.8 collective-permute-done.8.refs_4_
  158.4 1.0 copy-done.6
  159.4 0.7 collective-permute-done.9.refs_5_
  160.1 1.1 copy-done.7
  161.1 0.6 collective-permute-done.10.refs_6_
  161.8 1.0 copy-done.8
  162.8 0.8 collective-permute-done.11.refs_7_
  163.6 2.9 %all-to-all-done.4 = bf16[32,8,2048]{2,1,0:T(8,128)(2,1)} async-done(((bf16[32,8,2048]{2,1,0:T(8,128)(2,1)}), bf16[32,8,2048]{2,1,0:T(8,128)(2,1)}, u32[]{:S(2)}, u32[]{:S(2)}) %all-to-all-start.4) | async-done | bytes 1048608 | tf_op jit(solution)/shard_map/all_to_all | solution.py:379
  166.5 7.1 %expert.1 = bf16[256,2048]{1,0:T(8,128)(2,1)} custom-call(bf16[256,2048]{1,0:T(8,128)(2,1)} %bitcast.23.rows_ref, bf16[288,2048]{1,0:T(8,128)(2,1)} %copy-done.3, bf16[288,2048]{1,0:T(8,128)(2,1)} %collective-permute-done.5.refs_1_, bf16[288,2048]{1,0:T(8,128)(2,1)} %collective-permute-done.6.refs_2_, bf16[288,2048]{1,0:T(8,128)(2,1)} %collective-permute-done.7.refs_3_, ...), custom_call_target="tpu_custom_call" | custom-call | flops 2400000000 | bytes 11500000 | tf_op jit(solution)/shard_map/expert/pallas_call | solution.py:185
  173.6 5.4 %all-to-all-start.5 = ((bf16[32,8,2048]{2,1,0:T(8,128)(2,1)}), bf16[32,8,2048]{2,1,0:T(8,128)(2,1)S(1)}, u32[]{:S(2)}, u32[]{:S(2)}) async-start(bf16[32,8,2048]{2,1,0:T(8,128)(2,1)} %bitcast.64), calls=%async_computation.5 | async-start | bytes 2097152 | tf_op jit(solution)/shard_map/all_to_all | solution.py:383
  179.4 1.0 fusion.7
  180.4 0.8 convert_element_type.157
  181.2 1.0 select_convert_fusion
  182.4 13.6 %all-to-all-done.5 = bf16[32,8,2048]{2,1,0:T(8,128)(2,1)S(1)} async-done(((bf16[32,8,2048]{2,1,0:T(8,128)(2,1)}), bf16[32,8,2048]{2,1,0:T(8,128)(2,1)S(1)}, u32[]{:S(2)}, u32[]{:S(2)}) %all-to-all-start.5) | async-done | bytes 1048608 | tf_op jit(solution)/shard_map/all_to_all | solution.py:383
  196.0 1.2 fusion.4
  197.1 0.3 fusion.49
  197.5 2.1 %collective-permute-start.14 = (bf16[16,2048]{1,0:T(8,128)(2,1)S(1)}, bf16[16,2048]{1,0:T(8,128)(2,1)S(1)}, u32[]{:S(2)}, u32[]{:S(2)}) collective-permute-start(bf16[16,2048]{1,0:T(8,128)(2,1)S(1)} %get-tuple-element.20), channel_id=1, source_target_pairs={{0,64},{64,128},{128,192},{192,0},{1,65},{65,129},{129,193},{193,1... | collective-permute-start | bytes 196616 | tf_op jit(solution)/shard_map/ppermute | solution.py:395
  199.6 4.0 %collective-permute-start.13 = (bf16[16,2048]{1,0:T(8,128)(2,1)S(1)}, bf16[16,2048]{1,0:T(8,128)(2,1)S(1)}, u32[]{:S(2)}, u32[]{:S(2)}) collective-permute-start(bf16[16,2048]{1,0:T(8,128)(2,1)S(1)} %get-tuple-element.21), channel_id=1, source_target_pairs={{0,128},{64,192},{128,0},{192,64},{1,129},{65,193},{129,1},{193,65... | collective-permute-start | bytes 196616 | tf_op jit(solution)/shard_map/ppermute | solution.py:395
  203.6 4.0 %collective-permute-start.12 = (bf16[16,2048]{1,0:T(8,128)(2,1)S(1)}, bf16[16,2048]{1,0:T(8,128)(2,1)S(1)}, u32[]{:S(2)}, u32[]{:S(2)}) collective-permute-start(bf16[16,2048]{1,0:T(8,128)(2,1)S(1)} %get-tuple-element.19), channel_id=1, source_target_pairs={{0,192},{64,0},{128,64},{192,128},{1,193},{65,1},{129,65},{193,129... | collective-permute-start | bytes 196616 | tf_op jit(solution)/shard_map/ppermute | solution.py:395
  207.7 0.6 collective-permute-done.13
  208.2 1.4 collective-permute-done.12
  209.6 0.7 fusion.22
  (87 shorter events, 3.0 us)
Async XLA Ops:
  0.0 40.3 %copy-start = (bf16[2048,512]{1,0:T(8,128)(2,1)S(1)}, bf16[2048,512]{1,0:T(8,128)(2,1)}, u32[]{:S(2)}) copy-start(bf16[2048,512]{1,0:T(8,128)(2,1)} %param.16) | copy-start | bytes 6291460
  0.0 2.9 %copy-start.4 = (bf16[128,2048]{1,0:T(8,128)(2,1)S(1)}, bf16[128,2048]{1,0:T(8,128)(2,1)}, u32[]{:S(2)}) copy-start(bf16[128,2048]{1,0:T(8,128)(2,1)} %param.14) | copy-start | bytes 1572868
  0.0 3.0 %copy-start.10 = (f32[2048]{0:T(1024)S(1)}, f32[2048]{0:T(1024)}, u32[]{:S(2)}) copy-start(f32[2048]{0:T(1024)} %param.15) | copy-start | bytes 24580
  0.0 3.0 %copy-start.16 = (bf16[2048,64]{0,1:T(8,128)(2,1)S(1)}, bf16[2048,64]{0,1:T(8,128)(2,1)}, u32[]{:S(2)}) copy-start(bf16[2048,64]{0,1:T(8,128)(2,1)} %param.17) | copy-start | bytes 786436
  1.4 8.4 %copy-start.12 = (f32[128,8]{0,1:T(8,128)S(1)}, f32[128,8]{0,1:T(8,128)}, u32[]{:S(2)}) copy-start(f32[128,8]{0,1:T(8,128)} %param.24) | copy-start | bytes 12292
  1.4 8.5 %copy-start.13 = (s32[128,8]{0,1:T(8,128)S(1)}, s32[128,8]{0,1:T(8,128)}, u32[]{:S(2)}) copy-start(s32[128,8]{0,1:T(8,128)} %param.23) | copy-start | bytes 12292
  3.0 12.0 %copy-start.14 = (f32[128]{0:T(128)S(1)}, f32[128]{0:T(128)}, u32[]{:S(2)}) copy-start(f32[128]{0:T(128)} %param.20) | copy-start | bytes 1540
  4.0 10.8 %all-to-all-start = ((f32[8,16,128]{2,1,0:T(8,128)}), f32[8,16,128]{2,1,0:T(8,128)S(1)}, u32[]{:S(2)}, u32[]{:S(2)}) async-start(f32[8,16,128]{2,1,0:T(8,128)} %bitcast.10), calls=%async_computation | async-start | bytes 131072 | tf_op jit(solution)/shard_map/all_to_all | solution.py:308
  33.8 0.7 copy-start.5
  35.8 16.4 %all-to-all-start.2 = ((bf16[4,8,128,128]{3,2,1,0:T(8,128)(2,1)}), bf16[4,8,128,128]{3,2,1,0:T(8,128)(2,1)S(1)}, u32[]{:S(2)}, u32[]{:S(2)}) async-start(bf16[4,8,128,128]{3,2,1,0:T(8,128)(2,1)} %broadcast_in_dim.23), calls=%async_computation.2 | async-start | bytes 2097152 | tf_op jit(solution)/shard_map/all_to_all | solution.py:241
  40.3 12.3 %copy-start.15 = (f32[128]{0:T(128)S(1)}, f32[128]{0:T(128)}, u32[]{:S(2)}) copy-start(f32[128]{0:T(128)} %param.19) | copy-start | bytes 1540
  52.2 2.7 %collective-permute-start = (bf16[4,4,2,128,128]{4,3,2,1,0:T(8,128)(2,1)S(1)}, bf16[4,4,2,128,128]{4,3,2,1,0:T(8,128)(2,1)S(1)}, u32[]{:S(2)}, u32[]{:S(2)}) collective-permute-start(bf16[4,4,2,128,128]{4,3,2,1,0:T(8,128)(2,1)S(1)} %bitcast.60), channel_id=1, source_target_pairs={{0,8},{8,0},{1,9},{9,1},{2,10},{10,2},{3,11},{11,3},{4,12},{12,4},... | collective-permute-start | bytes 3145736 | tf_op jit(solution)/shard_map/ppermute | solution.py:336
  52.3 2.6 %copy-start.2 = (bf16[512,2048]{1,0:T(8,128)(2,1)S(1)}, bf16[512,2048]{1,0:T(8,128)(2,1)}, u32[]{:S(2)}) copy-start(bf16[512,2048]{1,0:T(8,128)(2,1)} %w_out_ref.1) | copy-start | bytes 6291460
  57.5 0.8 copy-start.1
  58.3 19.9 %all-to-all-start.3 = ((bf16[8,16,2048]{2,1,0:T(8,128)(2,1)}), bf16[8,16,2048]{2,1,0:T(8,128)(2,1)S(1)}, u32[]{:S(2)}, u32[]{:S(2)}) async-start(bf16[8,16,2048]{2,1,0:T(8,128)(2,1)} %bitcast.62), calls=%async_computation.3 | async-start | bytes 1048576 | tf_op jit(solution)/shard_map/all_to_all | solution.py:349
  63.3 14.0 %slice-start = ((bf16[8,144,128]{2,1,0:T(8,128)(2,1)}), bf16[8,16,128]{2,1,0:T(8,128)(2,1)S(1)}, s32[]{:S(2)}) async-start(bf16[8,144,128]{2,1,0:T(8,128)(2,1)} %copy-done.5), calls=%async_computation.6 | async-start | bytes 65536 | tf_op jit(solution)/shard_map/slice | solution.py:327
  67.9 11.4 %copy-start.11 = (f32[2048]{0:T(1024)S(1)}, f32[2048]{0:T(1024)}, u32[]{:S(2)}) copy-start(f32[2048]{0:T(1024)} %param.22) | copy-start | bytes 24580
  67.9 86.1 %collective-permute-start.4 = (bf16[288,2048]{1,0:T(8,128)(2,1)}, bf16[288,2048]{1,0:T(8,128)(2,1)}, u32[]{:S(2)}, u32[]{:S(2)}) collective-permute-start(bf16[288,2048]{1,0:T(8,128)(2,1)} %get-tuple-element.9), channel_id=1, source_target_pairs={{1,8},{3,10},{5,12},{7,14},{8,1},{10,3},{12,5},{14,7},{17,24},{19,... | collective-permute-start | bytes 3538952 | tf_op jit(solution)/shard_map/ppermute | solution.py:260
  69.8 85.7 %collective-permute-start.5 = (bf16[288,2048]{1,0:T(8,128)(2,1)}, bf16[288,2048]{1,0:T(8,128)(2,1)}, u32[]{:S(2)}, u32[]{:S(2)}) collective-permute-start(bf16[288,2048]{1,0:T(8,128)(2,1)} %get-tuple-element.10), channel_id=1, source_target_pairs={{0,2},{1,10},{2,4},{3,12},{4,6},{5,14},{6,0},{7,8},{8,3},{9,11},{1... | collective-permute-start | bytes 3538952 | tf_op jit(solution)/shard_map/ppermute | solution.py:260
  72.6 83.5 %collective-permute-start.6 = (bf16[288,2048]{1,0:T(8,128)(2,1)}, bf16[288,2048]{1,0:T(8,128)(2,1)}, u32[]{:S(2)}, u32[]{:S(2)}) collective-permute-start(bf16[288,2048]{1,0:T(8,128)(2,1)} %get-tuple-element.11), channel_id=1, source_target_pairs={{0,4},{1,12},{2,6},{3,14},{4,0},{5,8},{6,2},{7,10},{8,5},{9,13},{1... | collective-permute-start | bytes 3538952 | tf_op jit(solution)/shard_map/ppermute | solution.py:260
  74.7 81.5 %collective-permute-start.7 = (bf16[288,2048]{1,0:T(8,128)(2,1)}, bf16[288,2048]{1,0:T(8,128)(2,1)}, u32[]{:S(2)}, u32[]{:S(2)}) collective-permute-start(bf16[288,2048]{1,0:T(8,128)(2,1)} %get-tuple-element.12), channel_id=1, source_target_pairs={{0,6},{1,14},{2,0},{3,8},{4,2},{5,10},{6,4},{7,12},{8,7},{9,15},{1... | collective-permute-start | bytes 3538952 | tf_op jit(solution)/shard_map/ppermute | solution.py:260
  79.4 50.6 %collective-permute-start.3 = (bf16[16,2048]{1,0:T(8,128)(2,1)S(1)}, bf16[16,2048]{1,0:T(8,128)(2,1)S(1)}, u32[]{:S(2)}, u32[]{:S(2)}) collective-permute-start(bf16[16,2048]{1,0:T(8,128)(2,1)S(1)} %fusion.18), channel_id=1, source_target_pairs={{0,192},{64,0},{128,64},{192,128},{1,193},{65,1},{129,65},{193,129... | collective-permute-start | bytes 196616 | tf_op jit(solution)/shard_map/ppermute | solution.py:355
  130.0 8.7 %collective-permute-start.2 = (bf16[16,2048]{1,0:T(8,128)(2,1)S(1)}, bf16[16,2048]{1,0:T(8,128)(2,1)S(1)}, u32[]{:S(2)}, u32[]{:S(2)}) collective-permute-start(bf16[16,2048]{1,0:T(8,128)(2,1)S(1)} %fusion.18), channel_id=1, source_target_pairs={{0,128},{64,192},{128,0},{192,64},{1,129},{65,193},{129,1},{193,65... | collective-permute-start | bytes 196616 | tf_op jit(solution)/shard_map/ppermute | solution.py:355
  136.4 10.1 %copy-start.9 = (pred[4,16,32,2]{1,0,3,2:T(4,128)(4,1)}, pred[4,16,32,2]{1,0,3,2:T(4,128)(4,1)S(1)}, u32[]{:S(2)}) copy-start(pred[4,16,32,2]{1,0,3,2:T(4,128)(4,1)S(1)} %fusion.23) | copy-start | bytes 12292
  138.7 6.4 %collective-permute-start.1 = (bf16[16,2048]{1,0:T(8,128)(2,1)S(1)}, bf16[16,2048]{1,0:T(8,128)(2,1)S(1)}, u32[]{:S(2)}, u32[]{:S(2)}) collective-permute-start(bf16[16,2048]{1,0:T(8,128)(2,1)S(1)} %fusion.18), channel_id=1, source_target_pairs={{0,64},{64,128},{128,192},{192,0},{1,65},{65,129},{129,193},{193,1... | collective-permute-start | bytes 196616 | tf_op jit(solution)/shard_map/ppermute | solution.py:355
  146.5 20.1 %all-to-all-start.4 = ((bf16[32,8,2048]{2,1,0:T(8,128)(2,1)}), bf16[32,8,2048]{2,1,0:T(8,128)(2,1)}, u32[]{:S(2)}, u32[]{:S(2)}) async-start(bf16[32,8,2048]{2,1,0:T(8,128)(2,1)} %fusion), calls=%async_computation.4 | async-start | bytes 2097152 | tf_op jit(solution)/shard_map/all_to_all | solution.py:379
  155.5 11.1 %copy-start.3 = (bf16[288,2048]{1,0:T(8,128)(2,1)}, bf16[288,2048]{1,0:T(8,128)(2,1)S(1)}, u32[]{:S(2)}) copy-start(bf16[288,2048]{1,0:T(8,128)(2,1)S(1)} %broadcast_select_fusion.refs_0_) | copy-start | bytes 3538948
  155.5 2.9 %collective-permute-start.8 = (bf16[288,2048]{1,0:T(8,128)(2,1)S(1)}, bf16[288,2048]{1,0:T(8,128)(2,1)S(1)}, u32[]{:S(2)}, u32[]{:S(2)}) collective-permute-start(bf16[288,2048]{1,0:T(8,128)(2,1)S(1)} %broadcast_select_fusion.refs_0_), channel_id=1, source_target_pairs={{0,8},{8,0},{1,9},{9,1},{2,10},{10,2},{3,11},{11,3},{4,12},{12,4},... | collective-permute-start | bytes 3538952 | tf_op jit(solution)/shard_map/ppermute | solution.py:266
  155.6 4.5 %collective-permute-start.9 = (bf16[288,2048]{1,0:T(8,128)(2,1)}, bf16[288,2048]{1,0:T(8,128)(2,1)S(1)}, u32[]{:S(2)}, u32[]{:S(2)}) collective-permute-start(bf16[288,2048]{1,0:T(8,128)(2,1)} %collective-permute-done.5.refs_1_), channel_id=1, source_target_pairs={{0,8},{8,0},{1,9},{9,1},{2,10},{10,2},{3,11},{11,3},{4,12},{12,4},... | collective-permute-start | bytes 3538952 | tf_op jit(solution)/shard_map/ppermute | solution.py:266
  156.1 5.7 %collective-permute-start.10 = (bf16[288,2048]{1,0:T(8,128)(2,1)}, bf16[288,2048]{1,0:T(8,128)(2,1)S(1)}, u32[]{:S(2)}, u32[]{:S(2)}) collective-permute-start(bf16[288,2048]{1,0:T(8,128)(2,1)} %collective-permute-done.6.refs_2_), channel_id=1, source_target_pairs={{0,8},{8,0},{1,9},{9,1},{2,10},{10,2},{3,11},{11,3},{4,12},{12,4},... | collective-permute-start | bytes 3538952 | tf_op jit(solution)/shard_map/ppermute | solution.py:266
  156.2 7.4 %collective-permute-start.11 = (bf16[288,2048]{1,0:T(8,128)(2,1)}, bf16[288,2048]{1,0:T(8,128)(2,1)}, u32[]{:S(2)}, u32[]{:S(2)}) collective-permute-start(bf16[288,2048]{1,0:T(8,128)(2,1)} %collective-permute-done.7.refs_3_), channel_id=1, source_target_pairs={{0,8},{8,0},{1,9},{9,1},{2,10},{10,2},{3,11},{11,3},{4,12},{12,4},... | collective-permute-start | bytes 3538952 | tf_op jit(solution)/shard_map/ppermute | solution.py:266
  158.4 1.0 copy-start.6
  160.1 1.1 copy-start.7
  161.8 1.0 copy-start.8
  173.6 22.3 %all-to-all-start.5 = ((bf16[32,8,2048]{2,1,0:T(8,128)(2,1)}), bf16[32,8,2048]{2,1,0:T(8,128)(2,1)S(1)}, u32[]{:S(2)}, u32[]{:S(2)}) async-start(bf16[32,8,2048]{2,1,0:T(8,128)(2,1)} %bitcast.64), calls=%async_computation.5 | async-start | bytes 2097152 | tf_op jit(solution)/shard_map/all_to_all | solution.py:383
  197.5 10.2 %collective-permute-start.14 = (bf16[16,2048]{1,0:T(8,128)(2,1)S(1)}, bf16[16,2048]{1,0:T(8,128)(2,1)S(1)}, u32[]{:S(2)}, u32[]{:S(2)}) collective-permute-start(bf16[16,2048]{1,0:T(8,128)(2,1)S(1)} %get-tuple-element.20), channel_id=1, source_target_pairs={{0,64},{64,128},{128,192},{192,0},{1,65},{65,129},{129,193},{193,1... | collective-permute-start | bytes 196616 | tf_op jit(solution)/shard_map/ppermute | solution.py:395
  199.6 8.6 %collective-permute-start.13 = (bf16[16,2048]{1,0:T(8,128)(2,1)S(1)}, bf16[16,2048]{1,0:T(8,128)(2,1)S(1)}, u32[]{:S(2)}, u32[]{:S(2)}) collective-permute-start(bf16[16,2048]{1,0:T(8,128)(2,1)S(1)} %get-tuple-element.21), channel_id=1, source_target_pairs={{0,128},{64,192},{128,0},{192,64},{1,129},{65,193},{129,1},{193,65... | collective-permute-start | bytes 196616 | tf_op jit(solution)/shard_map/ppermute | solution.py:395
  203.6 5.9 %collective-permute-start.12 = (bf16[16,2048]{1,0:T(8,128)(2,1)S(1)}, bf16[16,2048]{1,0:T(8,128)(2,1)S(1)}, u32[]{:S(2)}, u32[]{:S(2)}) collective-permute-start(bf16[16,2048]{1,0:T(8,128)(2,1)S(1)} %get-tuple-element.19), channel_id=1, source_target_pairs={{0,192},{64,0},{128,64},{192,128},{1,193},{65,1},{129,65},{193,129... | collective-permute-start | bytes 196616 | tf_op jit(solution)/shard_map/ppermute | solution.py:395

commit v3 on v2

--- a/solution.py
+++ b/solution.py
@@ -21,7 +21,6 @@
 PLANE = ("y", "x", "zl")
 
 norm_eps = 1e-06
-ATTEND_VMEM = 16 * 1024 * 1024
 EXPERT_VMEM = 60 * 1024 * 1024
 BF = jnp.bfloat16
 F32 = jnp.float32
@@ -42,15 +41,19 @@
 
 
 def attention_kernel(
-    where_ref, q_ref, own_ref, other_ref, w_out_ref, out_ref, q_all, acc, peak, total, attended, out, sems
+    where_ref, q_ref, cos_ref, sin_ref, gain_ref, own_ref, other_ref, w_out_ref, out_ref, q_all, acc, peak, total, attended, w_out, sem
 ):
     rows = q_ref.shape[0]
     heads = q_ref.shape[1] // HEAD
-    pair_here = where_ref[0]
-    core = where_ref[1]
+    pair_here, core = where_ref[0], where_ref[1]
     factor = math.log2(math.e) / math.sqrt(HEAD)
+    fetch = pltpu.make_async_copy(w_out_ref, w_out, sem)
+    fetch.start()
     for h in range(heads):
-        q_all[h * rows : (h + 1) * rows, :] = q_ref[:, h * HEAD : (h + 1) * HEAD]
+        q = q_ref[:, h * HEAD : (h + 1) * HEAD]
+        q = q * lax.rsqrt(jnp.mean(q * q, axis=-1, keepdims=True) + norm_eps) * gain_ref[...]
+        q = q * cos_ref[...] + pltpu.roll(q, HEAD // 2, 1) * sin_ref[...]
+        q_all[h * rows : (h + 1) * rows, :] = q.astype(BF)
     acc[...] = jnp.zeros_like(acc)
     total[...] = jnp.zeros_like(total)
     peak[...] = jnp.full_like(peak, -1e30)
@@ -91,43 +94,117 @@
     for h in range(heads):
         part = slice(h * rows, (h + 1) * rows)
         attended[:, h * HEAD : (h + 1) * HEAD] = (acc[part, :] / summed[part]).astype(BF)
-    copies = []
+    fetch.wait()
     for i in range(D // SPAN):
-        out[i] = jnp.dot(
-            attended[...], w_out_ref[:, i * SPAN : (i + 1) * SPAN], preferred_element_type=F32
+        part = slice(i * SPAN, (i + 1) * SPAN)
+        out_ref[:, part] = jnp.dot(
+            attended[...], w_out[:, part], preferred_element_type=F32
         ).astype(BF)
-        copies.append(
-            pltpu.make_async_copy(out.at[i], out_ref.at[:, pl.ds(i * SPAN, SPAN)], sems.at[i])
-        )
-        copies[i].start()
-    for copy in copies:
-        copy.wait()
-
-
-def attention(where, query, own, other, w_out):
+
+
+def attention(where, query, cosine, sine, gain, own, other, w_out):
     rows = query.shape[0]
     heads = query.shape[1] // HEAD
     vmem = pl.BlockSpec(memory_space=pltpu.VMEM)
     return pl.pallas_call(
         attention_kernel,
         out_shape=jax.ShapeDtypeStruct((rows, D), BF),
-        in_specs=[pl.BlockSpec(memory_space=pltpu.SMEM), vmem, vmem, vmem, vmem],
-        out_specs=pl.BlockSpec(memory_space=pltpu.HBM),
+        in_specs=[pl.BlockSpec(memory_space=pltpu.SMEM)]
+        + [vmem] * 6
+        + [pl.BlockSpec(memory_space=pl.ANY)],
+        out_specs=vmem,
         scratch_shapes=[
             pltpu.VMEM((heads * rows, HEAD), BF),
             pltpu.VMEM((heads * rows, HEAD), F32),
             pltpu.VMEM((heads * rows, 1), F32),
             pltpu.VMEM((heads * rows, HEAD), F32),
             pltpu.VMEM((rows, heads * HEAD), BF),
-            pltpu.VMEM((D // SPAN, rows, SPAN), BF),
-            pltpu.SemaphoreType.DMA((D // SPAN,)),
+            pltpu.VMEM(w_out.shape, BF),
+            pltpu.SemaphoreType.DMA,
         ],
-        compiler_params=pltpu.CompilerParams(vmem_limit_bytes=ATTEND_VMEM),
         cost_estimate=pl.CostEstimate(
             flops=1400000000, bytes_accessed=5000000, transcendentals=2000000
         ),
         name="attend",
-    )(where, query, own, other, w_out)
+    )(where, query, cosine, sine, gain, own, other, w_out)
+
+
+def carry_kernel(blocks_ref, tokens_ref, gain_ref, carried_ref, normed_ref):
+    mixed = jnp.sum(blocks_ref[...].astype(F32), axis=0)
+    carried = (tokens_ref[...].astype(F32) + mixed).astype(BF)
+    carried_ref[...] = carried
+    normed_ref[...] = rms_norm(carried, gain_ref[...]).astype(BF)
+
+
+def carry(blocks, tokens, gain):
+    vmem = pl.BlockSpec(memory_space=pltpu.VMEM)
+    shape = jax.ShapeDtypeStruct(tokens.shape, BF)
+    return pl.pallas_call(
+        carry_kernel,
+        out_shape=[shape, shape],
+        in_specs=[vmem] * 3,
+        out_specs=[vmem] * 2,
+        cost_estimate=pl.CostEstimate(flops=600000, bytes_accessed=800000, transcendentals=16),
+        name="carry",
+    )(blocks, tokens, gain.reshape(1, -1))
+
+
+def route_kernel(where_ref, ring_ref, *refs):
+    rows, (out_ref, high_ref, low_ref) = refs[:ZH], refs[ZH:]
+    zh, zl = where_ref[0], where_ref[1]
+    share = rows[0].shape[0]
+    tails = jnp.concatenate(
+        [ring_ref[(zh + ZH - k) % ZH * ZL + zl, HEAD:, :] for k in range(ZH)], axis=0
+    ).astype(F32)
+    shape = (ZH * share, Y * X * ZL * ZH * CAP)
+    row = lax.broadcasted_iota(jnp.int32, shape, 0)
+    column = lax.broadcasted_iota(jnp.int32, shape, 1)
+    slot, source, chip = column % CAP, column // CAP % ZH, column // (CAP * ZH)
+    expert_of = (
+        zh * (Y * X * ZL) + chip // (X * ZL) * (X * ZL) + chip % ZL * X + chip // ZL % X
+    ).astype(F32)
+    hits = jnp.zeros(shape, F32)
+    gate = jnp.zeros(shape, F32)
+    for k in range(TOPK):
+        same = tails[:, k : k + 1] == expert_of
+        weight = tails[:, TOPK + k : TOPK + k + 1] + tails[:, 2 * TOPK + k : 2 * TOPK + k + 1]
+        hits = jnp.where(same, 1.0, hits)
+        gate = jnp.where(same, weight, gate)
+    one = lax.broadcasted_iota(jnp.int32, (ZH * share, ZH * share), 0)
+    two = lax.broadcasted_iota(jnp.int32, (ZH * share, ZH * share), 1)
+    before = jnp.where(jnp.logical_and(two < one, two // share == one // share), 1.0, 0.0)
+    earlier = jnp.dot(before.astype(BF), hits.astype(BF), preferred_element_type=F32)
+    placed = jnp.logical_and(source == row // share, earlier == slot.astype(F32))
+    table = jnp.where(placed, hits, 0.0)
+    mixing = table * gate
+    high = mixing.astype(BF)
+    high_ref[...] = high
+    low_ref[...] = (mixing - high.astype(F32)).astype(BF)
+    whole = jnp.concatenate([ref[...] for ref in rows], axis=0)
+    turned_table = table.T.astype(BF)
+    for i in range(D // SPAN):
+        part = slice(i * SPAN, (i + 1) * SPAN)
+        out_ref[:, part] = jnp.dot(
+            turned_table, whole[:, part], preferred_element_type=F32
+        ).astype(BF)
+
+
+def route(where, ring, rows):
+    vmem = pl.BlockSpec(memory_space=pltpu.VMEM)
+    slots = Y * X * ZL * ZH * CAP
+    count = sum(r.shape[0] for r in rows)
+    return pl.pallas_call(
+        route_kernel,
+        out_shape=[
+            jax.ShapeDtypeStruct((slots, D), BF),
+            jax.ShapeDtypeStruct((count, slots), BF),
+            jax.ShapeDtypeStruct((count, slots), BF),
+        ],
+        in_specs=[pl.BlockSpec(memory_space=pltpu.SMEM)] + [vmem] * (1 + len(rows)),
+        out_specs=[vmem] * 3,
+        cost_estimate=pl.CostEstimate(flops=70000000, bytes_accessed=1700000, transcendentals=0),
+        name="route",
+    )(where, ring, *rows)
 
 
 def expert_kernel(rows_ref, *refs):
@@ -247,20 +324,23 @@
 
 def weight_pieces(w_gate, w_up, w_down, c, x, zl):
     packed = pack(x, jnp.swapaxes(w_gate, 1, 2), jnp.swapaxes(w_up, 1, 2), w_down)
+
+    def shifted(k, straight):
+        return [
+            ((cs * X + xs) * ZL + zs, (zs * X + (xs + k) % X) * ZL + cs)
+            for cs in range(C)
+            for xs in range(X)
+            for zs in range(ZL)
+            if (cs == zs) == straight
+        ]
+
     own = []
     for k in range(X):
-        pairs = []
-        for cs in range(C):
-            for xs in range(X):
-                for zs in range(ZL):
-                    source = (cs * X + xs) * ZL + zs
-                    target = (zs * X + (xs + k) % X) * ZL + cs
-                    if source != target:
-                        pairs.append((source, target))
-        moved = lax.ppermute(packed[k], ("c", "x", "zl"), pairs)
-        if k == 0:
-            moved = jnp.where(zl == c, packed[k], moved)
-        own.append(moved)
+        straight = packed[0]
+        if k > 0:
+            straight = lax.ppermute(packed[k], ("c", "x", "zl"), shifted(k, True))
+        crossed = lax.ppermute(packed[k], ("c", "x", "zl"), shifted(k, False))
+        own.append(jnp.where(zl == c, straight, crossed))
     other = []
     for k in range(X):
         other.append(lax.ppermute(own[k], "c", [(0, 1), (1, 0)]))
@@ -324,58 +404,25 @@
         [ids.astype(BF), gates_high, gates_low, jnp.zeros((share, HEAD - 3 * TOPK), BF)], axis=1
     )
     ring = spread(jnp.concatenate([piece, tail], axis=0), ("zh", "zl"), ZH * ZL)
-    tails = ring[:, HEAD:].reshape(ZH, ZL, share, HEAD)
-    tails = lax.dynamic_index_in_dim(tails, zl, 1, keepdims=False)
-    routes = jnp.concatenate(
-        [lax.dynamic_index_in_dim(tails, (zh - k) % ZH, 0, keepdims=False) for k in range(ZH)],
-        axis=0,
-    ).astype(F32)
-    ring = ring[:, :HEAD]
-    own = spread(ring, "y", Y)
+    own = spread(ring[:, :HEAD], "y", Y)
     own = own.reshape(Y, ZH, ZL, HEAD, HEAD)
     other = lax.ppermute(own, "c", [(0, 1), (1, 0)])
 
-    query = jnp.dot(normed, w_query, preferred_element_type=F32).reshape(local_rows, -1, HEAD)
-    query = rms_norm(query, query_gain)
-    lead, trail = query[..., :half], query[..., half:]
-    cos_q, sin_q = cosine[:, None, :], sine[:, None, :]
-    query = jnp.concatenate(
-        [lead * cos_q - trail * sin_q, trail * cos_q + lead * sin_q], axis=-1
-    ).astype(BF)
-    query = query.reshape(local_rows, -1)
-
+    query = jnp.dot(normed, w_query, preferred_element_type=F32)
     where = jnp.stack([zh * Y + y, c]).astype(jnp.int32)
-    partial = attention(where, query, own, other, w_out)
+    place = jnp.stack([zh, zl]).astype(jnp.int32)
+    cosines = jnp.concatenate([cosine, cosine], axis=1)
+    sines = jnp.concatenate([-sine, sine], axis=1)
+    partial = attention(
+        where, query, cosines, sines, query_gain.reshape(1, -1), own, other, w_out
+    )
+    partial, tokens = lax.optimization_barrier((partial, tokens))
     blocks = lax.all_to_all(partial.reshape(X * ZL, share, D), NARROW, 0, 0, tiled=True)
-    mixed = jnp.sum(blocks.astype(F32), axis=0)
     own_tokens = lax.dynamic_slice_in_dim(tokens, narrow * share, share, 0)
-    carried = (own_tokens.astype(F32) + mixed).astype(BF)
-    moe_in = rms_norm(carried, moe_gain).astype(BF)
+    carried, moe_in = carry(blocks, own_tokens, moe_gain)
 
     rows = [moe_in] + [lax.ppermute(moe_in, "zh", turned(ZH, k)) for k in range(1, ZH)]
-    rows = jnp.concatenate(rows, axis=0)
-    ids_f = routes[:, :TOPK]
-    gates_all = routes[:, TOPK : 2 * TOPK] + routes[:, 2 * TOPK : 3 * TOPK]
-    chips = jnp.arange(Y * X * ZL, dtype=jnp.int32)
-    expert_of = (
-        zh * (Y * X * ZL) + chips // (X * ZL) * (X * ZL) + chips % ZL * X + chips // ZL % X
-    ).astype(F32)
-    hits = ids_f[:, :, None] == expert_of[None, None, :]
-    named = jnp.any(hits, axis=1).reshape(ZH, share, -1)
-    gate_of = jnp.sum(jnp.where(hits, gates_all[:, :, None], 0.0), axis=1).reshape(ZH, share, -1)
-    named_f = named.astype(F32)
-    earlier = jnp.cumsum(named_f, axis=1) - named_f
-    slot = jnp.arange(CAP, dtype=F32)
-    chosen = named[..., None] & (earlier[..., None] == slot)
-    same = jnp.eye(ZH, dtype=jnp.bool_)
-    table = chosen[:, :, :, None, :] & same[:, None, None, :, None]
-    table = table.reshape(ZH * share, -1)
-    shared_gate = jnp.broadcast_to(
-        gate_of[:, :, :, None, None], (ZH, share, Y * X * ZL, ZH, CAP)
-    ).reshape(ZH * share, -1)
-    outgoing = lax.dot_general(
-        table.astype(BF), rows, (((0,), (0,)), ((), ())), preferred_element_type=F32
-    ).astype(BF)
+    outgoing, mixing_high, mixing_low = route(place, ring, rows)
     arrived = lax.all_to_all(
         outgoing.reshape(Y * X * ZL, ZH * CAP, D), PLANE, 0, 0, tiled=True
     ).reshape(-1, D)
@@ -383,9 +430,6 @@
     returned = lax.all_to_all(
         answers.reshape(Y * X * ZL, ZH * CAP, D), PLANE, 0, 0, tiled=True
     ).reshape(-1, D)
-    mixing = jnp.where(table, shared_gate, 0.0)
-    mixing_high = mixing.astype(BF)
-    mixing_low = (mixing - mixing_high.astype(F32)).astype(BF)
     sums = jnp.dot(mixing_high, returned, preferred_element_type=F32) + jnp.dot(
         mixing_low, returned, preferred_element_type=F32
     )

time: 213 us -> 208 us (0.977)
  waiting for transfers between devices: 85.9 us -> 47.1 us
  blocking collectives: 18.3 us -> 55.9 us
  Pallas kernels: 14.3 us -> 21 us
  local copies, waits for them, and re-layouts: 9.54 us -> 4.66 us
  starting transfers between devices: 64.9 us -> 61.3 us
  matrix products: 6.98 us -> 3.68 us
  other arithmetic: 9.78 us -> 12.2 us
    ppermute x3, waiting for transfers between devices: 48.9 us -> 14.8 us  [on_device(): lax.ppermute(moe_in, 'zh', turned(ZH, k))]
    all_to_all x2 -> x0, waiting for transfers between devices: 22.1 us -> none  [the longest x1 13.6 us: on_device(): lax.all_to_all(answers.reshape(Y * X * ZL, ZH * CAP, D), PLANE, 0, 0, til...]
    all_to_all x0 -> x1, blocking collectives: none -> 21.2 us  [on_device(): lax.all_to_all(answers.reshape(Y * X * ZL, ZH * CAP, D), PLANE, 0, 0, til...]
    all_to_all x1 -> x2, blocking collectives: 18.3 us -> 34.7 us  [spread(): return lax.all_to_all(copies, axes, 0, 0, tiled=True)]
    ppermute x4, starting transfers between devices: 1.09 us -> 13.3 us  [weight_pieces(): other.append(lax.ppermute(own[k], 'c', [(0, 1), (1, 0)]))]
    ppermute x3, starting transfers between devices: 16.1 us -> 5.4 us  [on_device(): lax.ppermute(moe_in, 'zh', turned(ZH, k))]
    all_to_all x1, waiting for transfers between devices: 0.01 us -> 10.6 us  [on_device(): lax.all_to_all(partial.reshape(X * ZL, share, D), NARROW, 0, 0, tiled=True)]
    ppermute x4 -> x7, starting transfers between devices: 9.41 us -> 19.5 us  [the longest x4 14.3 us: weight_pieces(): crossed = lax.ppermute(packed[k], ('c', 'x', 'zl'), shifted(k, False))]
  transfers between devices with their start and end apart: 20 -> 21, of which waited for: 14 -> 9; matrix products, arithmetic and copies ran while one was open for 7% -> 5% of each run, Pallas kernels for 2% -> 7%
where the time goes in v3:
time: 208 us; the launch traced here: 206 us
  starting transfers between devices  61.3 us (29%)
  blocking collectives  55.9 us (27%)
  waiting for transfers between devices  47.1 us (23%)
  Pallas kernels  21 us (10%)
  other arithmetic  12.2 us (6%)
  local copies, waits for them, and re-layouts  4.66 us (2%)
  matrix products  3.68 us (2%)
    all_to_all x2, blocking collectives, spread(): return lax.all_to_all(copies, axes, 0, 0, tiled=True)  34.7 us
    all_to_all x1, blocking collectives, on_device(): lax.all_to_all(answers.reshape(Y * X * ZL, ZH * CAP, D), PLANE, 0, 0, til...  21.2 us
    ppermute x3, waiting for transfers between devices, on_device(): lax.ppermute(moe_in, 'zh', turned(ZH, k))  14.8 us
    ppermute x4, starting transfers between devices, weight_pieces(): crossed = lax.ppermute(packed[k], ('c', 'x', 'zl'), shifted(k, False))  14.3 us
    ppermute x4, starting transfers between devices, weight_pieces(): other.append(lax.ppermute(own[k], 'c', [(0, 1), (1, 0)]))  13.3 us
    all_to_all x1, waiting for transfers between devices, on_device(): lax.all_to_all(outgoing.reshape(Y * X * ZL, ZH * CAP, D), PLANE, 0, 0, ti...  10.7 us
    all_to_all x1, waiting for transfers between devices, on_device(): lax.all_to_all(partial.reshape(X * ZL, share, D), NARROW, 0, 0, tiled=True)  10.6 us
    pallas_call x1, Pallas kernels, expert(): pl.pallas_call(expert_kernel, out_shape=jax.ShapeDtypeStruct((count, D),...  7.13 us
  transfers between devices with their start and end apart: 21, of which 9 were waited for; matrix products, arithmetic and copies ran while one was open for 5% of the time, Pallas kernels for 7%

profile of v3, /device:TPU:32, one launch (start us, length us, event | category | flops | bytes accessed | tf_op | source)
XLA Modules:
  0.0 206.2 jit_solution(10173609773091017486)
XLA Ops:
  0.0 1.4 fusion
  1.4 1.5 fusion.20
  3.0 0.4 fusion.22
  3.4 0.6 pad_maximum_fusion.2
  4.0 5.8 %all-to-all-start = ((f32[8,16,128]{2,1,0:T(8,128)}), f32[8,16,128]{2,1,0:T(8,128)S(1)}, u32[]{:S(2)}, u32[]{:S(2)}) async-start(f32[8,16,128]{2,1,0:T(8,128)} %bitcast.11), calls=%async_computation | async-start | bytes 131072 | tf_op jit(solution)/shard_map/all_to_all | solution.py:388
  9.8 0.1 fusion.26
  10.2 4.6 %all-to-all-done = f32[8,16,128]{2,1,0:T(8,128)S(1)} async-done(((f32[8,16,128]{2,1,0:T(8,128)}), f32[8,16,128]{2,1,0:T(8,128)S(1)}, u32[]{:S(2)}, u32[]{:S(2)}) %all-to-all-start) | async-done | bytes 65568 | tf_op jit(solution)/shard_map/all_to_all | solution.py:388
  14.9 0.1 copy.32
  15.0 0.1 multiply_multiply_fusion
  15.1 0.2 fusion.15
  15.5 18.3 %all_to_all.30.ring_ref = bf16[8,144,128]{2,1,0:T(8,128)(2,1)S(1)} all-to-all(bf16[8,144,128]{2,1,0:T(8,128)(2,1)S(1)} %broadcast_in_dim.7), channel_id=1, replica_groups=mesh['zh'=4,'y'=4,'c'=2,'x'=4,'zl'=2] {'zh','zl'}, dimensions={0} | all-to-all | bytes 589824 | tf_op jit(solution)/shard_map/all_to_all | solution.py:318
  33.8 0.7 copy-done.4
  34.5 0.2 broadcast_in_dim.8
  34.8 16.3 %all_to_all.31 = bf16[4,8,128,128]{3,2,1,0:T(8,128)(2,1)} all-to-all(bf16[4,8,128,128]{3,2,1,0:T(8,128)(2,1)S(1)} %broadcast_in_dim.8), channel_id=1, replica_groups=mesh['zh'=4,'y'=4,'c'=2,'x'=4,'zl'=2] {'y'}, dimensions={0} | all-to-all | bytes 2097152 | tf_op jit(solution)/shard_map/all_to_all | solution.py:318
  51.1 4.6 %pack.1 = (bf16[288,2048]{1,0:T(8,128)(2,1)}, bf16[288,2048]{1,0:T(8,128)(2,1)}, bf16[288,2048]{1,0:T(8,128)(2,1)}, bf16[288,2048]{1,0:T(8,128)(2,1)}) custom-call(s32[1]{0:T(128)} %bitcast.21.x_ref, bf16[4,96,2048]{2,1,0:T(8,128)(2,1)} %bitcast.46, bf16[4,96,2048]{2,1,0:T(8,128)(2,1)} %bitcast.47, bf16[4,96,2048]{2,1,0:T(8,128)(2,1)} %down_ref.1), custom_call_target="tpu_custom_call" | custom-call | bytes 9500000 | tf_op jit(solution)/shard_map/pack/pallas_call | solution.py:305
  55.7 1.7 collective-permute-start.5
  57.4 3.6 %collective-permute-start.6 = (bf16[288,2048]{1,0:T(8,128)(2,1)}, bf16[288,2048]{1,0:T(8,128)(2,1)}, u32[]{:S(2)}, u32[]{:S(2)}) collective-permute-start(bf16[288,2048]{1,0:T(8,128)(2,1)} %get-tuple-element.23), channel_id=1, source_target_pairs={{1,10},{3,12},{5,14},{7,8},{8,3},{10,5},{12,7},{14,1},{17,26},{19,... | collective-permute-start | bytes 3538952 | tf_op jit(solution)/shard_map/ppermute | solution.py:342
  61.0 1.9 collective-permute-start.4
  63.0 0.3 fusion.18
  63.3 1.2 fusion.24.q_ref
  64.5 0.7 pad_maximum_fusion
  65.2 0.6 pad_add_fusion.where_ref
  65.9 4.6 %attend.1 = bf16[128,2048]{1,0:T(8,128)(2,1)} custom-call(s32[2]{0:T(128)} %pad_add_fusion.where_ref, f32[128,512]{1,0:T(8,128)} %fusion.24.q_ref, f32[128,128]{1,0:T(8,128)} %get-tuple-element.43.cos_ref, f32[128,128]{1,0:T(8,128)} %get-tuple-element.44.sin_ref, f32[1,128]{1,0:T(1,128)} %bitcast.54, bf16[4,4,2,128,128]{4,3,2,1,0:T(8,128)(2,1)} %bitcast.14.own_ref, ...), custom_call_target="tpu_custom_call" | custom-call | flops 1400000000 | bytes 5000000 | tf_op jit(solution)/shard_map/attend/pallas_call | solution.py:109
  70.5 5.4 %all-to-all-start.3 = ((bf16[8,16,2048]{2,1,0:T(8,128)(2,1)}), bf16[8,16,2048]{2,1,0:T(8,128)(2,1)S(1)}, u32[]{:S(2)}, u32[]{:S(2)}) async-start(bf16[8,16,2048]{2,1,0:T(8,128)(2,1)} %bitcast.50), calls=%async_computation.3 | async-start | bytes 1048576 | tf_op jit(solution)/shard_map/all_to_all | solution.py:420
  75.9 1.7 collective-permute-start.7
  77.5 4.6 %collective-permute-start.8 = (bf16[288,2048]{1,0:T(8,128)(2,1)}, bf16[288,2048]{1,0:T(8,128)(2,1)}, u32[]{:S(2)}, u32[]{:S(2)}) collective-permute-start(bf16[288,2048]{1,0:T(8,128)(2,1)} %get-tuple-element.24), channel_id=1, source_target_pairs={{1,12},{3,14},{5,8},{7,10},{8,5},{10,7},{12,1},{14,3},{17,28},{19,... | collective-permute-start | bytes 3538952 | tf_op jit(solution)/shard_map/ppermute | solution.py:342
  82.1 0.6 constant_dynamic-slice_fusion.tokens_ref
  82.7 10.6 %all-to-all-done.3.blocks_ref = bf16[8,16,2048]{2,1,0:T(8,128)(2,1)S(1)} async-done(((bf16[8,16,2048]{2,1,0:T(8,128)(2,1)}), bf16[8,16,2048]{2,1,0:T(8,128)(2,1)S(1)}, u32[]{:S(2)}, u32[]{:S(2)}) %all-to-all-start.3) | async-done | bytes 524320 | tf_op jit(solution)/shard_map/all_to_all | solution.py:420
  93.3 0.8 copy-done.6
  94.1 1.9 carry.1
  96.0 0.3 collective-permute-start.1
  96.4 0.6 pad_add_fusion.1.where_ref
  97.0 1.8 collective-permute-start.9
  98.8 4.1 %collective-permute-start.10 = (bf16[288,2048]{1,0:T(8,128)(2,1)}, bf16[288,2048]{1,0:T(8,128)(2,1)}, u32[]{:S(2)}, u32[]{:S(2)}) collective-permute-start(bf16[288,2048]{1,0:T(8,128)(2,1)} %get-tuple-element.25), channel_id=1, source_target_pairs={{1,14},{3,8},{5,10},{7,12},{8,7},{10,1},{12,3},{14,5},{17,30},{19,... | collective-permute-start | bytes 3538952 | tf_op jit(solution)/shard_map/ppermute | solution.py:342
  103.0 2.6 %collective-permute-start.2 = (bf16[16,2048]{1,0:T(8,128)(2,1)}, bf16[16,2048]{1,0:T(8,128)(2,1)S(1)}, u32[]{:S(2)}, u32[]{:S(2)}) collective-permute-start(bf16[16,2048]{1,0:T(8,128)(2,1)} %get-tuple-element.19.refs_0_), channel_id=1, source_target_pairs={{0,128},{64,192},{128,0},{192,64},{1,129},{65,193},{129,1},{193,65... | collective-permute-start | bytes 196616 | tf_op jit(solution)/shard_map/ppermute | solution.py:424
  105.6 1.4 broadcast_select_fusion.3.refs_0_
  107.1 14.5 %collective-permute-done.2.refs_2_ = bf16[16,2048]{1,0:T(8,128)(2,1)S(1)} collective-permute-done((bf16[16,2048]{1,0:T(8,128)(2,1)}, bf16[16,2048]{1,0:T(8,128)(2,1)S(1)}, u32[]{:S(2)}, u32[]{:S(2)}) %collective-permute-start.2) | collective-permute-done | bytes 65568 | tf_op jit(solution)/shard_map/ppermute | solution.py:424
  121.5 2.4 %collective-permute-start.3 = (bf16[16,2048]{1,0:T(8,128)(2,1)S(1)}, bf16[16,2048]{1,0:T(8,128)(2,1)S(1)}, u32[]{:S(2)}, u32[]{:S(2)}) collective-permute-start(bf16[16,2048]{1,0:T(8,128)(2,1)S(1)} %copy-done.10), channel_id=1, source_target_pairs={{0,192},{64,0},{128,64},{192,128},{1,193},{65,1},{129,65},{193,129... | collective-permute-start | bytes 196616 | tf_op jit(solution)/shard_map/ppermute | solution.py:424
  124.0 2.4 %broadcast_select_fusion.2.refs_1_ = bf16[288,2048]{1,0:T(8,128)(2,1)} fusion(bf16[288,2048]{1,0:T(8,128)(2,1)} %collective-permute-done.5, bf16[288,2048]{1,0:T(8,128)(2,1)} %collective-permute-done.6, pred[]{:T(512)S(6)} %eq.10), kind=kLoop, calls=%fused_computation.5 | loop fusion | flops 589824 | bytes 3538945 | tf_op jit(solution)/shard_map/jit(_where)/select_n | solution.py:343
  126.3 0.3 collective-permute-done.3.refs_3_
  126.7 12.1 %collective-permute-start.11 = (bf16[288,2048]{1,0:T(8,128)(2,1)S(1)}, bf16[288,2048]{1,0:T(8,128)(2,1)}, u32[]{:S(2)}, u32[]{:S(2)}) collective-permute-start(bf16[288,2048]{1,0:T(8,128)(2,1)S(1)} %broadcast_select_fusion.3.refs_0_), channel_id=1, source_target_pairs={{0,8},{8,0},{1,9},{9,1},{2,10},{10,2},{3,11},{11,3},{4,12},{12,4},... | collective-permute-start | bytes 3538952 | tf_op jit(solution)/shard_map/ppermute | solution.py:346
  138.8 2.8 %route.1 = (bf16[256,2048]{1,0:T(8,128)(2,1)}, bf16[64,256]{1,0:T(8,128)(2,1)}, bf16[64,256]{1,0:T(8,128)(2,1)}) custom-call(s32[2]{0:T(128)} %pad_add_fusion.1.where_ref, bf16[8,144,128]{2,1,0:T(8,128)(2,1)} %copy-done.4, bf16[16,2048]{1,0:T(8,128)(2,1)} %get-tuple-element.19.refs_0_, bf16[16,2048]{1,0:T(8,128)(2,1)} %copy-done.11, ...), custom_call_target="tpu_custom_call" | custom-call | flops 70000000 | bytes 1700000 | tf_op jit(solution)/shard_map/route/pallas_call | solution.py:196
  141.6 5.3 %all-to-all-start.4 = ((bf16[32,8,2048]{2,1,0:T(8,128)(2,1)}), bf16[32,8,2048]{2,1,0:T(8,128)(2,1)}, u32[]{:S(2)}, u32[]{:S(2)}) async-start(bf16[32,8,2048]{2,1,0:T(8,128)(2,1)} %bitcast.48), calls=%async_computation.4 | async-start | bytes 2097152 | tf_op jit(solution)/shard_map/all_to_all | solution.py:426
  146.9 0.1 collective-permute-start.12
  147.0 1.4 broadcast_select_fusion.1.refs_2_
  148.4 0.6 collective-permute-start.13
  149.0 1.4 broadcast_select_fusion.refs_3_
  150.4 0.6 collective-permute-start.14
  151.0 0.7 collective-permute-done.13.refs_6_
  151.7 0.3 copy-done.7
  152.0 1.1 copy-done.8
  153.1 0.6 collective-permute-done.14.refs_7_
  153.7 10.7 %all-to-all-done.4 = bf16[32,8,2048]{2,1,0:T(8,128)(2,1)} async-done(((bf16[32,8,2048]{2,1,0:T(8,128)(2,1)}), bf16[32,8,2048]{2,1,0:T(8,128)(2,1)}, u32[]{:S(2)}, u32[]{:S(2)}) %all-to-all-start.4) | async-done | bytes 1048608 | tf_op jit(solution)/shard_map/all_to_all | solution.py:426
  164.3 7.1 %expert.1 = bf16[256,2048]{1,0:T(8,128)(2,1)} custom-call(bf16[256,2048]{1,0:T(8,128)(2,1)} %bitcast.20.rows_ref, bf16[288,2048]{1,0:T(8,128)(2,1)} %copy-done.1, bf16[288,2048]{1,0:T(8,128)(2,1)} %broadcast_select_fusion.2.refs_1_, bf16[288,2048]{1,0:T(8,128)(2,1)} %copy-done.2, bf16[288,2048]{1,0:T(8,128)(2,1)} %copy-done.3, ...), custom_call_target="tpu_custom_call" | custom-call | flops 2400000000 | bytes 11500000 | tf_op jit(solution)/shard_map/expert/pallas_call | solution.py:262
  171.5 21.2 %all_to_all.32 = bf16[32,8,2048]{2,1,0:T(8,128)(2,1)S(1)} all-to-all(bf16[32,8,2048]{2,1,0:T(8,128)(2,1)} %bitcast.45), channel_id=1, replica_groups=mesh['zh'=4,'y'=4,'c'=2,'x'=4,'zl'=2] {'y','x','zl'}, dimensions={0} | all-to-all | bytes 2097152 | tf_op jit(solution)/shard_map/all_to_all | solution.py:430
  192.7 0.3 fusion.3
  193.0 0.5 copy-done.14
  193.4 0.3 fusion.28
  193.8 2.3 %collective-permute-start.17 = (bf16[16,2048]{1,0:T(8,128)(2,1)S(1)}, bf16[16,2048]{1,0:T(8,128)(2,1)S(1)}, u32[]{:S(2)}, u32[]{:S(2)}) collective-permute-start(bf16[16,2048]{1,0:T(8,128)(2,1)S(1)} %get-tuple-element.30), channel_id=1, source_target_pairs={{0,64},{64,128},{128,192},{192,0},{1,65},{65,129},{129,193},{193,1... | collective-permute-start | bytes 196616 | tf_op jit(solution)/shard_map/ppermute | solution.py:439
  196.1 3.5 %collective-permute-start.16 = (bf16[16,2048]{1,0:T(8,128)(2,1)S(1)}, bf16[16,2048]{1,0:T(8,128)(2,1)S(1)}, u32[]{:S(2)}, u32[]{:S(2)}) collective-permute-start(bf16[16,2048]{1,0:T(8,128)(2,1)S(1)} %get-tuple-element.31), channel_id=1, source_target_pairs={{0,128},{64,192},{128,0},{192,64},{1,129},{65,193},{129,1},{193,65... | collective-permute-start | bytes 196616 | tf_op jit(solution)/shard_map/ppermute | solution.py:439
  199.6 0.9 collective-permute-start.15
  200.4 1.3 collective-permute-done.17
  201.7 3.8 %collective-permute-done.16 = bf16[16,2048]{1,0:T(8,128)(2,1)S(1)} collective-permute-done((bf16[16,2048]{1,0:T(8,128)(2,1)S(1)}, bf16[16,2048]{1,0:T(8,128)(2,1)S(1)}, u32[]{:S(2)}, u32[]{:S(2)}) %collective-permute-start.16) | collective-permute-done | bytes 65568 | tf_op jit(solution)/shard_map/ppermute | solution.py:439
  205.5 0.7 fusion.9
  (67 shorter events, 0.7 us)
Async XLA Ops:
  0.0 63.3 %copy-start = (bf16[2048,512]{1,0:T(8,128)(2,1)S(1)}, bf16[2048,512]{1,0:T(8,128)(2,1)}, u32[]{:S(2)}) copy-start(bf16[2048,512]{1,0:T(8,128)(2,1)} %param.16) | copy-start | bytes 6291460
  0.0 2.9 %copy-start.5 = (bf16[128,2048]{1,0:T(8,128)(2,1)S(1)}, bf16[128,2048]{1,0:T(8,128)(2,1)}, u32[]{:S(2)}) copy-start(bf16[128,2048]{1,0:T(8,128)(2,1)} %param.14) | copy-start | bytes 1572868
  0.0 3.0 %copy-start.16 = (f32[2048]{0:T(1024)S(1)}, f32[2048]{0:T(1024)}, u32[]{:S(2)}) copy-start(f32[2048]{0:T(1024)} %param.15) | copy-start | bytes 24580
  0.0 3.0 %copy-start.20 = (bf16[2048,64]{0,1:T(8,128)(2,1)S(1)}, bf16[2048,64]{0,1:T(8,128)(2,1)}, u32[]{:S(2)}) copy-start(bf16[2048,64]{0,1:T(8,128)(2,1)} %param.17) | copy-start | bytes 786436
  1.4 8.4 %copy-start.17 = (f32[128,8]{0,1:T(8,128)S(1)}, f32[128,8]{0,1:T(8,128)}, u32[]{:S(2)}) copy-start(f32[128,8]{0,1:T(8,128)} %param.24) | copy-start | bytes 12292
  1.4 8.5 %copy-start.18 = (s32[128,8]{0,1:T(8,128)S(1)}, s32[128,8]{0,1:T(8,128)}, u32[]{:S(2)}) copy-start(s32[128,8]{0,1:T(8,128)} %param.23) | copy-start | bytes 12292
  3.0 12.0 %copy-start.19 = (f32[128]{0:T(128)S(1)}, f32[128]{0:T(128)}, u32[]{:S(2)}) copy-start(f32[128]{0:T(128)} %param.20) | copy-start | bytes 1540
  4.0 10.8 %all-to-all-start = ((f32[8,16,128]{2,1,0:T(8,128)}), f32[8,16,128]{2,1,0:T(8,128)S(1)}, u32[]{:S(2)}, u32[]{:S(2)}) async-start(f32[8,16,128]{2,1,0:T(8,128)} %bitcast.11), calls=%async_computation | async-start | bytes 131072 | tf_op jit(solution)/shard_map/all_to_all | solution.py:388
  33.8 0.7 copy-start.4
  51.1 14.7 %collective-permute-start = (bf16[4,4,2,128,128]{4,3,2,1,0:T(8,128)(2,1)}, bf16[4,4,2,128,128]{4,3,2,1,0:T(8,128)(2,1)}, u32[]{:S(2)}, u32[]{:S(2)}) collective-permute-start(bf16[4,4,2,128,128]{4,3,2,1,0:T(8,128)(2,1)} %bitcast.14.own_ref), channel_id=1, source_target_pairs={{0,8},{8,0},{1,9},{9,1},{2,10},{10,2},{3,11},{11,3},{4,12},{12,4},... | collective-permute-start | bytes 3145736 | tf_op jit(solution)/shard_map/ppermute | solution.py:409
  55.7 41.3 %collective-permute-start.5 = (bf16[288,2048]{1,0:T(8,128)(2,1)}, bf16[288,2048]{1,0:T(8,128)(2,1)}, u32[]{:S(2)}, u32[]{:S(2)}) collective-permute-start(bf16[288,2048]{1,0:T(8,128)(2,1)} %get-tuple-element.23), channel_id=1, source_target_pairs={{0,2},{2,4},{4,6},{6,0},{9,11},{11,13},{13,15},{15,9},{16,18},{18,... | collective-permute-start | bytes 3538952 | tf_op jit(solution)/shard_map/ppermute | solution.py:341
  57.4 41.4 %collective-permute-start.6 = (bf16[288,2048]{1,0:T(8,128)(2,1)}, bf16[288,2048]{1,0:T(8,128)(2,1)}, u32[]{:S(2)}, u32[]{:S(2)}) collective-permute-start(bf16[288,2048]{1,0:T(8,128)(2,1)} %get-tuple-element.23), channel_id=1, source_target_pairs={{1,10},{3,12},{5,14},{7,8},{8,3},{10,5},{12,7},{14,1},{17,26},{19,... | collective-permute-start | bytes 3538952 | tf_op jit(solution)/shard_map/ppermute | solution.py:342
  61.0 35.0 %collective-permute-start.4 = (bf16[288,2048]{1,0:T(8,128)(2,1)}, bf16[288,2048]{1,0:T(8,128)(2,1)}, u32[]{:S(2)}, u32[]{:S(2)}) collective-permute-start(bf16[288,2048]{1,0:T(8,128)(2,1)} %get-tuple-element.22), channel_id=1, source_target_pairs={{1,8},{3,10},{5,12},{7,14},{8,1},{10,3},{12,5},{14,7},{17,24},{19,... | collective-permute-start | bytes 3538952 | tf_op jit(solution)/shard_map/ppermute | solution.py:342
  70.5 22.9 %all-to-all-start.3 = ((bf16[8,16,2048]{2,1,0:T(8,128)(2,1)}), bf16[8,16,2048]{2,1,0:T(8,128)(2,1)S(1)}, u32[]{:S(2)}, u32[]{:S(2)}) async-start(bf16[8,16,2048]{2,1,0:T(8,128)(2,1)} %bitcast.50), calls=%async_computation.3 | async-start | bytes 1048576 | tf_op jit(solution)/shard_map/all_to_all | solution.py:420
  75.9 71.0 %collective-permute-start.7 = (bf16[288,2048]{1,0:T(8,128)(2,1)}, bf16[288,2048]{1,0:T(8,128)(2,1)}, u32[]{:S(2)}, u32[]{:S(2)}) collective-permute-start(bf16[288,2048]{1,0:T(8,128)(2,1)} %get-tuple-element.24), channel_id=1, source_target_pairs={{0,4},{2,6},{4,0},{6,2},{9,13},{11,15},{13,9},{15,11},{16,20},{18,... | collective-permute-start | bytes 3538952 | tf_op jit(solution)/shard_map/ppermute | solution.py:341
  77.5 69.5 %collective-permute-start.8 = (bf16[288,2048]{1,0:T(8,128)(2,1)}, bf16[288,2048]{1,0:T(8,128)(2,1)}, u32[]{:S(2)}, u32[]{:S(2)}) collective-permute-start(bf16[288,2048]{1,0:T(8,128)(2,1)} %get-tuple-element.24), channel_id=1, source_target_pairs={{1,12},{3,14},{5,8},{7,10},{8,5},{10,7},{12,1},{14,3},{17,28},{19,... | collective-permute-start | bytes 3538952 | tf_op jit(solution)/shard_map/ppermute | solution.py:342
  93.3 0.8 copy-start.6
  96.0 7.0 %collective-permute-start.1 = (bf16[16,2048]{1,0:T(8,128)(2,1)}, bf16[16,2048]{1,0:T(8,128)(2,1)S(1)}, u32[]{:S(2)}, u32[]{:S(2)}) collective-permute-start(bf16[16,2048]{1,0:T(8,128)(2,1)} %get-tuple-element.19.refs_0_), channel_id=1, source_target_pairs={{0,64},{64,128},{128,192},{192,0},{1,65},{65,129},{129,193},{193,1... | collective-permute-start | bytes 196616 | tf_op jit(solution)/shard_map/ppermute | solution.py:424
  97.0 24.6 %copy-start.10 = (bf16[16,2048]{1,0:T(8,128)(2,1)S(1)}, bf16[16,2048]{1,0:T(8,128)(2,1)}, u32[]{:S(2)}) copy-start(bf16[16,2048]{1,0:T(8,128)(2,1)} %get-tuple-element.19.refs_0_) | copy-start | bytes 196612
  97.0 52.0 %collective-permute-start.9 = (bf16[288,2048]{1,0:T(8,128)(2,1)}, bf16[288,2048]{1,0:T(8,128)(2,1)}, u32[]{:S(2)}, u32[]{:S(2)}) collective-permute-start(bf16[288,2048]{1,0:T(8,128)(2,1)} %get-tuple-element.25), channel_id=1, source_target_pairs={{0,6},{2,0},{4,2},{6,4},{9,15},{11,9},{13,11},{15,13},{16,22},{18,... | collective-permute-start | bytes 3538952 | tf_op jit(solution)/shard_map/ppermute | solution.py:341
  98.8 50.2 %collective-permute-start.10 = (bf16[288,2048]{1,0:T(8,128)(2,1)}, bf16[288,2048]{1,0:T(8,128)(2,1)}, u32[]{:S(2)}, u32[]{:S(2)}) collective-permute-start(bf16[288,2048]{1,0:T(8,128)(2,1)} %get-tuple-element.25), channel_id=1, source_target_pairs={{1,14},{3,8},{5,10},{7,12},{8,7},{10,1},{12,3},{14,5},{17,30},{19,... | collective-permute-start | bytes 3538952 | tf_op jit(solution)/shard_map/ppermute | solution.py:342
  103.0 4.1 %copy-start.11 = (bf16[16,2048]{1,0:T(8,128)(2,1)}, bf16[16,2048]{1,0:T(8,128)(2,1)S(1)}, u32[]{:S(2)}) copy-start(bf16[16,2048]{1,0:T(8,128)(2,1)S(1)} %collective-permute-done.1.refs_1_) | copy-start | bytes 196612
  103.0 18.5 %collective-permute-start.2 = (bf16[16,2048]{1,0:T(8,128)(2,1)}, bf16[16,2048]{1,0:T(8,128)(2,1)S(1)}, u32[]{:S(2)}, u32[]{:S(2)}) collective-permute-start(bf16[16,2048]{1,0:T(8,128)(2,1)} %get-tuple-element.19.refs_0_), channel_id=1, source_target_pairs={{0,128},{64,192},{128,0},{192,64},{1,129},{65,193},{129,1},{193,65... | collective-permute-start | bytes 196616 | tf_op jit(solution)/shard_map/ppermute | solution.py:424
  107.0 19.7 %copy-start.1 = (bf16[288,2048]{1,0:T(8,128)(2,1)}, bf16[288,2048]{1,0:T(8,128)(2,1)S(1)}, u32[]{:S(2)}) copy-start(bf16[288,2048]{1,0:T(8,128)(2,1)S(1)} %broadcast_select_fusion.3.refs_0_) | copy-start | bytes 3538948
  121.5 4.8 %copy-start.12 = (bf16[16,2048]{1,0:T(8,128)(2,1)}, bf16[16,2048]{1,0:T(8,128)(2,1)S(1)}, u32[]{:S(2)}) copy-start(bf16[16,2048]{1,0:T(8,128)(2,1)S(1)} %collective-permute-done.2.refs_2_) | copy-start | bytes 196612
  121.5 5.2 %collective-permute-start.3 = (bf16[16,2048]{1,0:T(8,128)(2,1)S(1)}, bf16[16,2048]{1,0:T(8,128)(2,1)S(1)}, u32[]{:S(2)}, u32[]{:S(2)}) collective-permute-start(bf16[16,2048]{1,0:T(8,128)(2,1)S(1)} %copy-done.10), channel_id=1, source_target_pairs={{0,192},{64,0},{128,64},{192,128},{1,193},{65,1},{129,65},{193,129... | collective-permute-start | bytes 196616 | tf_op jit(solution)/shard_map/ppermute | solution.py:424
  126.7 12.1 %copy-start.13 = (bf16[16,2048]{1,0:T(8,128)(2,1)}, bf16[16,2048]{1,0:T(8,128)(2,1)S(1)}, u32[]{:S(2)}) copy-start(bf16[16,2048]{1,0:T(8,128)(2,1)S(1)} %collective-permute-done.3.refs_3_) | copy-start | bytes 196612
  126.7 24.3 %collective-permute-start.11 = (bf16[288,2048]{1,0:T(8,128)(2,1)S(1)}, bf16[288,2048]{1,0:T(8,128)(2,1)}, u32[]{:S(2)}, u32[]{:S(2)}) collective-permute-start(bf16[288,2048]{1,0:T(8,128)(2,1)S(1)} %broadcast_select_fusion.3.refs_0_), channel_id=1, source_target_pairs={{0,8},{8,0},{1,9},{9,1},{2,10},{10,2},{3,11},{11,3},{4,12},{12,4},... | collective-permute-start | bytes 3538952 | tf_op jit(solution)/shard_map/ppermute | solution.py:346
  141.6 22.7 %all-to-all-start.4 = ((bf16[32,8,2048]{2,1,0:T(8,128)(2,1)}), bf16[32,8,2048]{2,1,0:T(8,128)(2,1)}, u32[]{:S(2)}, u32[]{:S(2)}) async-start(bf16[32,8,2048]{2,1,0:T(8,128)(2,1)} %bitcast.48), calls=%async_computation.4 | async-start | bytes 2097152 | tf_op jit(solution)/shard_map/all_to_all | solution.py:426
  146.9 4.1 %collective-permute-start.12 = (bf16[288,2048]{1,0:T(8,128)(2,1)}, bf16[288,2048]{1,0:T(8,128)(2,1)S(1)}, u32[]{:S(2)}, u32[]{:S(2)}) collective-permute-start(bf16[288,2048]{1,0:T(8,128)(2,1)} %broadcast_select_fusion.2.refs_1_), channel_id=1, source_target_pairs={{0,8},{8,0},{1,9},{9,1},{2,10},{10,2},{3,11},{11,3},{4,12},{12,4},... | collective-permute-start | bytes 3538952 | tf_op jit(solution)/shard_map/ppermute | solution.py:346
  148.4 2.0 copy-start.2
  148.4 3.3 %collective-permute-start.13 = (bf16[288,2048]{1,0:T(8,128)(2,1)S(1)}, bf16[288,2048]{1,0:T(8,128)(2,1)S(1)}, u32[]{:S(2)}, u32[]{:S(2)}) collective-permute-start(bf16[288,2048]{1,0:T(8,128)(2,1)S(1)} %broadcast_select_fusion.1.refs_2_), channel_id=1, source_target_pairs={{0,8},{8,0},{1,9},{9,1},{2,10},{10,2},{3,11},{11,3},{4,12},{12,4},... | collective-permute-start | bytes 3538952 | tf_op jit(solution)/shard_map/ppermute | solution.py:346
  150.4 1.3 copy-start.3
  150.4 3.2 %collective-permute-start.14 = (bf16[288,2048]{1,0:T(8,128)(2,1)S(1)}, bf16[288,2048]{1,0:T(8,128)(2,1)}, u32[]{:S(2)}, u32[]{:S(2)}) collective-permute-start(bf16[288,2048]{1,0:T(8,128)(2,1)S(1)} %broadcast_select_fusion.refs_3_), channel_id=1, source_target_pairs={{0,8},{8,0},{1,9},{9,1},{2,10},{10,2},{3,11},{11,3},{4,12},{12,4},... | collective-permute-start | bytes 3538952 | tf_op jit(solution)/shard_map/ppermute | solution.py:346
  151.0 1.0 copy-start.7
  152.0 1.1 copy-start.8
  171.5 21.2 %copy-start.15 = (bf16[64,256]{1,0:T(8,128)(2,1)S(1)}, bf16[64,256]{1,0:T(8,128)(2,1)}, u32[]{:S(2)}) copy-start(bf16[64,256]{1,0:T(8,128)(2,1)} %get-tuple-element.26) | copy-start | bytes 98308
  192.7 0.8 copy-start.14
  193.4 12.0 %copy-start.9 = (bf16[16,2048]{1,0:T(8,128)(2,1)S(1)}, bf16[16,2048]{1,0:T(8,128)(2,1)}, u32[]{:S(2)}) copy-start(bf16[16,2048]{1,0:T(8,128)(2,1)} %get-tuple-element.18) | copy-start | bytes 196612
  193.8 7.9 %collective-permute-start.17 = (bf16[16,2048]{1,0:T(8,128)(2,1)S(1)}, bf16[16,2048]{1,0:T(8,128)(2,1)S(1)}, u32[]{:S(2)}, u32[]{:S(2)}) collective-permute-start(bf16[16,2048]{1,0:T(8,128)(2,1)S(1)} %get-tuple-element.30), channel_id=1, source_target_pairs={{0,64},{64,128},{128,192},{192,0},{1,65},{65,129},{129,193},{193,1... | collective-permute-start | bytes 196616 | tf_op jit(solution)/shard_map/ppermute | solution.py:439
  196.1 9.4 %collective-permute-start.16 = (bf16[16,2048]{1,0:T(8,128)(2,1)S(1)}, bf16[16,2048]{1,0:T(8,128)(2,1)S(1)}, u32[]{:S(2)}, u32[]{:S(2)}) collective-permute-start(bf16[16,2048]{1,0:T(8,128)(2,1)S(1)} %get-tuple-element.31), channel_id=1, source_target_pairs={{0,128},{64,192},{128,0},{192,64},{1,129},{65,193},{129,1},{193,65... | collective-permute-start | bytes 196616 | tf_op jit(solution)/shard_map/ppermute | solution.py:439
  199.6 5.9 %collective-permute-start.15 = (bf16[16,2048]{1,0:T(8,128)(2,1)S(1)}, bf16[16,2048]{1,0:T(8,128)(2,1)S(1)}, u32[]{:S(2)}, u32[]{:S(2)}) collective-permute-start(bf16[16,2048]{1,0:T(8,128)(2,1)S(1)} %get-tuple-element.29), channel_id=1, source_target_pairs={{0,192},{64,0},{128,64},{192,128},{1,193},{65,1},{129,65},{193,129... | collective-permute-start | bytes 196616 | tf_op jit(solution)/shard_map/ppermute | solution.py:439

commit v4 on v3

--- a/solution.py
+++ b/solution.py
@@ -1,3 +1,4 @@
+import functools
 import math
 
 import jax
@@ -21,6 +22,7 @@
 PLANE = ("y", "x", "zl")
 
 norm_eps = 1e-06
+SPLIT = (2,)
 EXPERT_VMEM = 60 * 1024 * 1024
 BF = jnp.bfloat16
 F32 = jnp.float32
@@ -149,10 +151,9 @@
     )(blocks, tokens, gain.reshape(1, -1))
 
 
-def route_kernel(where_ref, ring_ref, *refs):
-    rows, (out_ref, high_ref, low_ref) = refs[:ZH], refs[ZH:]
+def table_kernel(gates, where_ref, ring_ref, table_ref):
     zh, zl = where_ref[0], where_ref[1]
-    share = rows[0].shape[0]
+    share = ring_ref.shape[1] - HEAD
     tails = jnp.concatenate(
         [ring_ref[(zh + ZH - k) % ZH * ZL + zl, HEAD:, :] for k in range(ZH)], axis=0
     ).astype(F32)
@@ -176,35 +177,49 @@
     earlier = jnp.dot(before.astype(BF), hits.astype(BF), preferred_element_type=F32)
     placed = jnp.logical_and(source == row // share, earlier == slot.astype(F32))
     table = jnp.where(placed, hits, 0.0)
-    mixing = table * gate
-    high = mixing.astype(BF)
-    high_ref[...] = high
-    low_ref[...] = (mixing - high.astype(F32)).astype(BF)
+    if gates:
+        mixing = table * gate
+        high = mixing.astype(BF)
+        table_ref[: ZH * share, :] = high
+        table_ref[ZH * share :, :] = (mixing - high.astype(F32)).astype(BF)
+    else:
+        table_ref[...] = table.T.astype(BF)
+
+
+def slot_table(where, ring, gates):
+    slots = Y * X * ZL * ZH * CAP
+    count = ZH * (ring.shape[1] - HEAD)
+    vmem = pl.BlockSpec(memory_space=pltpu.VMEM)
+    return pl.pallas_call(
+        functools.partial(table_kernel, gates),
+        out_shape=jax.ShapeDtypeStruct((2 * count, slots) if gates else (slots, count), BF),
+        in_specs=[pl.BlockSpec(memory_space=pltpu.SMEM), vmem],
+        out_specs=vmem,
+        cost_estimate=pl.CostEstimate(flops=3000000, bytes_accessed=400000, transcendentals=0),
+        name="gates" if gates else "table",
+    )(where, ring)
+
+
+def route_kernel(table_ref, *refs):
+    rows, out_ref = refs[:-1], refs[-1]
     whole = jnp.concatenate([ref[...] for ref in rows], axis=0)
-    turned_table = table.T.astype(BF)
     for i in range(D // SPAN):
         part = slice(i * SPAN, (i + 1) * SPAN)
         out_ref[:, part] = jnp.dot(
-            turned_table, whole[:, part], preferred_element_type=F32
+            table_ref[...], whole[:, part], preferred_element_type=F32
         ).astype(BF)
 
 
-def route(where, ring, rows):
+def route(table, rows):
     vmem = pl.BlockSpec(memory_space=pltpu.VMEM)
-    slots = Y * X * ZL * ZH * CAP
-    count = sum(r.shape[0] for r in rows)
     return pl.pallas_call(
         route_kernel,
-        out_shape=[
-            jax.ShapeDtypeStruct((slots, D), BF),
-            jax.ShapeDtypeStruct((count, slots), BF),
-            jax.ShapeDtypeStruct((count, slots), BF),
-        ],
-        in_specs=[pl.BlockSpec(memory_space=pltpu.SMEM)] + [vmem] * (1 + len(rows)),
-        out_specs=[vmem] * 3,
-        cost_estimate=pl.CostEstimate(flops=70000000, bytes_accessed=1700000, transcendentals=0),
+        out_shape=jax.ShapeDtypeStruct((table.shape[0], D), BF),
+        in_specs=[vmem] * (1 + len(rows)),
+        out_specs=vmem,
+        cost_estimate=pl.CostEstimate(flops=70000000, bytes_accessed=1400000, transcendentals=0),
         name="route",
-    )(where, ring, *rows)
+    )(table, *rows)
 
 
 def expert_kernel(rows_ref, *refs):
@@ -325,22 +340,27 @@
 def weight_pieces(w_gate, w_up, w_down, c, x, zl):
     packed = pack(x, jnp.swapaxes(w_gate, 1, 2), jnp.swapaxes(w_up, 1, 2), w_down)
 
-    def shifted(k, straight):
+    def shifted(k, straight, crossing):
         return [
             ((cs * X + xs) * ZL + zs, (zs * X + (xs + k) % X) * ZL + cs)
             for cs in range(C)
             for xs in range(X)
             for zs in range(ZL)
-            if (cs == zs) == straight
+            if (straight if cs == zs else crossing)
         ]
 
+    axes = ("c", "x", "zl")
     own = []
     for k in range(X):
-        straight = packed[0]
-        if k > 0:
-            straight = lax.ppermute(packed[k], ("c", "x", "zl"), shifted(k, True))
-        crossed = lax.ppermute(packed[k], ("c", "x", "zl"), shifted(k, False))
-        own.append(jnp.where(zl == c, straight, crossed))
+        if k in SPLIT:
+            straight = lax.ppermute(packed[k], axes, shifted(k, True, False))
+            moved = lax.ppermute(packed[k], axes, shifted(k, False, True))
+        else:
+            straight = packed[k]
+            moved = lax.ppermute(packed[k], axes, shifted(k, k > 0, True))
+        if k == 0 or k in SPLIT:
+            moved = jnp.where(zl == c, straight, moved)
+        own.append(moved)
     other = []
     for k in range(X):
         other.append(lax.ppermute(own[k], "c", [(0, 1), (1, 0)]))
@@ -422,7 +442,8 @@
     carried, moe_in = carry(blocks, own_tokens, moe_gain)
 
     rows = [moe_in] + [lax.ppermute(moe_in, "zh", turned(ZH, k)) for k in range(1, ZH)]
-    outgoing, mixing_high, mixing_low = route(place, ring, rows)
+    table = slot_table(place, ring, False)
+    outgoing = route(table, rows)
     arrived = lax.all_to_all(
         outgoing.reshape(Y * X * ZL, ZH * CAP, D), PLANE, 0, 0, tiled=True
     ).reshape(-1, D)
@@ -430,9 +451,9 @@
     returned = lax.all_to_all(
         answers.reshape(Y * X * ZL, ZH * CAP, D), PLANE, 0, 0, tiled=True
     ).reshape(-1, D)
-    sums = jnp.dot(mixing_high, returned, preferred_element_type=F32) + jnp.dot(
-        mixing_low, returned, preferred_element_type=F32
-    )
+    mixing = slot_table(place, ring, True)
+    sums = jnp.dot(mixing, returned, preferred_element_type=F32)
+    sums = sums[: ZH * share] + sums[ZH * share :]
     sums = sums.reshape(ZH, share, D)
     result = carried.astype(F32) + sums[0]
     for k in range(1, ZH):

time: 208 us -> 204 us (0.981)
  blocking collectives: 55.9 us -> 34.7 us
  waiting for transfers between devices: 47.1 us -> 55.8 us
  starting transfers between devices: 61.3 us -> 68.5 us
  other arithmetic: 12.2 us -> 8.78 us
  Pallas kernels: 21 us -> 24.4 us
    all_to_all x1 -> x0, blocking collectives: 21.2 us -> none  [on_device(): lax.all_to_all(answers.reshape(Y * X * ZL, ZH * CAP, D), PLANE, 0, 0, til...]
    ppermute x7 -> x5, waiting for transfers between devices: 0.02 us -> 17.2 us  [the longest x3 17.2 us: weight_pieces(): moved = lax.ppermute(packed[k], axes, shifted(k, k > 0, True))]
    all_to_all x0 -> x1, waiting for transfers between devices: none -> 13.9 us  [on_device(): lax.all_to_all(answers.reshape(Y * X * ZL, ZH * CAP, D), PLANE, 0, 0, til...]
    ppermute x4, starting transfers between devices: 13.3 us -> 0.69 us  [weight_pieces(): other.append(lax.ppermute(own[k], 'c', [(0, 1), (1, 0)]))]
    ppermute x3, waiting for transfers between devices: 14.8 us -> 3.21 us  [on_device(): lax.ppermute(moe_in, 'zh', turned(ZH, k))]
    all_to_all x0 -> x1, starting transfers between devices: none -> 11.4 us  [on_device(): lax.all_to_all(answers.reshape(Y * X * ZL, ZH * CAP, D), PLANE, 0, 0, til...]
    all_to_all x1, waiting for transfers between devices: 10.7 us -> 0.01 us  [on_device(): lax.all_to_all(outgoing.reshape(Y * X * ZL, ZH * CAP, D), PLANE, 0, 0, ti...]
    all_to_all x1, starting transfers between devices: 5.28 us -> 14.9 us  [on_device(): lax.all_to_all(outgoing.reshape(Y * X * ZL, ZH * CAP, D), PLANE, 0, 0, ti...]
  transfers between devices with their start and end apart: 21 -> 20, of which waited for: 9 -> 9; matrix products, arithmetic and copies ran while one was open for 5% -> 4% of each run, Pallas kernels for 7% -> 9%
where the time goes in v4:
time: 204 us; the launch traced here: 202 us
  starting transfers between devices  68.5 us (34%)
  waiting for transfers between devices  55.8 us (27%)
  blocking collectives  34.7 us (17%)
  Pallas kernels  24.4 us (12%)
  other arithmetic  8.78 us (4%)
  local copies, waits for them, and re-layouts  5.52 us (3%)
  matrix products  4.21 us (2%)
    all_to_all x2, blocking collectives, spread(): return lax.all_to_all(copies, axes, 0, 0, tiled=True)  34.7 us
    ppermute x3, waiting for transfers between devices, weight_pieces(): moved = lax.ppermute(packed[k], axes, shifted(k, k > 0, True))  17.2 us
    all_to_all x1, starting transfers between devices, on_device(): lax.all_to_all(outgoing.reshape(Y * X * ZL, ZH * CAP, D), PLANE, 0, 0, ti...  14.9 us
    all_to_all x1, waiting for transfers between devices, on_device(): lax.all_to_all(answers.reshape(Y * X * ZL, ZH * CAP, D), PLANE, 0, 0, til...  13.9 us
    all_to_all x1, waiting for transfers between devices, on_device(): lax.all_to_all(partial.reshape(X * ZL, share, D), NARROW, 0, 0, tiled=True)  13.6 us
    all_to_all x1, starting transfers between devices, on_device(): lax.all_to_all(answers.reshape(Y * X * ZL, ZH * CAP, D), PLANE, 0, 0, til...  11.4 us
    ppermute x3, starting transfers between devices, on_device(): back = lax.ppermute(sums[k].astype(BF), 'zh', turned(ZH, -k))  9.7 us
    ppermute x3, starting transfers between devices, on_device(): lax.ppermute(moe_in, 'zh', turned(ZH, k))  9.04 us
  transfers between devices with their start and end apart: 20, of which 9 were waited for; matrix products, arithmetic and copies ran while one was open for 4% of the time, Pallas kernels for 9%

profile of v4, /device:TPU:32, one launch (start us, length us, event | category | flops | bytes accessed | tf_op | source)
XLA Modules:
  0.0 202.2 jit_solution(10231960718605728948)
XLA Ops:
  0.0 1.4 fusion
  1.4 1.5 fusion.19
  3.0 0.4 fusion.21
  3.4 0.6 pad_maximum_fusion.2
  4.0 5.8 %all-to-all-start = ((f32[8,16,128]{2,1,0:T(8,128)}), f32[8,16,128]{2,1,0:T(8,128)S(1)}, u32[]{:S(2)}, u32[]{:S(2)}) async-start(f32[8,16,128]{2,1,0:T(8,128)} %bitcast.11), calls=%async_computation | async-start | bytes 131072 | tf_op jit(solution)/shard_map/all_to_all | solution.py:408
  9.8 0.1 fusion.26
  9.9 0.1 copy.36
  9.9 0.1 constant_dynamic-slice_fusion.2
  10.0 0.1 fusion.18
  10.1 0.1 copy.35
  10.2 4.6 %all-to-all-done = f32[8,16,128]{2,1,0:T(8,128)S(1)} async-done(((f32[8,16,128]{2,1,0:T(8,128)}), f32[8,16,128]{2,1,0:T(8,128)S(1)}, u32[]{:S(2)}, u32[]{:S(2)}) %all-to-all-start) | async-done | bytes 65568 | tf_op jit(solution)/shard_map/all_to_all | solution.py:408
  14.9 0.1 copy.32
  15.0 0.1 multiply_multiply_fusion
  15.1 0.2 fusion.14
  15.3 0.1 maximum_maximum_fusion
  15.5 18.3 %all_to_all.30.ring_ref = bf16[8,144,128]{2,1,0:T(8,128)(2,1)S(1)} all-to-all(bf16[8,144,128]{2,1,0:T(8,128)(2,1)S(1)} %broadcast_in_dim.7), channel_id=1, replica_groups=mesh['zh'=4,'y'=4,'c'=2,'x'=4,'zl'=2] {'zh','zl'}, dimensions={0} | all-to-all | bytes 589824 | tf_op jit(solution)/shard_map/all_to_all | solution.py:333
  33.8 0.2 broadcast_in_dim.8
  34.1 16.3 %all_to_all.31 = bf16[4,8,128,128]{3,2,1,0:T(8,128)(2,1)} all-to-all(bf16[4,8,128,128]{3,2,1,0:T(8,128)(2,1)S(1)} %broadcast_in_dim.8), channel_id=1, replica_groups=mesh['zh'=4,'y'=4,'c'=2,'x'=4,'zl'=2] {'y'}, dimensions={0} | all-to-all | bytes 2097152 | tf_op jit(solution)/shard_map/all_to_all | solution.py:333
  50.4 4.6 %pack.1 = (bf16[288,2048]{1,0:T(8,128)(2,1)}, bf16[288,2048]{1,0:T(8,128)(2,1)}, bf16[288,2048]{1,0:T(8,128)(2,1)}, bf16[288,2048]{1,0:T(8,128)(2,1)}) custom-call(s32[1]{0:T(128)} %bitcast.21.x_ref, bf16[4,96,2048]{2,1,0:T(8,128)(2,1)} %bitcast.43, bf16[4,96,2048]{2,1,0:T(8,128)(2,1)} %bitcast.44, bf16[4,96,2048]{2,1,0:T(8,128)(2,1)} %down_ref.1), custom_call_target="tpu_custom_call" | custom-call | bytes 9500000 | tf_op jit(solution)/shard_map/pack/pallas_call | solution.py:320
  55.0 3.6 %collective-permute-start.4 = (bf16[288,2048]{1,0:T(8,128)(2,1)}, bf16[288,2048]{1,0:T(8,128)(2,1)}, u32[]{:S(2)}, u32[]{:S(2)}) collective-permute-start(bf16[288,2048]{1,0:T(8,128)(2,1)} %get-tuple-element.17), channel_id=1, source_target_pairs={{1,8},{3,10},{5,12},{7,14},{8,1},{10,3},{12,5},{14,7},{17,24},{19,... | collective-permute-start | bytes 3538952 | tf_op jit(solution)/shard_map/ppermute | solution.py:360
  58.6 0.6 pad_add_fusion.where_ref
  59.2 0.3 fusion.17
  59.6 0.8 pad_maximum_fusion
  60.3 1.2 fusion.23.q_ref
  61.5 4.6 %attend.1 = bf16[128,2048]{1,0:T(8,128)(2,1)} custom-call(s32[2]{0:T(128)} %pad_add_fusion.where_ref, f32[128,512]{1,0:T(8,128)} %fusion.23.q_ref, f32[128,128]{1,0:T(8,128)} %get-tuple-element.37.cos_ref, f32[128,128]{1,0:T(8,128)} %get-tuple-element.38.sin_ref, f32[1,128]{1,0:T(1,128)} %bitcast.50, bf16[4,4,2,128,128]{4,3,2,1,0:T(8,128)(2,1)} %bitcast.14.own_ref, ...), custom_call_target="tpu_custom_call" | custom-call | flops 1400000000 | bytes 5000000 | tf_op jit(solution)/shard_map/attend/pallas_call | solution.py:111
  66.1 4.0 %all-to-all-start.3 = ((bf16[8,16,2048]{2,1,0:T(8,128)(2,1)}), bf16[8,16,2048]{2,1,0:T(8,128)(2,1)S(1)}, u32[]{:S(2)}, u32[]{:S(2)}) async-start(bf16[8,16,2048]{2,1,0:T(8,128)(2,1)} %bitcast.46), calls=%async_computation.3 | async-start | bytes 1048576 | tf_op jit(solution)/shard_map/all_to_all | solution.py:440
  70.1 1.7 collective-permute-start.6
  71.8 4.1 %collective-permute-start.7 = (bf16[288,2048]{1,0:T(8,128)(2,1)}, bf16[288,2048]{1,0:T(8,128)(2,1)}, u32[]{:S(2)}, u32[]{:S(2)}) collective-permute-start(bf16[288,2048]{1,0:T(8,128)(2,1)} %get-tuple-element.19), channel_id=1, source_target_pairs={{1,12},{3,14},{5,8},{7,10},{8,5},{10,7},{12,1},{14,3},{17,28},{19,... | collective-permute-start | bytes 3538952 | tf_op jit(solution)/shard_map/ppermute | solution.py:357
  75.8 0.6 constant_dynamic-slice_fusion.tokens_ref
  76.5 13.6 %all-to-all-done.3.blocks_ref = bf16[8,16,2048]{2,1,0:T(8,128)(2,1)S(1)} async-done(((bf16[8,16,2048]{2,1,0:T(8,128)(2,1)}), bf16[8,16,2048]{2,1,0:T(8,128)(2,1)S(1)}, u32[]{:S(2)}, u32[]{:S(2)}) %all-to-all-start.3) | async-done | bytes 524320 | tf_op jit(solution)/shard_map/all_to_all | solution.py:440
  90.1 0.8 copy-done.6
  90.9 1.9 carry.1
  92.8 5.4 %collective-permute-start.2 = (bf16[16,2048]{1,0:T(8,128)(2,1)}, bf16[16,2048]{1,0:T(8,128)(2,1)S(1)}, u32[]{:S(2)}, u32[]{:S(2)}) collective-permute-start(bf16[16,2048]{1,0:T(8,128)(2,1)} %get-tuple-element.16.refs_0_), channel_id=1, source_target_pairs={{0,128},{64,192},{128,0},{192,64},{1,129},{65,193},{129,1},{193,65... | collective-permute-start | bytes 196616 | tf_op jit(solution)/shard_map/ppermute | solution.py:444
  98.2 1.2 collective-permute-done.1.refs_1_
  99.4 3.6 %collective-permute-start.3 = (bf16[16,2048]{1,0:T(8,128)(2,1)}, bf16[16,2048]{1,0:T(8,128)(2,1)S(1)}, u32[]{:S(2)}, u32[]{:S(2)}) collective-permute-start(bf16[16,2048]{1,0:T(8,128)(2,1)} %get-tuple-element.16.refs_0_), channel_id=1, source_target_pairs={{0,192},{64,0},{128,64},{192,128},{1,193},{65,1},{129,65},{193,129... | collective-permute-start | bytes 196616 | tf_op jit(solution)/shard_map/ppermute | solution.py:444
  103.0 0.2 collective-permute-start.5
  103.2 2.0 %collective-permute-done.3.refs_3_ = bf16[16,2048]{1,0:T(8,128)(2,1)S(1)} collective-permute-done((bf16[16,2048]{1,0:T(8,128)(2,1)}, bf16[16,2048]{1,0:T(8,128)(2,1)S(1)}, u32[]{:S(2)}, u32[]{:S(2)}) %collective-permute-start.3) | collective-permute-done | bytes 65568 | tf_op jit(solution)/shard_map/ppermute | solution.py:444
  105.3 3.5 %collective-permute-start.8 = (bf16[288,2048]{1,0:T(8,128)(2,1)}, bf16[288,2048]{1,0:T(8,128)(2,1)}, u32[]{:S(2)}, u32[]{:S(2)}) collective-permute-start(bf16[288,2048]{1,0:T(8,128)(2,1)} %get-tuple-element.20), channel_id=1, source_target_pairs={{0,6},{1,14},{2,0},{3,8},{4,2},{5,10},{6,4},{7,12},{8,7},{9,15},{1... | collective-permute-start | bytes 3538952 | tf_op jit(solution)/shard_map/ppermute | solution.py:360
  108.8 0.6 pad_add_fusion.1.where_ref
  109.4 2.0 table.1.table_ref
  111.3 2.3 %route.1 = bf16[256,2048]{1,0:T(8,128)(2,1)} custom-call(bf16[256,64]{1,0:T(8,128)(2,1)} %table.1.table_ref, bf16[16,2048]{1,0:T(8,128)(2,1)} %get-tuple-element.16.refs_0_, bf16[16,2048]{1,0:T(8,128)(2,1)} %copy-done.11, bf16[16,2048]{1,0:T(8,128)(2,1)} %copy-done.12, bf16[16,2048]{1,0:T(8,128)(2,1)} %copy-done.13), custom_call_target="tpu_custom_call" | custom-call | flops 70000000 | bytes 1400000 | tf_op jit(solution)/shard_map/route/pallas_call | solution.py:215
  113.7 14.9 %all-to-all-start.4 = ((bf16[32,8,2048]{2,1,0:T(8,128)(2,1)}), bf16[32,8,2048]{2,1,0:T(8,128)(2,1)S(1)}, u32[]{:S(2)}, u32[]{:S(2)}) async-start(bf16[32,8,2048]{2,1,0:T(8,128)(2,1)} %bitcast.40), calls=%async_computation.4 | async-start | bytes 2097152 | tf_op jit(solution)/shard_map/all_to_all | solution.py:447
  128.6 1.4 broadcast_select_fusion.1.refs_0_
  130.0 0.1 collective-permute-start.9
  130.1 1.7 broadcast_select_fusion.refs_2_
  131.8 0.3 collective-permute-start.11
  132.1 0.3 collective-permute-start.10
  132.4 17.2 %collective-permute-done.8.refs_3_ = bf16[288,2048]{1,0:T(8,128)(2,1)} collective-permute-done((bf16[288,2048]{1,0:T(8,128)(2,1)}, bf16[288,2048]{1,0:T(8,128)(2,1)}, u32[]{:S(2)}, u32[]{:S(2)}) %collective-permute-start.8) | collective-permute-done | bytes 1179680 | tf_op jit(solution)/shard_map/ppermute | solution.py:360
  149.7 1.0 copy-done.7
  150.7 0.4 copy-done.9
  151.0 1.0 copy-done.8
  152.1 0.7 collective-permute-done.12.refs_7_
  152.8 1.0 copy-done.4
  153.8 7.1 %expert.1 = bf16[256,2048]{1,0:T(8,128)(2,1)} custom-call(bf16[256,2048]{1,0:T(8,128)(2,1)} %bitcast.41, bf16[288,2048]{1,0:T(8,128)(2,1)} %copy-done.1, bf16[288,2048]{1,0:T(8,128)(2,1)} %collective-permute-done.5.refs_1_, bf16[288,2048]{1,0:T(8,128)(2,1)} %copy-done.2, bf16[288,2048]{1,0:T(8,128)(2,1)} %collective-permute-done.8.refs_3_, ...), custom_call_target="tpu_custom_call" | custom-call | flops 2400000000 | bytes 11500000 | tf_op jit(solution)/shard_map/expert/pallas_call | solution.py:277
  160.9 11.4 %all-to-all-start.5 = ((bf16[32,8,2048]{2,1,0:T(8,128)(2,1)}), bf16[32,8,2048]{2,1,0:T(8,128)(2,1)S(1)}, u32[]{:S(2)}, u32[]{:S(2)}) async-start(bf16[32,8,2048]{2,1,0:T(8,128)(2,1)} %bitcast.42), calls=%async_computation.5 | async-start | bytes 2097152 | tf_op jit(solution)/shard_map/all_to_all | solution.py:451
  172.3 1.9 gates.1
  174.2 13.9 %all-to-all-done.5 = bf16[32,8,2048]{2,1,0:T(8,128)(2,1)S(1)} async-done(((bf16[32,8,2048]{2,1,0:T(8,128)(2,1)}), bf16[32,8,2048]{2,1,0:T(8,128)(2,1)S(1)}, u32[]{:S(2)}, u32[]{:S(2)}) %all-to-all-start.5) | async-done | bytes 1048608 | tf_op jit(solution)/shard_map/all_to_all | solution.py:451
  188.0 1.1 fusion.3
  189.3 0.2 collective-permute-start.15
  189.5 6.6 %collective-permute-start.14 = (bf16[16,2048]{1,0:T(8,128)(2,1)S(1)}, bf16[16,2048]{1,0:T(8,128)(2,1)S(1)}, u32[]{:S(2)}, u32[]{:S(2)}) collective-permute-start(bf16[16,2048]{1,0:T(8,128)(2,1)S(1)} %get-tuple-element.27), channel_id=1, source_target_pairs={{0,128},{64,192},{128,0},{192,64},{1,129},{65,193},{129,1},{193,65... | collective-permute-start | bytes 196616 | tf_op jit(solution)/shard_map/ppermute | solution.py:460
  196.1 2.9 %collective-permute-start.13 = (bf16[16,2048]{1,0:T(8,128)(2,1)S(1)}, bf16[16,2048]{1,0:T(8,128)(2,1)S(1)}, u32[]{:S(2)}, u32[]{:S(2)}) collective-permute-start(bf16[16,2048]{1,0:T(8,128)(2,1)S(1)} %get-tuple-element.25), channel_id=1, source_target_pairs={{0,192},{64,0},{128,64},{192,128},{1,193},{65,1},{129,65},{193,129... | collective-permute-start | bytes 196616 | tf_op jit(solution)/shard_map/ppermute | solution.py:460
  199.0 1.1 collective-permute-done.14
  200.1 1.4 collective-permute-done.13
  201.5 0.7 fusion.8
  (60 shorter events, 0.3 us)
Async XLA Ops:
  0.0 60.3 %copy-start = (bf16[2048,512]{1,0:T(8,128)(2,1)S(1)}, bf16[2048,512]{1,0:T(8,128)(2,1)}, u32[]{:S(2)}) copy-start(bf16[2048,512]{1,0:T(8,128)(2,1)} %param.16) | copy-start | bytes 6291460
  0.0 2.9 %copy-start.5 = (bf16[128,2048]{1,0:T(8,128)(2,1)S(1)}, bf16[128,2048]{1,0:T(8,128)(2,1)}, u32[]{:S(2)}) copy-start(bf16[128,2048]{1,0:T(8,128)(2,1)} %param.14) | copy-start | bytes 1572868
  0.0 3.0 %copy-start.14 = (f32[2048]{0:T(1024)S(1)}, f32[2048]{0:T(1024)}, u32[]{:S(2)}) copy-start(f32[2048]{0:T(1024)} %param.15) | copy-start | bytes 24580
  0.0 3.0 %copy-start.18 = (bf16[2048,64]{0,1:T(8,128)(2,1)S(1)}, bf16[2048,64]{0,1:T(8,128)(2,1)}, u32[]{:S(2)}) copy-start(bf16[2048,64]{0,1:T(8,128)(2,1)} %param.17) | copy-start | bytes 786436
  1.4 8.4 %copy-start.15 = (f32[128,8]{0,1:T(8,128)S(1)}, f32[128,8]{0,1:T(8,128)}, u32[]{:S(2)}) copy-start(f32[128,8]{0,1:T(8,128)} %param.24) | copy-start | bytes 12292
  1.4 8.5 %copy-start.16 = (s32[128,8]{0,1:T(8,128)S(1)}, s32[128,8]{0,1:T(8,128)}, u32[]{:S(2)}) copy-start(s32[128,8]{0,1:T(8,128)} %param.23) | copy-start | bytes 12292
  3.0 12.0 %copy-start.17 = (f32[128]{0:T(128)S(1)}, f32[128]{0:T(128)}, u32[]{:S(2)}) copy-start(f32[128]{0:T(128)} %param.20) | copy-start | bytes 1540
  4.0 10.8 %all-to-all-start = ((f32[8,16,128]{2,1,0:T(8,128)}), f32[8,16,128]{2,1,0:T(8,128)S(1)}, u32[]{:S(2)}, u32[]{:S(2)}) async-start(f32[8,16,128]{2,1,0:T(8,128)} %bitcast.11), calls=%async_computation | async-start | bytes 131072 | tf_op jit(solution)/shard_map/all_to_all | solution.py:408
  33.8 16.6 %copy-start.3 = (bf16[8,144,128]{2,1,0:T(8,128)(2,1)}, bf16[8,144,128]{2,1,0:T(8,128)(2,1)S(1)}, u32[]{:S(2)}) copy-start(bf16[8,144,128]{2,1,0:T(8,128)(2,1)S(1)} %all_to_all.30.ring_ref) | copy-start | bytes 884740
  50.4 11.1 %collective-permute-start = (bf16[4,4,2,128,128]{4,3,2,1,0:T(8,128)(2,1)}, bf16[4,4,2,128,128]{4,3,2,1,0:T(8,128)(2,1)}, u32[]{:S(2)}, u32[]{:S(2)}) collective-permute-start(bf16[4,4,2,128,128]{4,3,2,1,0:T(8,128)(2,1)} %bitcast.14.own_ref), channel_id=1, source_target_pairs={{0,8},{8,0},{1,9},{9,1},{2,10},{10,2},{3,11},{11,3},{4,12},{12,4},... | collective-permute-start | bytes 3145736 | tf_op jit(solution)/shard_map/ppermute | solution.py:429
  55.0 73.6 %collective-permute-start.4 = (bf16[288,2048]{1,0:T(8,128)(2,1)}, bf16[288,2048]{1,0:T(8,128)(2,1)}, u32[]{:S(2)}, u32[]{:S(2)}) collective-permute-start(bf16[288,2048]{1,0:T(8,128)(2,1)} %get-tuple-element.17), channel_id=1, source_target_pairs={{1,8},{3,10},{5,12},{7,14},{8,1},{10,3},{12,5},{14,7},{17,24},{19,... | collective-permute-start | bytes 3538952 | tf_op jit(solution)/shard_map/ppermute | solution.py:360
  66.1 24.0 %all-to-all-start.3 = ((bf16[8,16,2048]{2,1,0:T(8,128)(2,1)}), bf16[8,16,2048]{2,1,0:T(8,128)(2,1)S(1)}, u32[]{:S(2)}, u32[]{:S(2)}) async-start(bf16[8,16,2048]{2,1,0:T(8,128)(2,1)} %bitcast.46), calls=%async_computation.3 | async-start | bytes 1048576 | tf_op jit(solution)/shard_map/all_to_all | solution.py:440
  70.1 60.0 %collective-permute-start.6 = (bf16[288,2048]{1,0:T(8,128)(2,1)}, bf16[288,2048]{1,0:T(8,128)(2,1)}, u32[]{:S(2)}, u32[]{:S(2)}) collective-permute-start(bf16[288,2048]{1,0:T(8,128)(2,1)} %get-tuple-element.19), channel_id=1, source_target_pairs={{0,4},{2,6},{4,0},{6,2},{9,13},{11,15},{13,9},{15,11},{16,20},{18,... | collective-permute-start | bytes 3538952 | tf_op jit(solution)/shard_map/ppermute | solution.py:356
  71.8 58.3 %collective-permute-start.7 = (bf16[288,2048]{1,0:T(8,128)(2,1)}, bf16[288,2048]{1,0:T(8,128)(2,1)}, u32[]{:S(2)}, u32[]{:S(2)}) collective-permute-start(bf16[288,2048]{1,0:T(8,128)(2,1)} %get-tuple-element.19), channel_id=1, source_target_pairs={{1,12},{3,14},{5,8},{7,10},{8,5},{10,7},{12,1},{14,3},{17,28},{19,... | collective-permute-start | bytes 3538952 | tf_op jit(solution)/shard_map/ppermute | solution.py:357
  90.1 0.8 copy-start.6
  92.8 6.6 %collective-permute-start.1 = (bf16[16,2048]{1,0:T(8,128)(2,1)}, bf16[16,2048]{1,0:T(8,128)(2,1)S(1)}, u32[]{:S(2)}, u32[]{:S(2)}) collective-permute-start(bf16[16,2048]{1,0:T(8,128)(2,1)} %get-tuple-element.16.refs_0_), channel_id=1, source_target_pairs={{0,64},{64,128},{128,192},{192,0},{1,65},{65,129},{129,193},{193,1... | collective-permute-start | bytes 196616 | tf_op jit(solution)/shard_map/ppermute | solution.py:444
  92.8 10.2 %collective-permute-start.2 = (bf16[16,2048]{1,0:T(8,128)(2,1)}, bf16[16,2048]{1,0:T(8,128)(2,1)S(1)}, u32[]{:S(2)}, u32[]{:S(2)}) collective-permute-start(bf16[16,2048]{1,0:T(8,128)(2,1)} %get-tuple-element.16.refs_0_), channel_id=1, source_target_pairs={{0,128},{64,192},{128,0},{192,64},{1,129},{65,193},{129,1},{193,65... | collective-permute-start | bytes 196616 | tf_op jit(solution)/shard_map/ppermute | solution.py:444
  99.4 11.9 %copy-start.11 = (bf16[16,2048]{1,0:T(8,128)(2,1)}, bf16[16,2048]{1,0:T(8,128)(2,1)S(1)}, u32[]{:S(2)}) copy-start(bf16[16,2048]{1,0:T(8,128)(2,1)S(1)} %collective-permute-done.1.refs_1_) | copy-start | bytes 196612
  99.4 5.8 %collective-permute-start.3 = (bf16[16,2048]{1,0:T(8,128)(2,1)}, bf16[16,2048]{1,0:T(8,128)(2,1)S(1)}, u32[]{:S(2)}, u32[]{:S(2)}) collective-permute-start(bf16[16,2048]{1,0:T(8,128)(2,1)} %get-tuple-element.16.refs_0_), channel_id=1, source_target_pairs={{0,192},{64,0},{128,64},{192,128},{1,193},{65,1},{129,65},{193,129... | collective-permute-start | bytes 196616 | tf_op jit(solution)/shard_map/ppermute | solution.py:444
  103.0 8.3 %copy-start.12 = (bf16[16,2048]{1,0:T(8,128)(2,1)}, bf16[16,2048]{1,0:T(8,128)(2,1)S(1)}, u32[]{:S(2)}) copy-start(bf16[16,2048]{1,0:T(8,128)(2,1)S(1)} %collective-permute-done.2.refs_2_) | copy-start | bytes 196612
  103.0 29.1 %collective-permute-start.5 = (bf16[288,2048]{1,0:T(8,128)(2,1)}, bf16[288,2048]{1,0:T(8,128)(2,1)}, u32[]{:S(2)}, u32[]{:S(2)}) collective-permute-start(bf16[288,2048]{1,0:T(8,128)(2,1)} %get-tuple-element.18), channel_id=1, source_target_pairs={{0,2},{1,10},{2,4},{3,12},{4,6},{5,14},{6,0},{7,8},{8,3},{9,11},{1... | collective-permute-start | bytes 3538952 | tf_op jit(solution)/shard_map/ppermute | solution.py:360
  105.3 6.1 %copy-start.13 = (bf16[16,2048]{1,0:T(8,128)(2,1)}, bf16[16,2048]{1,0:T(8,128)(2,1)S(1)}, u32[]{:S(2)}) copy-start(bf16[16,2048]{1,0:T(8,128)(2,1)S(1)} %collective-permute-done.3.refs_3_) | copy-start | bytes 196612
  105.3 44.3 %collective-permute-start.8 = (bf16[288,2048]{1,0:T(8,128)(2,1)}, bf16[288,2048]{1,0:T(8,128)(2,1)}, u32[]{:S(2)}, u32[]{:S(2)}) collective-permute-start(bf16[288,2048]{1,0:T(8,128)(2,1)} %get-tuple-element.20), channel_id=1, source_target_pairs={{0,6},{1,14},{2,0},{3,8},{4,2},{5,10},{6,4},{7,12},{8,7},{9,15},{1... | collective-permute-start | bytes 3538952 | tf_op jit(solution)/shard_map/ppermute | solution.py:360
  113.7 39.1 %all-to-all-start.4 = ((bf16[32,8,2048]{2,1,0:T(8,128)(2,1)}), bf16[32,8,2048]{2,1,0:T(8,128)(2,1)S(1)}, u32[]{:S(2)}, u32[]{:S(2)}) async-start(bf16[32,8,2048]{2,1,0:T(8,128)(2,1)} %bitcast.40), calls=%async_computation.4 | async-start | bytes 2097152 | tf_op jit(solution)/shard_map/all_to_all | solution.py:447
  130.0 1.8 copy-start.1
  130.0 19.6 %collective-permute-start.9 = (bf16[288,2048]{1,0:T(8,128)(2,1)S(1)}, bf16[288,2048]{1,0:T(8,128)(2,1)S(1)}, u32[]{:S(2)}, u32[]{:S(2)}) collective-permute-start(bf16[288,2048]{1,0:T(8,128)(2,1)S(1)} %broadcast_select_fusion.1.refs_0_), channel_id=1, source_target_pairs={{0,8},{8,0},{1,9},{9,1},{2,10},{10,2},{3,11},{11,3},{4,12},{12,4},... | collective-permute-start | bytes 3538952 | tf_op jit(solution)/shard_map/ppermute | solution.py:366
  131.8 17.8 %copy-start.2 = (bf16[288,2048]{1,0:T(8,128)(2,1)}, bf16[288,2048]{1,0:T(8,128)(2,1)S(1)}, u32[]{:S(2)}) copy-start(bf16[288,2048]{1,0:T(8,128)(2,1)S(1)} %broadcast_select_fusion.refs_2_) | copy-start | bytes 3538948
  131.8 17.8 %collective-permute-start.11 = (bf16[288,2048]{1,0:T(8,128)(2,1)S(1)}, bf16[288,2048]{1,0:T(8,128)(2,1)S(1)}, u32[]{:S(2)}, u32[]{:S(2)}) collective-permute-start(bf16[288,2048]{1,0:T(8,128)(2,1)S(1)} %broadcast_select_fusion.refs_2_), channel_id=1, source_target_pairs={{0,8},{8,0},{1,9},{9,1},{2,10},{10,2},{3,11},{11,3},{4,12},{12,4},... | collective-permute-start | bytes 3538952 | tf_op jit(solution)/shard_map/ppermute | solution.py:366
  132.1 17.5 %collective-permute-start.10 = (bf16[288,2048]{1,0:T(8,128)(2,1)}, bf16[288,2048]{1,0:T(8,128)(2,1)S(1)}, u32[]{:S(2)}, u32[]{:S(2)}) collective-permute-start(bf16[288,2048]{1,0:T(8,128)(2,1)} %collective-permute-done.5.refs_1_), channel_id=1, source_target_pairs={{0,8},{8,0},{1,9},{9,1},{2,10},{10,2},{3,11},{11,3},{4,12},{12,4},... | collective-permute-start | bytes 3538952 | tf_op jit(solution)/shard_map/ppermute | solution.py:366
  149.6 3.2 %collective-permute-start.12 = (bf16[288,2048]{1,0:T(8,128)(2,1)}, bf16[288,2048]{1,0:T(8,128)(2,1)}, u32[]{:S(2)}, u32[]{:S(2)}) collective-permute-start(bf16[288,2048]{1,0:T(8,128)(2,1)} %collective-permute-done.8.refs_3_), channel_id=1, source_target_pairs={{0,8},{8,0},{1,9},{9,1},{2,10},{10,2},{3,11},{11,3},{4,12},{12,4},... | collective-permute-start | bytes 3538952 | tf_op jit(solution)/shard_map/ppermute | solution.py:366
  149.6 1.1 copy-start.7
  149.6 1.4 copy-start.9
  151.0 1.0 copy-start.8
  152.8 1.0 copy-start.4
  160.9 27.1 %all-to-all-start.5 = ((bf16[32,8,2048]{2,1,0:T(8,128)(2,1)}), bf16[32,8,2048]{2,1,0:T(8,128)(2,1)S(1)}, u32[]{:S(2)}, u32[]{:S(2)}) async-start(bf16[32,8,2048]{2,1,0:T(8,128)(2,1)} %bitcast.42), calls=%async_computation.5 | async-start | bytes 2097152 | tf_op jit(solution)/shard_map/all_to_all | solution.py:451
  189.2 12.3 %copy-start.10 = (bf16[16,2048]{1,0:T(8,128)(2,1)S(1)}, bf16[16,2048]{1,0:T(8,128)(2,1)}, u32[]{:S(2)}) copy-start(bf16[16,2048]{1,0:T(8,128)(2,1)} %get-tuple-element.15) | copy-start | bytes 196612
  189.3 9.7 %collective-permute-start.15 = (bf16[16,2048]{1,0:T(8,128)(2,1)S(1)}, bf16[16,2048]{1,0:T(8,128)(2,1)S(1)}, u32[]{:S(2)}, u32[]{:S(2)}) collective-permute-start(bf16[16,2048]{1,0:T(8,128)(2,1)S(1)} %get-tuple-element.26), channel_id=1, source_target_pairs={{0,64},{64,128},{128,192},{192,0},{1,65},{65,129},{129,193},{193,1... | collective-permute-start | bytes 196616 | tf_op jit(solution)/shard_map/ppermute | solution.py:460
  189.5 10.6 %collective-permute-start.14 = (bf16[16,2048]{1,0:T(8,128)(2,1)S(1)}, bf16[16,2048]{1,0:T(8,128)(2,1)S(1)}, u32[]{:S(2)}, u32[]{:S(2)}) collective-permute-start(bf16[16,2048]{1,0:T(8,128)(2,1)S(1)} %get-tuple-element.27), channel_id=1, source_target_pairs={{0,128},{64,192},{128,0},{192,64},{1,129},{65,193},{129,1},{193,65... | collective-permute-start | bytes 196616 | tf_op jit(solution)/shard_map/ppermute | solution.py:460
  196.1 5.4 %collective-permute-start.13 = (bf16[16,2048]{1,0:T(8,128)(2,1)S(1)}, bf16[16,2048]{1,0:T(8,128)(2,1)S(1)}, u32[]{:S(2)}, u32[]{:S(2)}) collective-permute-start(bf16[16,2048]{1,0:T(8,128)(2,1)S(1)} %get-tuple-element.25), channel_id=1, source_target_pairs={{0,192},{64,0},{128,64},{192,128},{1,193},{65,1},{129,65},{193,129... | collective-permute-start | bytes 196616 | tf_op jit(solution)/shard_map/ppermute | solution.py:460

commit v5 on v4

--- a/solution.py
+++ b/solution.py
@@ -295,23 +295,29 @@
 
 
 def pack_kernel(x_ref, gate_ref, up_ref, down_ref, *refs):
-    outs, sems = refs[:X], refs[X]
+    outs, held, sems, out_sems = refs[:X], refs[X], refs[X + 1], refs[X + 2]
     width = down_ref.shape[1]
 
-    def copy(k, part):
+    def fetch(k, part):
         source = (gate_ref, up_ref, down_ref)[part]
         return pltpu.make_async_copy(
             source.at[(x_ref[0] + k) % X],
-            outs[k].at[pl.ds(part * width, width)],
+            held.at[k, pl.ds(part * width, width)],
             sems.at[k, part],
         )
 
+    def store(k):
+        return pltpu.make_async_copy(held.at[k], outs[k], out_sems.at[k])
+
     for k in range(X):
         for part in range(3):
-            copy(k, part).start()
+            fetch(k, part).start()
     for k in range(X):
         for part in range(3):
-            copy(k, part).wait()
+            fetch(k, part).wait()
+        store(k).start()
+    for k in range(X):
+        store(k).wait()
 
 
 def pack(x, gate_t, up_t, w_down):
@@ -321,11 +327,45 @@
         pack_kernel,
         out_shape=[jax.ShapeDtypeStruct((3 * width, D), BF)] * X,
         in_specs=[pl.BlockSpec(memory_space=pltpu.SMEM), hbm, hbm, hbm],
-        out_specs=[pl.BlockSpec(memory_space=pltpu.VMEM)] * X,
-        scratch_shapes=[pltpu.SemaphoreType.DMA((X, 3))],
+        out_specs=[hbm] * X,
+        scratch_shapes=[
+            pltpu.VMEM((X, 3 * width, D), BF),
+            pltpu.SemaphoreType.DMA((X, 3)),
+            pltpu.SemaphoreType.DMA((X,)),
+        ],
         cost_estimate=pl.CostEstimate(flops=0, bytes_accessed=9500000, transcendentals=0),
         name="pack",
     )(x.reshape(1).astype(jnp.int32), gate_t, up_t, w_down)
+
+
+def columns_kernel(tokens_ref, gain_ref, key_ref, value_ref, normed_ref, out_ref, held):
+    normed = rms_norm(tokens_ref[...], gain_ref[...]).astype(BF)
+    normed_ref[...] = normed
+    entries = out_ref.shape[1]
+    for i, ref in enumerate((key_ref, value_ref)):
+        held[i] = lax.dot_general(
+            ref[...], normed, (((1,), (1,)), ((), ())), preferred_element_type=F32
+        )
+        for h in range(KV_HEADS):
+            out_ref[2 * h + i] = held[i, pl.ds(h, entries, stride=KV_HEADS), :]
+
+
+def columns(tokens, gain, key_t, value_t):
+    rows = tokens.shape[0]
+    width = key_t.shape[0]
+    vmem = pl.BlockSpec(memory_space=pltpu.VMEM)
+    return pl.pallas_call(
+        columns_kernel,
+        out_shape=[
+            jax.ShapeDtypeStruct(tokens.shape, BF),
+            jax.ShapeDtypeStruct((2 * KV_HEADS, width // KV_HEADS, rows), F32),
+        ],
+        in_specs=[vmem] * 4,
+        out_specs=[vmem] * 2,
+        scratch_shapes=[pltpu.VMEM((2, width, rows), F32)],
+        cost_estimate=pl.CostEstimate(flops=70000000, bytes_accessed=1700000, transcendentals=128),
+        name="columns",
+    )(tokens, gain.reshape(1, -1), key_t, value_t)
 
 
 def spread(piece, axes, members):
@@ -395,16 +435,7 @@
 
     pieces = weight_pieces(w_gate, w_up, w_down, c, x, zl)
 
-    normed = rms_norm(tokens, attn_gain).astype(BF)
-
-    def columns(w):
-        turned_w = lax.dot_general(
-            w, normed, (((0,), (1,)), ((), ())), preferred_element_type=F32
-        )
-        return jnp.swapaxes(turned_w.reshape(-1, KV_HEADS, local_rows), 0, 1)
-
-    both = jnp.stack([columns(w_key), columns(w_value)], axis=1)
-    both = both.reshape(X * ZL, -1, local_rows)
+    normed, both = columns(tokens, attn_gain, w_key.T, w_value.T)
     one = lax.all_to_all(both, NARROW, 0, 0, tiled=True).reshape(HEAD, local_rows)
     key_t = one * lax.rsqrt(jnp.mean(one * one, axis=0, keepdims=True) + norm_eps)
     key_t = key_t * key_gain[:, None]

time: 204 us -> 203 us (level)
  starting transfers between devices: 68.5 us -> 64.2 us
  waiting for transfers between devices: 55.8 us -> 59.6 us
  Pallas kernels: 24.4 us -> 26.7 us
    ppermute x3, starting transfers between devices: 9.7 us -> 7.05 us  [on_device(): back = lax.ppermute(sums[k].astype(BF), 'zh', turned(ZH, -k))]
    pallas_call x0 -> x1, Pallas kernels: none -> 2.63 us  [columns(): pl.pallas_call(columns_kernel, out_shape=[jax.ShapeDtypeStruct(tokens.sha...]
    ppermute x3, waiting for transfers between devices: 2.52 us -> 5.01 us  [on_device(): back = lax.ppermute(sums[k].astype(BF), 'zh', turned(ZH, -k))]
    unnamed x40 -> x34, local copies, waits for them, and re-layouts: 4.38 us -> 4.23 us
  transfers between devices with their start and end apart: 20 -> 20, of which waited for: 9 -> 9; matrix products, arithmetic and copies ran while one was open for 4% -> 5% of each run, Pallas kernels for 9% -> 8%
where the time goes in v5:
time: 203 us; the launch traced here: 202 us
  starting transfers between devices  64.2 us (32%)
  waiting for transfers between devices  59.6 us (29%)
  blocking collectives  34.6 us (17%)
  Pallas kernels  26.7 us (13%)
  other arithmetic  6.74 us (3%)
  local copies, waits for them, and re-layouts  6.37 us (3%)
  matrix products  3.34 us (2%)
    all_to_all x2, blocking collectives, spread(): return lax.all_to_all(copies, axes, 0, 0, tiled=True)  34.6 us
    ppermute x3, waiting for transfers between devices, weight_pieces(): moved = lax.ppermute(packed[k], axes, shifted(k, k > 0, True))  16.9 us
    all_to_all x1, starting transfers between devices, on_device(): lax.all_to_all(outgoing.reshape(Y * X * ZL, ZH * CAP, D), PLANE, 0, 0, ti...  15.9 us
    all_to_all x1, waiting for transfers between devices, on_device(): lax.all_to_all(answers.reshape(Y * X * ZL, ZH * CAP, D), PLANE, 0, 0, til...  14.9 us
    all_to_all x1, waiting for transfers between devices, on_device(): lax.all_to_all(partial.reshape(X * ZL, share, D), NARROW, 0, 0, tiled=True)  13 us
    all_to_all x1, starting transfers between devices, on_device(): lax.all_to_all(answers.reshape(Y * X * ZL, ZH * CAP, D), PLANE, 0, 0, til...  10.3 us
    ppermute x3, starting transfers between devices, on_device(): lax.ppermute(moe_in, 'zh', turned(ZH, k))  8.61 us
    pallas_call x1, Pallas kernels, expert(): pl.pallas_call(expert_kernel, out_shape=jax.ShapeDtypeStruct((count, D),...  7.13 us
  transfers between devices with their start and end apart: 20, of which 9 were waited for; matrix products, arithmetic and copies ran while one was open for 5% of the time, Pallas kernels for 8%

profile of v5, /device:TPU:32, one launch (start us, length us, event | category | flops | bytes accessed | tf_op | source)
XLA Modules:
  0.0 201.8 jit_solution(17812100592233113610)
XLA Ops:
  0.0 2.6 %columns.1 = (bf16[128,2048]{1,0:T(8,128)(2,1)}, f32[8,16,128]{2,1,0:T(8,128)}) custom-call(bf16[128,2048]{1,0:T(8,128)(2,1)} %tokens_ref.1, f32[1,2048]{1,0:T(1,128)} %bitcast.38, bf16[64,2048]{1,0:T(8,128)(2,1)} %bitcast.36, bf16[64,2048]{1,0:T(8,128)(2,1)} %bitcast.37), custom_call_target="tpu_custom_call" | custom-call | flops 70000000 | bytes 1700000 | tf_op jit(solution)/shard_map/columns/pallas_call | solution.py:357
  2.7 5.8 %all-to-all-start = ((f32[8,16,128]{2,1,0:T(8,128)}), f32[8,16,128]{2,1,0:T(8,128)S(1)}, u32[]{:S(2)}, u32[]{:S(2)}) async-start(f32[8,16,128]{2,1,0:T(8,128)} %get-tuple-element.16), calls=%async_computation | async-start | bytes 131072 | tf_op jit(solution)/shard_map/all_to_all | solution.py:439
  8.4 0.1 dynamic-slice_reduce_fusion
  8.5 0.1 subtract_convert_fusion
  8.6 0.1 dynamic-slice_convert_fusion
  8.7 0.1 copy.18
  8.7 0.1 copy.17
  8.8 0.1 copy.16
  8.9 4.6 %all-to-all-done = f32[8,16,128]{2,1,0:T(8,128)S(1)} async-done(((f32[8,16,128]{2,1,0:T(8,128)}), f32[8,16,128]{2,1,0:T(8,128)S(1)}, u32[]{:S(2)}, u32[]{:S(2)}) %all-to-all-start) | async-done | bytes 65568 | tf_op jit(solution)/shard_map/all_to_all | solution.py:439
  13.5 0.1 copy.15
  13.6 0.1 multiply_multiply_fusion
  13.7 0.2 fusion.11
  14.0 0.1 maximum_maximum_fusion
  14.1 18.3 %all_to_all.30.ring_ref = bf16[8,144,128]{2,1,0:T(8,128)(2,1)S(1)} all-to-all(bf16[8,144,128]{2,1,0:T(8,128)(2,1)S(1)} %broadcast_in_dim.7), channel_id=1, replica_groups=mesh['zh'=4,'y'=4,'c'=2,'x'=4,'zl'=2] {'zh','zl'}, dimensions={0} | all-to-all | bytes 589824 | tf_op jit(solution)/shard_map/all_to_all | solution.py:373
  32.5 0.2 broadcast_in_dim.8
  32.7 16.2 %all_to_all.31 = bf16[4,8,128,128]{3,2,1,0:T(8,128)(2,1)S(1)} all-to-all(bf16[4,8,128,128]{3,2,1,0:T(8,128)(2,1)S(1)} %broadcast_in_dim.8), channel_id=1, replica_groups=mesh['zh'=4,'y'=4,'c'=2,'x'=4,'zl'=2] {'y'}, dimensions={0} | all-to-all | bytes 2097152 | tf_op jit(solution)/shard_map/all_to_all | solution.py:373
  48.9 0.0 collective-permute-start
  49.0 4.3 %pack.1 = (bf16[288,2048]{1,0:T(8,128)(2,1)}, bf16[288,2048]{1,0:T(8,128)(2,1)}, bf16[288,2048]{1,0:T(8,128)(2,1)}, bf16[288,2048]{1,0:T(8,128)(2,1)}) custom-call(s32[1]{0:T(128)} %bitcast.15.x_ref, bf16[4,96,2048]{2,1,0:T(8,128)(2,1)} %bitcast.30, bf16[4,96,2048]{2,1,0:T(8,128)(2,1)} %bitcast.31, bf16[4,96,2048]{2,1,0:T(8,128)(2,1)} %down_ref.1), custom_call_target="tpu_custom_call" | custom-call | bytes 9500000 | tf_op jit(solution)/shard_map/pack/pallas_call | solution.py:326
  53.2 3.2 %collective-permute-start.4 = (bf16[288,2048]{1,0:T(8,128)(2,1)}, bf16[288,2048]{1,0:T(8,128)(2,1)}, u32[]{:S(2)}, u32[]{:S(2)}) collective-permute-start(bf16[288,2048]{1,0:T(8,128)(2,1)} %get-tuple-element.21), channel_id=1, source_target_pairs={{1,8},{3,10},{5,12},{7,14},{8,1},{10,3},{12,5},{14,7},{17,24},{19,... | collective-permute-start | bytes 3538952 | tf_op jit(solution)/shard_map/ppermute | solution.py:400
  56.5 0.6 pad_add_fusion.where_ref
  57.1 0.3 fusion.14
  57.4 0.8 pad_maximum_fusion
  58.2 2.2 %fusion.19.q_ref = f32[128,512]{1,0:T(8,128)} fusion(bf16[128,2048]{1,0:T(8,128)(2,1)} %get-tuple-element.15, bf16[2048,512]{1,0:T(8,128)(2,1)S(1)} %copy-done), kind=kOutput, calls=%fused_computation.42 | convolution fusion | flops 268435456 | bytes 2883584 | tf_op jit(solution)/shard_map/dot_general | solution.py:462
  60.4 0.0 collective-permute-done.other_ref
  60.4 4.6 %attend.1 = bf16[128,2048]{1,0:T(8,128)(2,1)} custom-call(s32[2]{0:T(128)} %pad_add_fusion.where_ref, f32[128,512]{1,0:T(8,128)} %fusion.19.q_ref, f32[128,128]{1,0:T(8,128)} %get-tuple-element.37.cos_ref, f32[128,128]{1,0:T(8,128)} %get-tuple-element.38.sin_ref, f32[1,128]{1,0:T(1,128)} %bitcast.40, bf16[4,4,2,128,128]{4,3,2,1,0:T(8,128)(2,1)} %bitcast.33, ...), custom_call_target="tpu_custom_call" | custom-call | flops 1400000000 | bytes 5000000 | tf_op jit(solution)/shard_map/attend/pallas_call | solution.py:111
  65.0 4.0 %all-to-all-start.3 = ((bf16[8,16,2048]{2,1,0:T(8,128)(2,1)}), bf16[8,16,2048]{2,1,0:T(8,128)(2,1)S(1)}, u32[]{:S(2)}, u32[]{:S(2)}) async-start(bf16[8,16,2048]{2,1,0:T(8,128)(2,1)} %bitcast.35), calls=%async_computation.3 | async-start | bytes 1048576 | tf_op jit(solution)/shard_map/all_to_all | solution.py:471
  69.0 1.7 collective-permute-start.6
  70.7 4.4 %collective-permute-start.7 = (bf16[288,2048]{1,0:T(8,128)(2,1)}, bf16[288,2048]{1,0:T(8,128)(2,1)}, u32[]{:S(2)}, u32[]{:S(2)}) collective-permute-start(bf16[288,2048]{1,0:T(8,128)(2,1)} %get-tuple-element.23), channel_id=1, source_target_pairs={{1,12},{3,14},{5,8},{7,10},{8,5},{10,7},{12,1},{14,3},{17,28},{19,... | collective-permute-start | bytes 3538952 | tf_op jit(solution)/shard_map/ppermute | solution.py:397
  75.1 1.5 constant_dynamic-slice_fusion.tokens_ref
  76.6 13.0 %all-to-all-done.3.blocks_ref = bf16[8,16,2048]{2,1,0:T(8,128)(2,1)S(1)} async-done(((bf16[8,16,2048]{2,1,0:T(8,128)(2,1)}), bf16[8,16,2048]{2,1,0:T(8,128)(2,1)S(1)}, u32[]{:S(2)}, u32[]{:S(2)}) %all-to-all-start.3) | async-done | bytes 524320 | tf_op jit(solution)/shard_map/all_to_all | solution.py:471
  89.6 0.8 copy-done.5
  90.4 1.9 carry.1
  92.3 5.0 %collective-permute-start.2 = (bf16[16,2048]{1,0:T(8,128)(2,1)}, bf16[16,2048]{1,0:T(8,128)(2,1)S(1)}, u32[]{:S(2)}, u32[]{:S(2)}) collective-permute-start(bf16[16,2048]{1,0:T(8,128)(2,1)} %get-tuple-element.20.refs_0_), channel_id=1, source_target_pairs={{0,128},{64,192},{128,0},{192,64},{1,129},{65,193},{129,1},{193,65... | collective-permute-start | bytes 196616 | tf_op jit(solution)/shard_map/ppermute | solution.py:475
  97.3 1.6 collective-permute-done.1.refs_1_
  98.9 3.6 %collective-permute-start.3 = (bf16[16,2048]{1,0:T(8,128)(2,1)}, bf16[16,2048]{1,0:T(8,128)(2,1)S(1)}, u32[]{:S(2)}, u32[]{:S(2)}) collective-permute-start(bf16[16,2048]{1,0:T(8,128)(2,1)} %get-tuple-element.20.refs_0_), channel_id=1, source_target_pairs={{0,192},{64,0},{128,64},{192,128},{1,193},{65,1},{129,65},{193,129... | collective-permute-start | bytes 196616 | tf_op jit(solution)/shard_map/ppermute | solution.py:475
  102.5 2.8 %collective-permute-done.3.refs_3_ = bf16[16,2048]{1,0:T(8,128)(2,1)S(1)} collective-permute-done((bf16[16,2048]{1,0:T(8,128)(2,1)}, bf16[16,2048]{1,0:T(8,128)(2,1)S(1)}, u32[]{:S(2)}, u32[]{:S(2)}) %collective-permute-start.3) | collective-permute-done | bytes 65568 | tf_op jit(solution)/shard_map/ppermute | solution.py:475
  105.4 2.4 %collective-permute-start.8 = (bf16[288,2048]{1,0:T(8,128)(2,1)}, bf16[288,2048]{1,0:T(8,128)(2,1)}, u32[]{:S(2)}, u32[]{:S(2)}) collective-permute-start(bf16[288,2048]{1,0:T(8,128)(2,1)} %get-tuple-element.24), channel_id=1, source_target_pairs={{0,6},{1,14},{2,0},{3,8},{4,2},{5,10},{6,4},{7,12},{8,7},{9,15},{1... | collective-permute-start | bytes 3538952 | tf_op jit(solution)/shard_map/ppermute | solution.py:400
  107.7 0.6 pad_add_fusion.1.where_ref
  108.3 2.0 table.1.table_ref
  110.3 2.3 %route.1 = bf16[256,2048]{1,0:T(8,128)(2,1)} custom-call(bf16[256,64]{1,0:T(8,128)(2,1)} %table.1.table_ref, bf16[16,2048]{1,0:T(8,128)(2,1)} %get-tuple-element.20.refs_0_, bf16[16,2048]{1,0:T(8,128)(2,1)} %copy-done.11, bf16[16,2048]{1,0:T(8,128)(2,1)} %copy-done.12, bf16[16,2048]{1,0:T(8,128)(2,1)} %copy-done.13), custom_call_target="tpu_custom_call" | custom-call | flops 70000000 | bytes 1400000 | tf_op jit(solution)/shard_map/route/pallas_call | solution.py:215
  112.6 15.9 %all-to-all-start.4 = ((bf16[32,8,2048]{2,1,0:T(8,128)(2,1)}), bf16[32,8,2048]{2,1,0:T(8,128)(2,1)S(1)}, u32[]{:S(2)}, u32[]{:S(2)}) async-start(bf16[32,8,2048]{2,1,0:T(8,128)(2,1)} %bitcast.27), calls=%async_computation.4 | async-start | bytes 2097152 | tf_op jit(solution)/shard_map/all_to_all | solution.py:478
  128.6 1.4 broadcast_select_fusion.1.refs_0_
  130.0 0.2 collective-permute-start.9
  130.2 1.6 broadcast_select_fusion.refs_2_
  131.8 0.3 collective-permute-start.11
  132.1 0.3 collective-permute-start.10
  132.4 16.9 %collective-permute-done.8.refs_3_ = bf16[288,2048]{1,0:T(8,128)(2,1)} collective-permute-done((bf16[288,2048]{1,0:T(8,128)(2,1)}, bf16[288,2048]{1,0:T(8,128)(2,1)}, u32[]{:S(2)}, u32[]{:S(2)}) %collective-permute-start.8) | collective-permute-done | bytes 1179680 | tf_op jit(solution)/shard_map/ppermute | solution.py:400
  149.4 1.0 copy-done.6
  150.4 0.4 copy-done.8
  150.8 1.0 copy-done.7
  151.8 0.7 collective-permute-done.12.refs_7_
  152.5 1.0 copy-done.4
  153.5 7.1 %expert.1 = bf16[256,2048]{1,0:T(8,128)(2,1)} custom-call(bf16[256,2048]{1,0:T(8,128)(2,1)} %bitcast.28, bf16[288,2048]{1,0:T(8,128)(2,1)} %copy-done.1, bf16[288,2048]{1,0:T(8,128)(2,1)} %collective-permute-done.5.refs_1_, bf16[288,2048]{1,0:T(8,128)(2,1)} %copy-done.2, bf16[288,2048]{1,0:T(8,128)(2,1)} %collective-permute-done.8.refs_3_, ...), custom_call_target="tpu_custom_call" | custom-call | flops 2400000000 | bytes 11500000 | tf_op jit(solution)/shard_map/expert/pallas_call | solution.py:277
  160.7 10.3 %all-to-all-start.5 = ((bf16[32,8,2048]{2,1,0:T(8,128)(2,1)}), bf16[32,8,2048]{2,1,0:T(8,128)(2,1)S(1)}, u32[]{:S(2)}, u32[]{:S(2)}) async-start(bf16[32,8,2048]{2,1,0:T(8,128)(2,1)} %bitcast.29), calls=%async_computation.5 | async-start | bytes 2097152 | tf_op jit(solution)/shard_map/all_to_all | solution.py:482
  171.0 1.9 gates.1
  172.9 14.9 %all-to-all-done.5 = bf16[32,8,2048]{2,1,0:T(8,128)(2,1)S(1)} async-done(((bf16[32,8,2048]{2,1,0:T(8,128)(2,1)}), bf16[32,8,2048]{2,1,0:T(8,128)(2,1)S(1)}, u32[]{:S(2)}, u32[]{:S(2)}) %all-to-all-start.5) | async-done | bytes 1048608 | tf_op jit(solution)/shard_map/all_to_all | solution.py:482
  187.8 1.1 fusion
  189.0 0.1 fusion.16
  189.1 0.5 collective-permute-start.15
  189.6 5.8 %collective-permute-start.14 = (bf16[16,2048]{1,0:T(8,128)(2,1)S(1)}, bf16[16,2048]{1,0:T(8,128)(2,1)S(1)}, u32[]{:S(2)}, u32[]{:S(2)}) collective-permute-start(bf16[16,2048]{1,0:T(8,128)(2,1)S(1)} %get-tuple-element.31), channel_id=1, source_target_pairs={{0,128},{64,192},{128,0},{192,64},{1,129},{65,193},{129,1},{193,65... | collective-permute-start | bytes 196616 | tf_op jit(solution)/shard_map/ppermute | solution.py:491
  195.4 0.8 collective-permute-start.13
  196.1 3.0 %collective-permute-done.14 = bf16[16,2048]{1,0:T(8,128)(2,1)S(1)} collective-permute-done((bf16[16,2048]{1,0:T(8,128)(2,1)S(1)}, bf16[16,2048]{1,0:T(8,128)(2,1)S(1)}, u32[]{:S(2)}, u32[]{:S(2)}) %collective-permute-start.14) | collective-permute-done | bytes 65568 | tf_op jit(solution)/shard_map/ppermute | solution.py:491
  199.1 2.1 %collective-permute-done.13 = bf16[16,2048]{1,0:T(8,128)(2,1)S(1)} collective-permute-done((bf16[16,2048]{1,0:T(8,128)(2,1)S(1)}, bf16[16,2048]{1,0:T(8,128)(2,1)S(1)}, u32[]{:S(2)}, u32[]{:S(2)}) %collective-permute-start.13) | collective-permute-done | bytes 65568 | tf_op jit(solution)/shard_map/ppermute | solution.py:491
  201.2 0.7 fusion.5
  (51 shorter events, 0.2 us)
Async XLA Ops:
  0.0 58.2 %copy-start = (bf16[2048,512]{1,0:T(8,128)(2,1)S(1)}, bf16[2048,512]{1,0:T(8,128)(2,1)}, u32[]{:S(2)}) copy-start(bf16[2048,512]{1,0:T(8,128)(2,1)} %param.16) | copy-start | bytes 6291460
  0.0 8.4 %copy-start.14 = (f32[128,8]{0,1:T(8,128)S(1)}, f32[128,8]{0,1:T(8,128)}, u32[]{:S(2)}) copy-start(f32[128,8]{0,1:T(8,128)} %param.24) | copy-start | bytes 12292
  0.0 8.6 %copy-start.15 = (s32[128,8]{0,1:T(8,128)S(1)}, s32[128,8]{0,1:T(8,128)}, u32[]{:S(2)}) copy-start(s32[128,8]{0,1:T(8,128)} %param.23) | copy-start | bytes 12292
  0.0 13.6 %copy-start.16 = (f32[128]{0:T(128)S(1)}, f32[128]{0:T(128)}, u32[]{:S(2)}) copy-start(f32[128]{0:T(128)} %param.20) | copy-start | bytes 1540
  2.7 10.8 %all-to-all-start = ((f32[8,16,128]{2,1,0:T(8,128)}), f32[8,16,128]{2,1,0:T(8,128)S(1)}, u32[]{:S(2)}, u32[]{:S(2)}) async-start(f32[8,16,128]{2,1,0:T(8,128)} %get-tuple-element.16), calls=%async_computation | async-start | bytes 131072 | tf_op jit(solution)/shard_map/all_to_all | solution.py:439
  32.4 16.5 %copy-start.3 = (bf16[8,144,128]{2,1,0:T(8,128)(2,1)}, bf16[8,144,128]{2,1,0:T(8,128)(2,1)S(1)}, u32[]{:S(2)}) copy-start(bf16[8,144,128]{2,1,0:T(8,128)(2,1)S(1)} %all_to_all.30.ring_ref) | copy-start | bytes 884740
  48.9 4.3 %copy-start.9 = (bf16[4,8,128,128]{3,2,1,0:T(8,128)(2,1)}, bf16[4,8,128,128]{3,2,1,0:T(8,128)(2,1)S(1)}, u32[]{:S(2)}) copy-start(bf16[4,8,128,128]{3,2,1,0:T(8,128)(2,1)S(1)} %all_to_all.31) | copy-start | bytes 3145732
  48.9 11.4 %collective-permute-start = (bf16[4,4,2,128,128]{4,3,2,1,0:T(8,128)(2,1)S(1)}, bf16[4,4,2,128,128]{4,3,2,1,0:T(8,128)(2,1)}, u32[]{:S(2)}, u32[]{:S(2)}) collective-permute-start(bf16[4,4,2,128,128]{4,3,2,1,0:T(8,128)(2,1)S(1)} %bitcast.32), channel_id=1, source_target_pairs={{0,8},{8,0},{1,9},{9,1},{2,10},{10,2},{3,11},{11,3},{4,12},{12,4},... | collective-permute-start | bytes 3145736 | tf_op jit(solution)/shard_map/ppermute | solution.py:460
  53.2 75.3 %collective-permute-start.4 = (bf16[288,2048]{1,0:T(8,128)(2,1)}, bf16[288,2048]{1,0:T(8,128)(2,1)}, u32[]{:S(2)}, u32[]{:S(2)}) collective-permute-start(bf16[288,2048]{1,0:T(8,128)(2,1)} %get-tuple-element.21), channel_id=1, source_target_pairs={{1,8},{3,10},{5,12},{7,14},{8,1},{10,3},{12,5},{14,7},{17,24},{19,... | collective-permute-start | bytes 3538952 | tf_op jit(solution)/shard_map/ppermute | solution.py:400
  65.0 24.7 %all-to-all-start.3 = ((bf16[8,16,2048]{2,1,0:T(8,128)(2,1)}), bf16[8,16,2048]{2,1,0:T(8,128)(2,1)S(1)}, u32[]{:S(2)}, u32[]{:S(2)}) async-start(bf16[8,16,2048]{2,1,0:T(8,128)(2,1)} %bitcast.35), calls=%async_computation.3 | async-start | bytes 1048576 | tf_op jit(solution)/shard_map/all_to_all | solution.py:471
  69.0 61.2 %collective-permute-start.6 = (bf16[288,2048]{1,0:T(8,128)(2,1)}, bf16[288,2048]{1,0:T(8,128)(2,1)}, u32[]{:S(2)}, u32[]{:S(2)}) collective-permute-start(bf16[288,2048]{1,0:T(8,128)(2,1)} %get-tuple-element.23), channel_id=1, source_target_pairs={{0,4},{2,6},{4,0},{6,2},{9,13},{11,15},{13,9},{15,11},{16,20},{18,... | collective-permute-start | bytes 3538952 | tf_op jit(solution)/shard_map/ppermute | solution.py:396
  70.7 59.5 %collective-permute-start.7 = (bf16[288,2048]{1,0:T(8,128)(2,1)}, bf16[288,2048]{1,0:T(8,128)(2,1)}, u32[]{:S(2)}, u32[]{:S(2)}) collective-permute-start(bf16[288,2048]{1,0:T(8,128)(2,1)} %get-tuple-element.23), channel_id=1, source_target_pairs={{1,12},{3,14},{5,8},{7,10},{8,5},{10,7},{12,1},{14,3},{17,28},{19,... | collective-permute-start | bytes 3538952 | tf_op jit(solution)/shard_map/ppermute | solution.py:397
  89.6 0.8 copy-start.5
  92.3 6.6 %collective-permute-start.1 = (bf16[16,2048]{1,0:T(8,128)(2,1)}, bf16[16,2048]{1,0:T(8,128)(2,1)S(1)}, u32[]{:S(2)}, u32[]{:S(2)}) collective-permute-start(bf16[16,2048]{1,0:T(8,128)(2,1)} %get-tuple-element.20.refs_0_), channel_id=1, source_target_pairs={{0,64},{64,128},{128,192},{192,0},{1,65},{65,129},{129,193},{193,1... | collective-permute-start | bytes 196616 | tf_op jit(solution)/shard_map/ppermute | solution.py:475
  92.3 10.2 %collective-permute-start.2 = (bf16[16,2048]{1,0:T(8,128)(2,1)}, bf16[16,2048]{1,0:T(8,128)(2,1)S(1)}, u32[]{:S(2)}, u32[]{:S(2)}) collective-permute-start(bf16[16,2048]{1,0:T(8,128)(2,1)} %get-tuple-element.20.refs_0_), channel_id=1, source_target_pairs={{0,128},{64,192},{128,0},{192,64},{1,129},{65,193},{129,1},{193,65... | collective-permute-start | bytes 196616 | tf_op jit(solution)/shard_map/ppermute | solution.py:475
  98.9 11.4 %copy-start.11 = (bf16[16,2048]{1,0:T(8,128)(2,1)}, bf16[16,2048]{1,0:T(8,128)(2,1)S(1)}, u32[]{:S(2)}) copy-start(bf16[16,2048]{1,0:T(8,128)(2,1)S(1)} %collective-permute-done.1.refs_1_) | copy-start | bytes 196612
  98.9 6.5 %collective-permute-start.3 = (bf16[16,2048]{1,0:T(8,128)(2,1)}, bf16[16,2048]{1,0:T(8,128)(2,1)S(1)}, u32[]{:S(2)}, u32[]{:S(2)}) collective-permute-start(bf16[16,2048]{1,0:T(8,128)(2,1)} %get-tuple-element.20.refs_0_), channel_id=1, source_target_pairs={{0,192},{64,0},{128,64},{192,128},{1,193},{65,1},{129,65},{193,129... | collective-permute-start | bytes 196616 | tf_op jit(solution)/shard_map/ppermute | solution.py:475
  102.5 7.8 %copy-start.12 = (bf16[16,2048]{1,0:T(8,128)(2,1)}, bf16[16,2048]{1,0:T(8,128)(2,1)S(1)}, u32[]{:S(2)}) copy-start(bf16[16,2048]{1,0:T(8,128)(2,1)S(1)} %collective-permute-done.2.refs_2_) | copy-start | bytes 196612
  102.5 29.6 %collective-permute-start.5 = (bf16[288,2048]{1,0:T(8,128)(2,1)}, bf16[288,2048]{1,0:T(8,128)(2,1)}, u32[]{:S(2)}, u32[]{:S(2)}) collective-permute-start(bf16[288,2048]{1,0:T(8,128)(2,1)} %get-tuple-element.22), channel_id=1, source_target_pairs={{0,2},{1,10},{2,4},{3,12},{4,6},{5,14},{6,0},{7,8},{8,3},{9,11},{1... | collective-permute-start | bytes 3538952 | tf_op jit(solution)/shard_map/ppermute | solution.py:400
  105.4 4.9 %copy-start.13 = (bf16[16,2048]{1,0:T(8,128)(2,1)}, bf16[16,2048]{1,0:T(8,128)(2,1)S(1)}, u32[]{:S(2)}) copy-start(bf16[16,2048]{1,0:T(8,128)(2,1)S(1)} %collective-permute-done.3.refs_3_) | copy-start | bytes 196612
  105.4 44.0 %collective-permute-start.8 = (bf16[288,2048]{1,0:T(8,128)(2,1)}, bf16[288,2048]{1,0:T(8,128)(2,1)}, u32[]{:S(2)}, u32[]{:S(2)}) collective-permute-start(bf16[288,2048]{1,0:T(8,128)(2,1)} %get-tuple-element.24), channel_id=1, source_target_pairs={{0,6},{1,14},{2,0},{3,8},{4,2},{5,10},{6,4},{7,12},{8,7},{9,15},{1... | collective-permute-start | bytes 3538952 | tf_op jit(solution)/shard_map/ppermute | solution.py:400
  112.6 39.9 %all-to-all-start.4 = ((bf16[32,8,2048]{2,1,0:T(8,128)(2,1)}), bf16[32,8,2048]{2,1,0:T(8,128)(2,1)S(1)}, u32[]{:S(2)}, u32[]{:S(2)}) async-start(bf16[32,8,2048]{2,1,0:T(8,128)(2,1)} %bitcast.27), calls=%async_computation.4 | async-start | bytes 2097152 | tf_op jit(solution)/shard_map/all_to_all | solution.py:478
  130.0 1.8 copy-start.1
  130.0 19.4 %collective-permute-start.9 = (bf16[288,2048]{1,0:T(8,128)(2,1)S(1)}, bf16[288,2048]{1,0:T(8,128)(2,1)S(1)}, u32[]{:S(2)}, u32[]{:S(2)}) collective-permute-start(bf16[288,2048]{1,0:T(8,128)(2,1)S(1)} %broadcast_select_fusion.1.refs_0_), channel_id=1, source_target_pairs={{0,8},{8,0},{1,9},{9,1},{2,10},{10,2},{3,11},{11,3},{4,12},{12,4},... | collective-permute-start | bytes 3538952 | tf_op jit(solution)/shard_map/ppermute | solution.py:406
  131.8 17.5 %copy-start.2 = (bf16[288,2048]{1,0:T(8,128)(2,1)}, bf16[288,2048]{1,0:T(8,128)(2,1)S(1)}, u32[]{:S(2)}) copy-start(bf16[288,2048]{1,0:T(8,128)(2,1)S(1)} %broadcast_select_fusion.refs_2_) | copy-start | bytes 3538948
  131.8 17.6 %collective-permute-start.11 = (bf16[288,2048]{1,0:T(8,128)(2,1)S(1)}, bf16[288,2048]{1,0:T(8,128)(2,1)S(1)}, u32[]{:S(2)}, u32[]{:S(2)}) collective-permute-start(bf16[288,2048]{1,0:T(8,128)(2,1)S(1)} %broadcast_select_fusion.refs_2_), channel_id=1, source_target_pairs={{0,8},{8,0},{1,9},{9,1},{2,10},{10,2},{3,11},{11,3},{4,12},{12,4},... | collective-permute-start | bytes 3538952 | tf_op jit(solution)/shard_map/ppermute | solution.py:406
  132.1 17.3 %collective-permute-start.10 = (bf16[288,2048]{1,0:T(8,128)(2,1)}, bf16[288,2048]{1,0:T(8,128)(2,1)S(1)}, u32[]{:S(2)}, u32[]{:S(2)}) collective-permute-start(bf16[288,2048]{1,0:T(8,128)(2,1)} %collective-permute-done.5.refs_1_), channel_id=1, source_target_pairs={{0,8},{8,0},{1,9},{9,1},{2,10},{10,2},{3,11},{11,3},{4,12},{12,4},... | collective-permute-start | bytes 3538952 | tf_op jit(solution)/shard_map/ppermute | solution.py:406
  149.3 3.2 %collective-permute-start.12 = (bf16[288,2048]{1,0:T(8,128)(2,1)}, bf16[288,2048]{1,0:T(8,128)(2,1)}, u32[]{:S(2)}, u32[]{:S(2)}) collective-permute-start(bf16[288,2048]{1,0:T(8,128)(2,1)} %collective-permute-done.8.refs_3_), channel_id=1, source_target_pairs={{0,8},{8,0},{1,9},{9,1},{2,10},{10,2},{3,11},{11,3},{4,12},{12,4},... | collective-permute-start | bytes 3538952 | tf_op jit(solution)/shard_map/ppermute | solution.py:406
  149.4 1.1 copy-start.6
  149.4 1.4 copy-start.8
  150.8 1.0 copy-start.7
  152.5 1.0 copy-start.4
  160.7 27.2 %all-to-all-start.5 = ((bf16[32,8,2048]{2,1,0:T(8,128)(2,1)}), bf16[32,8,2048]{2,1,0:T(8,128)(2,1)S(1)}, u32[]{:S(2)}, u32[]{:S(2)}) async-start(bf16[32,8,2048]{2,1,0:T(8,128)(2,1)} %bitcast.29), calls=%async_computation.5 | async-start | bytes 2097152 | tf_op jit(solution)/shard_map/all_to_all | solution.py:482
  189.0 12.2 %copy-start.10 = (bf16[16,2048]{1,0:T(8,128)(2,1)S(1)}, bf16[16,2048]{1,0:T(8,128)(2,1)}, u32[]{:S(2)}) copy-start(bf16[16,2048]{1,0:T(8,128)(2,1)} %get-tuple-element.19) | copy-start | bytes 196612
  189.1 7.1 %collective-permute-start.15 = (bf16[16,2048]{1,0:T(8,128)(2,1)S(1)}, bf16[16,2048]{1,0:T(8,128)(2,1)S(1)}, u32[]{:S(2)}, u32[]{:S(2)}) collective-permute-start(bf16[16,2048]{1,0:T(8,128)(2,1)S(1)} %get-tuple-element.30), channel_id=1, source_target_pairs={{0,64},{64,128},{128,192},{192,0},{1,65},{65,129},{129,193},{193,1... | collective-permute-start | bytes 196616 | tf_op jit(solution)/shard_map/ppermute | solution.py:491
  189.6 9.5 %collective-permute-start.14 = (bf16[16,2048]{1,0:T(8,128)(2,1)S(1)}, bf16[16,2048]{1,0:T(8,128)(2,1)S(1)}, u32[]{:S(2)}, u32[]{:S(2)}) collective-permute-start(bf16[16,2048]{1,0:T(8,128)(2,1)S(1)} %get-tuple-element.31), channel_id=1, source_target_pairs={{0,128},{64,192},{128,0},{192,64},{1,129},{65,193},{129,1},{193,65... | collective-permute-start | bytes 196616 | tf_op jit(solution)/shard_map/ppermute | solution.py:491
  195.4 5.8 %collective-permute-start.13 = (bf16[16,2048]{1,0:T(8,128)(2,1)S(1)}, bf16[16,2048]{1,0:T(8,128)(2,1)S(1)}, u32[]{:S(2)}, u32[]{:S(2)}) collective-permute-start(bf16[16,2048]{1,0:T(8,128)(2,1)S(1)} %get-tuple-element.29), channel_id=1, source_target_pairs={{0,192},{64,0},{128,64},{192,128},{1,193},{65,1},{129,65},{193,129... | collective-permute-start | bytes 196616 | tf_op jit(solution)/shard_map/ppermute | solution.py:491
